TPU v7x, 32 devices: a whole 2x2x4 slice. The times are simulated.
32 devices in a mesh: grp: 2 (over y), tm: 8 (over z, x), row: 2 (over core).
Axes of the slice: x: 2, y: 2, z: 4, core: 2. Of those that a mesh axis runs over, the one named last changes fastest.
Arguments:
- queries: bfloat16 [4096, 768], P(('grp', 'tm', 'row')), parts along dimension 0, may hold values from -5 to 5
- keys: bfloat16 [4096, 768], P(('grp', 'tm', 'row')), parts along dimension 0, may hold values from -5 to 5
- values: bfloat16 [4096, 768], P(('grp', 'tm', 'row')), parts along dimension 0, may hold values from -6 to 6
- d_out: bfloat16 [4096, 768], P(('grp', 'tm', 'row')), parts along dimension 0, may hold values from -6 to 6
- action_table: bfloat16 [8, 768], replicated, may hold values from -5 to 5
- actions: int32 [16], P(('grp', 'tm')), parts along dimension 0, may hold values from 0 to 7
- temporal_list: int32 [32, 2], P(('grp', 'tm', 'row')), parts along dimension 0, may hold values from 1 to 3, as said below
Outputs:
- attended: bfloat16 [4096, 768], P(('grp', 'tm', 'row')), parts along dimension 0
- grad_queries: bfloat16 [4096, 768], P(('grp', 'tm', 'row')), parts along dimension 0
- grad_keys: bfloat16 [4096, 768], P(('grp', 'tm', 'row')), parts along dimension 0
- grad_values: bfloat16 [4096, 768], P(('grp', 'tm', 'row')), parts along dimension 0
- grad_table: float32 [16, 768], P('grp'), parts along dimension 0
There are 2 independent parts, one for each index of `grp`. A program takes and returns all parts, laid end to end along the dimension named above; an argument that names none is the same for every part. Nothing has to cross between parts.
Inputs may be any that keep to these rules, and one draw needn't show every extreme that they name: `temporal_list`: row b lists, in rising order, 2 different frame distances of 1 to 3.
All inputs are finite; a program needn't handle non-finite values.
Results may differ from a plain program's by a relative error of at most 0.012.
Values may be sent and summed in bfloat16 or wider, within the bound.
No kernel may reach another device: no remote copies, remote signals or barrier semaphores. Data moves between devices by JAX's collectives and lax.ppermute only.
A program may use at most 64 MiB of HBM per device.

v0:
```python
import math

import jax
import jax.numpy as jnp
from jax import lax
from jax.sharding import PartitionSpec as P

HEADS = 8
HEAD_DIM = 96
DIST = 3
LIST = 2


def from_behind(block, axis, distance):
    devices = range(lax.axis_size(axis))
    route = [(i - distance, i) for i in devices if i - distance in devices]
    return lax.ppermute(block, axis, route)


def attention_pass(queries, key_set, value_set, allowed, d_out):
    query_rows = queries.shape[0]
    key_rows = key_set.shape[0]
    model_width = queries.shape[1]
    score_scale = 1.0 / math.sqrt(HEAD_DIM)
    query_heads = queries.reshape(query_rows, HEADS, HEAD_DIM)
    key_heads = key_set.reshape(key_rows, HEADS, HEAD_DIM)
    value_heads = value_set.reshape(key_rows, HEADS, HEAD_DIM)
    grad_heads = d_out.reshape(query_rows, HEADS, HEAD_DIM)
    scores = (
        jnp.einsum("qhd,khd->hqk", query_heads, key_heads, preferred_element_type=jnp.float32)
        * score_scale
    )
    scores = jnp.where(allowed[None, None, :], scores, -1e30)
    highest = jnp.max(scores, axis=2, keepdims=True)
    weights = jnp.where(allowed[None, None, :], jnp.exp(scores - highest), 0.0)
    totals = jnp.sum(weights, axis=2, keepdims=True)
    probabilities = weights / totals
    log_total = (highest + jnp.log(totals))[:, :, 0].T
    probs_low = probabilities.astype(jnp.bfloat16)
    out_full = jnp.einsum(
        "hqk,khd->qhd", probs_low, value_heads, preferred_element_type=jnp.float32
    )
    d_probs = jnp.einsum(
        "qhd,khd->hqk", grad_heads, value_heads, preferred_element_type=jnp.float32
    )
    centre = jnp.sum(grad_heads.astype(jnp.float32) * out_full, axis=2)
    d_scores = (probabilities * (d_probs - centre.T[:, :, None])).astype(jnp.bfloat16)
    grad_query = (
        jnp.einsum("hqk,khd->qhd", d_scores, key_heads, preferred_element_type=jnp.float32)
        * score_scale
    )
    grad_key = None
    grad_value = None
    grad_key = (
        jnp.einsum(
            "hqk,qhd->khd", d_scores, query_heads, preferred_element_type=jnp.float32
        ).reshape(key_rows, model_width)
        * score_scale
    )
    grad_value = jnp.einsum(
        "hqk,qhd->khd", probs_low, grad_heads, preferred_element_type=jnp.float32
    ).reshape(key_rows, model_width)
    return (
        out_full.reshape(query_rows, model_width),
        grad_query.reshape(query_rows, model_width),
        grad_key,
        grad_value,
        log_total,
        centre,
    )


def on_device(queries, keys, values, d_out, action_table, actions, temporal_list):
    block_rows = queries.shape[0]
    model_width = queries.shape[1]
    frame_index = lax.axis_index("tm")
    labels = lax.iota(jnp.int32, action_table.shape[0])
    matches = actions[0] == labels
    action_row = jnp.dot(
        matches.astype(jnp.bfloat16)[None, :], action_table, preferred_element_type=jnp.float32
    )
    cond_values = (values.astype(jnp.float32) + action_row).astype(jnp.bfloat16)
    own_pair = jnp.stack([keys, cond_values])
    frame_pair = lax.all_gather(own_pair, "row", axis=1, tiled=True)
    earlier = []
    moving = own_pair
    for distance in range(DIST):
        moving = from_behind(moving, "tm", 1)
        earlier.append(moving)
    stacked = jnp.stack(earlier)
    distances = temporal_list[0]
    chosen = jnp.take(stacked, distances - 1, axis=0)
    frame_tokens = frame_pair.shape[1]
    key_set = jnp.concatenate(
        [frame_pair[0], chosen[:, 0].reshape(LIST * block_rows, model_width)], axis=0
    )
    value_set = jnp.concatenate(
        [frame_pair[1], chosen[:, 1].reshape(LIST * block_rows, model_width)], axis=0
    )
    present = frame_index - distances >= 0
    allowed = jnp.concatenate(
        [jnp.ones((frame_tokens,), dtype=bool), jnp.repeat(present, block_rows)]
    )
    out_full, grad_query, grad_key, grad_value, log_total, centre = attention_pass(
        queries, key_set, value_set, allowed, d_out
    )
    frame_terms = jnp.stack([grad_key[:frame_tokens], grad_value[:frame_tokens]])
    frame_grads = lax.psum_scatter(frame_terms, "row", scatter_dimension=1, tiled=True)
    slot_grads = []
    for listed in range(LIST):
        first_row = frame_tokens + listed * block_rows
        slot_grads.append(
            jnp.stack(
                [
                    grad_key[first_row : first_row + block_rows],
                    grad_value[first_row : first_row + block_rows],
                ]
            )
        )
    partials = []
    for distance in range(DIST):
        summed = jnp.zeros((2, block_rows, model_width), jnp.float32)
        for listed in range(LIST):
            summed = summed + jnp.where(distances[listed] == distance + 1, slot_grads[listed], 0.0)
        partials.append(summed)
    carried = jnp.zeros_like(partials[0])
    for distance in reversed(range(DIST)):
        carried = from_behind(carried + partials[distance], "tm", -1)
    key_total = frame_grads[0] + carried[0]
    value_total = frame_grads[1] + carried[1]
    column_sums = jnp.sum(value_total, axis=0)
    local_table = jnp.where(matches[:, None], column_sums[None, :], 0.0)
    grad_table = lax.psum(local_table, ("tm", "row"))
    return (
        out_full.astype(jnp.bfloat16),
        grad_query.astype(jnp.bfloat16),
        key_total.astype(jnp.bfloat16),
        value_total.astype(jnp.bfloat16),
        grad_table,
    )


def solution(mesh):
    return jax.shard_map(
        on_device,
        mesh=mesh,
        in_specs=(
            P(("grp", "tm", "row"), None),
            P(("grp", "tm", "row"), None),
            P(("grp", "tm", "row"), None),
            P(("grp", "tm", "row"), None),
            P(),
            P(("grp", "tm")),
            P(("grp", "tm", "row"), None),
        ),
        out_specs=(
            P(("grp", "tm", "row"), None),
            P(("grp", "tm", "row"), None),
            P(("grp", "tm", "row"), None),
            P(("grp", "tm", "row"), None),
            P("grp", None),
        ),
        check_vma=False,
    )
```

profile of v0, /device:TPU:0, one launch (start us, length us, event | category | flops | bytes accessed | tf_op | source)
XLA Modules:
  0.0 186.7 jit_solution(2967923302324929908)
XLA Ops:
  7.2 0.0 reduce-scatter.2.cloned.1.call-start
  8.0 0.1 convolution_reduce_fusion
  8.1 1.0 fusion.14
  9.1 1.0 pad_maximum_fusion.10
  10.1 4.9 %collective-permute-start = (bf16[2,128,768]{2,1,0:T(8,128)(2,1)S(1)}, bf16[2,128,768]{2,1,0:T(8,128)(2,1)S(1)}, u32[]{:S(2)}, u32[]{:S(2)}) collective-permute-start(bf16[2,128,768]{2,1,0:T(8,128)(2,1)S(1)} %pad_maximum_fusion.10), channel_id=1, source_target_pairs={{0,2},{2,4},{4,6},{6,8},{8,10},{10,12},{12,14},{1,3},{3,5},{5,7},{... | collective-permute-start | bytes 1179656 | tf_op jit(solution)/shard_map/ppermute | solution.py:17
  15.0 0.7 fusion.18
  15.6 0.7 compare_bitcast_fusion
  16.3 0.1 broadcast_bitcast_fusion
  16.4 6.9 %collective-permute-done = bf16[2,128,768]{2,1,0:T(8,128)(2,1)S(1)} collective-permute-done((bf16[2,128,768]{2,1,0:T(8,128)(2,1)S(1)}, bf16[2,128,768]{2,1,0:T(8,128)(2,1)S(1)}, u32[]{:S(2)}, u32[]{:S(2)}) %collective-permute-start) | collective-permute-done | bytes 393248 | tf_op jit(solution)/shard_map/ppermute | solution.py:17
  23.3 4.4 %collective-permute-start.1 = (bf16[2,128,768]{2,1,0:T(8,128)(2,1)S(1)}, bf16[2,128,768]{2,1,0:T(8,128)(2,1)S(1)}, u32[]{:S(2)}, u32[]{:S(2)}) collective-permute-start(bf16[2,128,768]{2,1,0:T(8,128)(2,1)S(1)} %collective-permute-done), channel_id=1, source_target_pairs={{0,2},{2,4},{4,6},{6,8},{8,10},{10,12},{12,14},{1,3},{3,5},{5,7},{... | collective-permute-start | bytes 1179656 | tf_op jit(solution)/shard_map/ppermute | solution.py:17
  27.7 2.4 %all_gather.3 = bf16[2,256,768]{2,1,0:T(8,128)(2,1)S(1)} all-gather(bf16[2,128,768]{2,1,0:T(8,128)(2,1)S(1)} %pad_maximum_fusion.10), channel_id=1, replica_groups=mesh['grp'=2,'tm'=8,'row'=2] {'row'}, dimensions={1}, use_global_device_ids=true | all-gather | bytes 1179648 | tf_op jit(solution)/shard_map/all_gather | solution.py:84
  30.1 0.1 fusion.29
  30.1 5.0 %collective-permute-done.1 = bf16[2,128,768]{2,1,0:T(8,128)(2,1)S(1)} collective-permute-done((bf16[2,128,768]{2,1,0:T(8,128)(2,1)S(1)}, bf16[2,128,768]{2,1,0:T(8,128)(2,1)S(1)}, u32[]{:S(2)}, u32[]{:S(2)}) %collective-permute-start.1) | collective-permute-done | bytes 393248 | tf_op jit(solution)/shard_map/ppermute | solution.py:17
  35.2 5.1 %collective-permute-start.2 = (bf16[2,128,768]{2,1,0:T(8,128)(2,1)S(1)}, bf16[2,128,768]{2,1,0:T(8,128)(2,1)}, u32[]{:S(2)}, u32[]{:S(2)}) collective-permute-start(bf16[2,128,768]{2,1,0:T(8,128)(2,1)S(1)} %collective-permute-done.1), channel_id=1, source_target_pairs={{0,2},{2,4},{4,6},{6,8},{8,10},{10,12},{12,14},{1,3},{3,5},{5,7},{... | collective-permute-start | bytes 1179656 | tf_op jit(solution)/shard_map/ppermute | solution.py:17
  40.3 0.6 fusion.31
  42.2 0.2 copy.35
  42.4 0.2 copy.37
  42.5 0.2 copy.33
  42.7 0.9 copy.31
  43.6 2.5 %collective-permute-done.2 = bf16[2,128,768]{2,1,0:T(8,128)(2,1)} collective-permute-done((bf16[2,128,768]{2,1,0:T(8,128)(2,1)S(1)}, bf16[2,128,768]{2,1,0:T(8,128)(2,1)}, u32[]{:S(2)}, u32[]{:S(2)}) %collective-permute-start.2) | collective-permute-done | bytes 393248 | tf_op jit(solution)/shard_map/ppermute | solution.py:17
  46.1 1.1 pad_maximum_fusion.1
  47.2 0.6 gather_fusion
  47.8 0.1 broadcast_select_fusion
  48.0 0.1 fusion.30
  48.0 0.4 copy.34
  48.5 0.3 concatenate.24
  48.7 0.4 copy.32
  49.2 0.3 concatenate.20
  49.4 0.5 fusion.12
  50.0 0.9 fusion.32
  50.8 1.6 convolution_bitcast_fusion
  52.5 1.1 multiply_reduce_fusion
  53.5 0.6 fusion.1
  54.1 1.0 copy-done.7
  55.1 0.5 multiply_bitcast_fusion
  55.6 0.1 slice.82
  55.7 1.0 fusion.27
  56.7 0.3 copy.41
  57.0 0.3 copy-done.1
  57.3 0.1 slice.83
  57.4 0.3 copy.42
  57.6 1.2 pad_maximum_fusion
  58.9 0.0 reduce-scatter.2.cloned.1.call-update
  58.9 1.4 copy-done.2
  60.3 0.1 fusion.28
  60.4 0.2 copy.43
  60.6 0.2 copy.45
  60.7 0.2 copy.44
  60.9 0.2 copy.46
  61.1 0.1 select_add_fusion
  61.2 1.3 collective-permute-start.3
  63.8 17.5 %collective-permute-done.3 = f32[2,128,768]{2,1,0:T(8,128)S(1)} collective-permute-done((f32[2,128,768]{2,1,0:T(8,128)S(1)}, f32[2,128,768]{2,1,0:T(8,128)S(1)}, u32[]{:S(2)}, u32[]{:S(2)}) %collective-permute-start.3) | collective-permute-done | bytes 786464 | tf_op jit(solution)/shard_map/ppermute | solution.py:17
  81.3 0.2 add_add_fusion.1
  81.4 1.4 collective-permute-start.4
  84.2 17.0 %collective-permute-done.4 = f32[2,128,768]{2,1,0:T(8,128)S(1)} collective-permute-done((f32[2,128,768]{2,1,0:T(8,128)S(1)}, f32[2,128,768]{2,1,0:T(8,128)S(1)}, u32[]{:S(2)}, u32[]{:S(2)}) %collective-permute-start.4) | collective-permute-done | bytes 786464 | tf_op jit(solution)/shard_map/ppermute | solution.py:17
  101.1 1.0 add_add_fusion
  102.2 1.3 collective-permute-start.5
  103.5 1.7 copy.47
  105.2 0.4 fusion.7
  105.6 0.8 copy.48
  106.4 13.7 %collective-permute-done.5 = f32[2,128,768]{2,1,0:T(8,128)S(1)} collective-permute-done((f32[2,128,768]{2,1,0:T(8,128)}, f32[2,128,768]{2,1,0:T(8,128)S(1)}, u32[]{:S(2)}, u32[]{:S(2)}) %collective-permute-start.5) | collective-permute-done | bytes 786464 | tf_op jit(solution)/shard_map/ppermute | solution.py:17
  120.1 2.0 %fusion.16 = (f32[768]{0:T(1024)S(1)}, bf16[128,768]{1,0:T(8,128)(2,1)}, bf16[128,768]{1,0:T(8,128)(2,1)}) fusion(f32[2,128,768]{2,1,0:T(8,128)S(1)} %collective-permute-done.5, f32[2,128,768]{2,1,0:T(8,128)} %reduce-scatter.2.cloned.1.call-done), kind=kLoop, calls=%fused_computation.41 | loop fusion | flops 490752 | bytes 1969152 | tf_op jit(solution)/shard_map/reduce_sum | solution.py:131
  122.1 0.1 broadcast_select_fusion.1
  122.2 57.6 %psum.7 = f32[8,768]{1,0:T(8,128)} all-reduce(f32[8,768]{1,0:T(8,128)S(1)} %broadcast_select_fusion.1), channel_id=1, replica_groups=mesh['grp'=2,'tm'=8,'row'=2] {'tm','row'}, use_global_device_ids=true, to_apply=%region_5.6 | all-reduce | flops 6144 | bytes 49152 | tf_op jit(solution)/shard_map/psum | solution.py:133
  (28 shorter events, 0.1 us)
Async XLA Ops:
  7.2 0.8 copy-start
  7.2 33.1 %copy-start.12 = (s32[1,2]{1,0:T(1,128)S(1)}, s32[1,2]{1,0:T(1,128)}, u32[]{:S(2)}) copy-start(s32[1,2]{1,0:T(1,128)} %param.13) | copy-start | bytes 28
  7.2 35.0 %copy-start.10 = (bf16[128,768]{1,0:T(8,128)(2,1)S(1)}, bf16[128,768]{1,0:T(8,128)(2,1)}, u32[]{:S(2)}) copy-start(bf16[128,768]{1,0:T(8,128)(2,1)} %param.7) | copy-start | bytes 589828
  7.2 112.9 %reduce-scatter.2.cloned.1.call-start = ((), (), s32[]{:S(2)}) async-start(), calls=%async_computation.1 | async-start | bytes 2359296 | tf_op jit(solution)/shard_map/reduce_scatter | solution.py:108
  8.1 34.2 %copy-start.11 = (bf16[128,768]{1,0:T(8,128)(2,1)S(1)}, bf16[128,768]{1,0:T(8,128)(2,1)}, u32[]{:S(2)}) copy-start(bf16[128,768]{1,0:T(8,128)(2,1)} %param.10) | copy-start | bytes 589828
  10.1 13.2 %collective-permute-start = (bf16[2,128,768]{2,1,0:T(8,128)(2,1)S(1)}, bf16[2,128,768]{2,1,0:T(8,128)(2,1)S(1)}, u32[]{:S(2)}, u32[]{:S(2)}) collective-permute-start(bf16[2,128,768]{2,1,0:T(8,128)(2,1)S(1)} %pad_maximum_fusion.10), channel_id=1, source_target_pairs={{0,2},{2,4},{4,6},{6,8},{8,10},{10,12},{12,14},{1,3},{3,5},{5,7},{... | collective-permute-start | bytes 1179656 | tf_op jit(solution)/shard_map/ppermute | solution.py:17
  23.3 11.9 %collective-permute-start.1 = (bf16[2,128,768]{2,1,0:T(8,128)(2,1)S(1)}, bf16[2,128,768]{2,1,0:T(8,128)(2,1)S(1)}, u32[]{:S(2)}, u32[]{:S(2)}) collective-permute-start(bf16[2,128,768]{2,1,0:T(8,128)(2,1)S(1)} %collective-permute-done), channel_id=1, source_target_pairs={{0,2},{2,4},{4,6},{6,8},{8,10},{10,12},{12,14},{1,3},{3,5},{5,7},{... | collective-permute-start | bytes 1179656 | tf_op jit(solution)/shard_map/ppermute | solution.py:17
  35.2 10.9 %collective-permute-start.2 = (bf16[2,128,768]{2,1,0:T(8,128)(2,1)S(1)}, bf16[2,128,768]{2,1,0:T(8,128)(2,1)}, u32[]{:S(2)}, u32[]{:S(2)}) collective-permute-start(bf16[2,128,768]{2,1,0:T(8,128)(2,1)S(1)} %collective-permute-done.1), channel_id=1, source_target_pairs={{0,2},{2,4},{4,6},{6,8},{8,10},{10,12},{12,14},{1,3},{3,5},{5,7},{... | collective-permute-start | bytes 1179656 | tf_op jit(solution)/shard_map/ppermute | solution.py:17
  48.7 1.2 copy-start.3
  50.8 1.6 copy-start.9
  54.1 1.0 copy-start.7
  55.6 1.7 copy-start.1
  58.9 1.4 copy-start.2
  58.9 1.5 copy-start.6
  58.9 1.7 copy-start.5
  61.2 20.1 %collective-permute-start.3 = (f32[2,128,768]{2,1,0:T(8,128)S(1)}, f32[2,128,768]{2,1,0:T(8,128)S(1)}, u32[]{:S(2)}, u32[]{:S(2)}) collective-permute-start(f32[2,128,768]{2,1,0:T(8,128)S(1)} %select_add_fusion), channel_id=1, source_target_pairs={{2,0},{4,2},{6,4},{8,6},{10,8},{12,10},{14,12},{3,1},{5,3},{7,5},{... | collective-permute-start | bytes 2359304 | tf_op jit(solution)/shard_map/ppermute | solution.py:17
  81.4 23.8 %copy-start.4 = (bf16[256,8,96]{0,2,1:T(8,128)(2,1)S(1)}, bf16[256,8,96]{0,2,1:T(8,128)(2,1)}, u32[]{:S(2)}) copy-start(bf16[256,8,96]{0,2,1:T(8,128)(2,1)} %copy-done.3) | copy-start | bytes 1179652
  81.4 23.8 %copy-start.8 = (bf16[8,128,512]{1,2,0:T(8,128)(2,1)S(1)}, bf16[8,128,512]{1,2,0:T(8,128)(2,1)}, u32[]{:S(2)}) copy-start(bf16[8,128,512]{1,2,0:T(8,128)(2,1)} %copy-done.7) | copy-start | bytes 3145732
  81.4 19.7 %collective-permute-start.4 = (f32[2,128,768]{2,1,0:T(8,128)S(1)}, f32[2,128,768]{2,1,0:T(8,128)S(1)}, u32[]{:S(2)}, u32[]{:S(2)}) collective-permute-start(f32[2,128,768]{2,1,0:T(8,128)S(1)} %add_add_fusion.1), channel_id=1, source_target_pairs={{2,0},{4,2},{6,4},{8,6},{10,8},{12,10},{14,12},{3,1},{5,3},{7,5},{... | collective-permute-start | bytes 2359304 | tf_op jit(solution)/shard_map/ppermute | solution.py:17
  102.2 18.0 %collective-permute-start.5 = (f32[2,128,768]{2,1,0:T(8,128)}, f32[2,128,768]{2,1,0:T(8,128)S(1)}, u32[]{:S(2)}, u32[]{:S(2)}) collective-permute-start(f32[2,128,768]{2,1,0:T(8,128)} %add_add_fusion), channel_id=1, source_target_pairs={{2,0},{4,2},{6,4},{8,6},{10,8},{12,10},{14,12},{3,1},{5,3},{7,5},{... | collective-permute-start | bytes 2359304 | tf_op jit(solution)/shard_map/ppermute | solution.py:17
Sparse Core Ops, SparseCore 0:
  59.0 13.1 reduce-scatter.1
where the time goes:
time: 187 us
  waiting for transfers between devices  62.6 us (33%)
  blocking collectives  60 us (32%)
  between operations  19 us (10%)
  starting transfers between devices  18.4 us (10%)
  local copies, waits for them, and re-layouts  11.8 us (6%)
  other arithmetic  10 us (5%)
  matrix products  4.76 us (3%)
    ppermute x6, waiting for transfers between devices, from_behind(): return lax.ppermute(block, axis, route)  62.6 us
    psum x1, blocking collectives, on_device(): grad_table = lax.psum(local_table, ('tm', 'row'))  57.6 us
    ppermute x6, starting transfers between devices, from_behind(): return lax.ppermute(block, axis, route)  18.4 us
    unnamed x30, local copies, waits for them, and re-layouts  5.64 us
  transfers between devices with their start and end apart: 7, of which 6 were waited for; matrix products, arithmetic and copies ran while one was open for 5% of the time, Pallas kernels for 0%

commit v1 on v0

v1 whole, which is shorter than its diff:
```python
import math

import jax
import jax.numpy as jnp
from jax import lax
from jax.experimental import pallas as pl
from jax.experimental.pallas import tpu as pltpu
from jax.sharding import PartitionSpec as P

HEADS = 8
HEAD_DIM = 96
LANES = 128
SCALE = 1.0 / math.sqrt(HEAD_DIM)
STAT_ROWS = 24
ACTION_ROWS = 16
MASKED = 1e30
F32 = jnp.float32
BF16 = jnp.bfloat16
VMEM_LIMIT = 56 * 1024 * 1024


def shift(block, distance):
    frames = range(lax.axis_size("tm"))
    return lax.ppermute(block, "tm", [(i - distance, i) for i in frames if i - distance in frames])


def shift_some(block, distance, parity):
    frames = range(lax.axis_size("tm"))
    route = [(i - distance, i) for i in frames if i - distance in frames and i % 2 == parity]
    return lax.ppermute(block, "tm", route)


def swap_pair(block):
    frames = range(lax.axis_size("tm"))
    return lax.ppermute(block, "tm", [(i, i ^ 1) for i in frames if i ^ 1 in frames])


def swap_row(block):
    return lax.ppermute(block, "row", [(0, 1), (1, 0)])


def head_span(head):
    first = head * HEAD_DIM
    low = first // LANES * LANES
    high = -(-(first + HEAD_DIM) // LANES) * LANES
    return slice(low, high), first - low


def own_lanes(block, head):
    span, offset = head_span(head)
    part = block[:, span]
    lane = lax.broadcasted_iota(jnp.int32, part.shape, 1)
    return jnp.where((lane >= offset) & (lane < offset + HEAD_DIM), part, jnp.zeros_like(part))


def join_heads(parts):
    tiles = []
    width = HEADS * HEAD_DIM
    for low in range(0, width, LANES):
        tile = None
        for head in range(HEADS):
            span, offset = head_span(head)
            if span.start <= low < span.stop:
                piece = parts[head][:, low - span.start : low - span.start + LANES]
                if tile is None:
                    tile = piece
                else:
                    lane = lax.broadcasted_iota(jnp.int32, piece.shape, 1) + low
                    tile = jnp.where(lane >= head * HEAD_DIM, piece, tile)
        tiles.append(tile)
    return jnp.concatenate(tiles, axis=1)


def dot_t(left, right):
    return lax.dot_general(left, right, (((1,), (1,)), ((), ())), preferred_element_type=F32)


def dot(left, right):
    return jnp.dot(left, right, preferred_element_type=F32)


def prepare_kernel(actions, queries, keys, values, d_out, table, kv_out, qo_out):
    rows = keys.shape[0]
    action = actions[0]
    chosen = jnp.zeros((1, table.shape[1]), F32)
    for label in range(table.shape[0]):
        row = table[label : label + 1, :].astype(F32)
        chosen = jnp.where(action == label, row, chosen)
    kv_out[0:rows, :] = keys[...]
    kv_out[rows : 2 * rows, :] = (values[...].astype(F32) + chosen).astype(BF16)
    kv_out[2 * rows :, :] = jnp.full((ACTION_ROWS, keys.shape[1]), action.astype(F32), F32).astype(BF16)
    qo_out[0:rows, :] = queries[...]
    qo_out[rows:, :] = d_out[...]


def forward_kernel(frame, listed, qo, own, partner, near2, pair, near3, near1,
                   attended, grad_queries, stats1, stats2, stats3, stats_row, table_out, picked):
    rows = qo.shape[0] // 2
    frame_id = frame[0]
    odd = frame_id % 2
    for slot in range(2):
        distance = listed[0, slot]
        code = jnp.where(distance == 1, jnp.where(odd == 1, 0, 1), distance)
        for value, source in ((0, pair), (1, near1), (2, near2), (3, near3)):
            @pl.when(code == value)
            def _(slot=slot, source=source):
                picked[slot] = source[...]
    present = [frame_id >= listed[0, slot] for slot in range(2)]
    blocks = [own, partner, picked.at[0], picked.at[1]]
    lane = lax.broadcasted_iota(jnp.int32, (rows, LANES), 1)
    columns = jnp.zeros((rows, LANES), F32)
    out_parts, query_parts, sums = [], [], [[], [], []]
    for head in range(HEADS):
        span, _ = head_span(head)
        query = own_lanes(qo[0:rows, :], head)
        grad = own_lanes(qo[rows:, :], head)
        key_blocks = [block[0:rows, span] for block in blocks]
        value_blocks = [block[rows : 2 * rows, span] for block in blocks]
        scores = [dot_t(query, block) * SCALE for block in key_blocks]
        for slot in range(2):
            scores[2 + slot] = jnp.where(present[slot], scores[2 + slot], -MASKED)
        highest = jnp.max(jnp.maximum(jnp.maximum(scores[0], scores[1]), jnp.maximum(scores[2], scores[3])), axis=1, keepdims=True)
        weights = [jnp.exp(block - highest) for block in scores]
        total = jnp.sum(weights[0] + weights[1] + weights[2] + weights[3], axis=1, keepdims=True)
        inverse = 1.0 / total
        probs = [block * inverse for block in weights]
        probs_low = [block.astype(BF16) for block in probs]
        rounded = [block.astype(F32) for block in probs_low]
        d_probs = [dot_t(grad, block) for block in value_blocks]
        centre = jnp.sum(rounded[0] * d_probs[0] + rounded[1] * d_probs[1] + rounded[2] * d_probs[2] + rounded[3] * d_probs[3], axis=1, keepdims=True)
        d_scores = [(p * (d - centre)).astype(BF16) for p, d in zip(probs, d_probs)]
        out_parts.append(sum(dot(p, v) for p, v in zip(probs_low, value_blocks)))
        query_parts.append(sum(dot(d, k) for d, k in zip(d_scores, key_blocks)))
        columns = jnp.where(lane == head, highest + jnp.log(total), columns)
        columns = jnp.where(lane == HEADS + head, centre, columns)
        wide = grad.astype(F32)
        masses = (rounded[0] + rounded[1], rounded[2], rounded[3])
        for group in range(3):
            mass = jnp.sum(masses[group], axis=1, keepdims=True)
            sums[group].append(jnp.sum(wide * mass, axis=0, keepdims=True))
    attended[...] = join_heads(out_parts).astype(BF16)
    grad_queries[...] = (join_heads(query_parts) * SCALE).astype(BF16)
    turned = columns.T
    for distance, stats in ((1, stats1), (2, stats2), (3, stats3)):
        in_list = (listed[0, 0] == distance) | (listed[0, 1] == distance)
        stats[0 : 2 * HEADS, :] = turned[0 : 2 * HEADS, :]
        stats[2 * HEADS :, :] = jnp.full((HEADS, LANES), jnp.where(in_list, 1.0, 0.0), F32)
    stats_row[...] = turned[0 : 2 * HEADS, :]
    label = lax.broadcasted_iota(jnp.int32, table_out.shape, 0).astype(F32)
    totals = jnp.zeros(table_out.shape, F32)
    for group, block in ((0, own), (1, picked.at[0]), (2, picked.at[1])):
        action = block[2 * rows :, :].astype(F32)[0:1, :]
        addend = join_heads(sums[group])
        totals = totals + jnp.where(label == action, addend, 0.0)
    table_out[...] = totals


def backward_kernel(frame, own, qo, qo_partner, late2, late_pair, late3, late1,
                    stats_own, stats_partner, stats1, stats2, stats3, grad_keys, grad_values):
    rows = qo.shape[0] // 2
    odd = frame[0] % 2
    key_parts, value_parts = [], []
    first = jnp.where(odd == 1, late1[...], late_pair[...])
    queries = [qo[0:rows, :], qo_partner[0:rows, :], first[0:rows, :], late2[0:rows, :], late3[0:rows, :]]
    grads = [qo[rows:, :], qo_partner[rows:, :], first[rows:, :], late2[rows:, :], late3[rows:, :]]
    queries = jnp.concatenate(queries, axis=0)
    grads = jnp.concatenate(grads, axis=0)
    late = []
    for stats in (stats1, stats2, stats3):
        late.append(jnp.where(stats[2 * HEADS :, :] > 0.5, stats[0:HEADS, :], MASKED))
    log_totals = jnp.concatenate([stats_own[0:HEADS, :], stats_partner[0:HEADS, :]] + late, axis=1)
    centres = jnp.concatenate([s[HEADS : 2 * HEADS, :] for s in (stats_own, stats_partner, stats1, stats2, stats3)], axis=1)
    for head in range(HEADS):
        span, _ = head_span(head)
        key = own_lanes(own[0:rows, :], head)
        value = own_lanes(own[rows : 2 * rows, :], head)
        scores = dot_t(key, queries[:, span]) * SCALE
        probs = jnp.exp(scores - log_totals[head : head + 1, :])
        d_probs = dot_t(value, grads[:, span])
        d_scores = (probs * (d_probs - centres[head : head + 1, :])).astype(BF16)
        value_parts.append(dot(probs.astype(BF16), grads[:, span]))
        key_parts.append(dot(d_scores, queries[:, span]))
    grad_keys[...] = (join_heads(key_parts) * SCALE).astype(BF16)
    grad_values[...] = join_heads(value_parts).astype(BF16)


def vmem(count):
    return [pl.BlockSpec(memory_space=pltpu.VMEM)] * count


def smem(count):
    return [pl.BlockSpec(memory_space=pltpu.SMEM)] * count


def params():
    return pltpu.CompilerParams(vmem_limit_bytes=VMEM_LIMIT)


def sum_table(table):
    frames = lax.axis_size("tm")
    if frames & (frames - 1):
        return lax.psum(table, ("tm", "row"))
    table = table + swap_row(table)
    step = 1
    while step < frames:
        table = table + lax.ppermute(table, "tm", [(i, i ^ step) for i in range(frames)])
        step *= 2
    return table


def on_device(queries, keys, values, d_out, action_table, actions, temporal_list):
    rows, width = queries.shape
    frame = lax.axis_index("tm").astype(jnp.int32).reshape(1)
    shape = jax.ShapeDtypeStruct
    kv, qo = pl.pallas_call(
        prepare_kernel,
        out_shape=(shape((2 * rows + ACTION_ROWS, width), BF16), shape((2 * rows, width), BF16)),
        in_specs=smem(1) + vmem(5),
        out_specs=vmem(2),
        compiler_params=params(),
    )(actions, queries, keys, values, d_out, action_table)
    near2 = shift(kv, 2)
    pair = swap_pair(kv)
    partner = swap_row(kv)
    near3 = shift(near2, 1)
    near1 = shift_some(pair, 2, 0)
    late2 = shift(qo, -2)
    late_pair = swap_pair(qo)
    qo_partner = swap_row(qo)
    late3 = shift(late2, -1)
    late1 = shift_some(late_pair, -2, 1)
    attended, grad_queries, stats1, stats2, stats3, stats_row, table = pl.pallas_call(
        forward_kernel,
        out_shape=(
            shape((rows, width), BF16),
            shape((rows, width), BF16),
            shape((STAT_ROWS, LANES), F32),
            shape((STAT_ROWS, LANES), F32),
            shape((STAT_ROWS, LANES), F32),
            shape((2 * HEADS, LANES), F32),
            shape(action_table.shape, F32),
        ),
        in_specs=smem(2) + vmem(7),
        out_specs=vmem(7),
        scratch_shapes=[pltpu.VMEM((2, 2 * rows + ACTION_ROWS, width), BF16)],
        compiler_params=params(),
    )(frame, temporal_list, qo, kv, partner, near2, pair, near3, near1)
    late_stats = [shift(stats, -distance) for distance, stats in ((1, stats1), (2, stats2), (3, stats3))]
    stats_partner = swap_row(stats_row)
    grad_table = sum_table(table)
    grad_keys, grad_values = pl.pallas_call(
        backward_kernel,
        out_shape=(shape((rows, width), BF16), shape((rows, width), BF16)),
        in_specs=smem(1) + vmem(12),
        out_specs=vmem(2),
        compiler_params=params(),
    )(frame, kv, qo, qo_partner, late2, late_pair, late3, late1, stats_row, stats_partner, *late_stats)
    return attended, grad_queries, grad_keys, grad_values, grad_table


def solution(mesh):
    split = P(("grp", "tm", "row"), None)
    return jax.shard_map(
        on_device,
        mesh=mesh,
        in_specs=(split, split, split, split, P(), P(("grp", "tm")), split),
        out_specs=(split, split, split, split, P("grp", None)),
        check_vma=False,
    )
```

time: 187 us -> 80.5 us (0.43)
  blocking collectives: 60 us -> 0 us
  waiting for transfers between devices: 62.6 us -> 25.9 us
  between operations: 19 us -> 1.54 us
  starting transfers between devices: 18.4 us -> 34.9 us
  Pallas kernels: 0 us -> 14.4 us
  local copies, waits for them, and re-layouts: 11.8 us -> 1.53 us
  other arithmetic: 10 us -> 1.36 us
  matrix products: 4.76 us -> 0 us
    psum x1 -> x0, blocking collectives: 57.6 us -> none  [on_device(): grad_table = lax.psum(local_table, ('tm', 'row'))]
    ppermute x6 -> x18, waiting for transfers between devices: 62.6 us -> 25.9 us  [the longest x7 16.1 us: shift(): lax.ppermute(block, 'tm', [(i - distance, i) for i in frames if i - dista...]
    ppermute x6 -> x18, starting transfers between devices: 18.4 us -> 34.9 us  [the longest x7 14.8 us: shift(): lax.ppermute(block, 'tm', [(i - distance, i) for i in frames if i - dista...]
    pallas_call x0 -> x3, Pallas kernels: none -> 14.4 us  [the longest x1 7.26 us: on_device(): pl.pallas_call(forward_kernel, out_shape=(shape((rows, width), BF16), sha...]
    dot_general x7 -> x0, matrix products: 4.76 us -> none  [the longest x1 1.63 us: attention_pass(): jnp.einsum('hqk,qhd->khd', probs_low, grad_heads, preferred_element_type=...]
    another operation x4 -> x0, other arithmetic: 4.34 us -> none  [the longest x2 1.97 us: on_device(): own_pair = jnp.stack([keys, cond_values])]
    unnamed x30 -> x32, local copies, waits for them, and re-layouts: 5.64 us -> 1.53 us
    slice x11 -> x0, local copies, waits for them, and re-layouts: 3.85 us -> none  [the longest x1 1.01 us: on_device(): grad_key[first_row:first_row + block_rows]]
  transfers between devices with their start and end apart: 7 -> 18, of which waited for: 6 -> 11; matrix products, arithmetic and copies ran while one was open for 5% -> 1% of each run, Pallas kernels for 0% -> 15%
where the time goes in v1:
time: 80.5 us; the launch traced here: 79.6 us
  starting transfers between devices  34.9 us (43%)
  waiting for transfers between devices  25.9 us (32%)
  Pallas kernels  14.4 us (18%)
  between operations  1.54 us (2%)
  local copies, waits for them, and re-layouts  1.53 us (2%)
  other arithmetic  1.36 us (2%)
    ppermute x7, waiting for transfers between devices, shift(): lax.ppermute(block, 'tm', [(i - distance, i) for i in frames if i - dista...  16.1 us
    ppermute x7, starting transfers between devices, shift(): lax.ppermute(block, 'tm', [(i - distance, i) for i in frames if i - dista...  14.8 us
    ppermute x3, starting transfers between devices, sum_table(): lax.ppermute(table, 'tm', [(i, i ^ step) for i in range(frames)])  12.3 us
    pallas_call x1, Pallas kernels, on_device(): pl.pallas_call(forward_kernel, out_shape=(shape((rows, width), BF16), sha...  7.26 us
    ppermute x2, starting transfers between devices, shift_some(): return lax.ppermute(block, 'tm', route)  5.48 us
    pallas_call x1, Pallas kernels, on_device(): pl.pallas_call(backward_kernel, out_shape=(shape((rows, width), BF16), sh...  4.97 us
    ppermute x2, waiting for transfers between devices, swap_pair(): lax.ppermute(block, 'tm', [(i, i ^ 1) for i in frames if i ^ 1 in frames])  3.63 us
    ppermute x3, waiting for transfers between devices, sum_table(): lax.ppermute(table, 'tm', [(i, i ^ step) for i in range(frames)])  3.61 us
  transfers between devices with their start and end apart: 18, of which 11 were waited for; matrix products, arithmetic and copies ran while one was open for 1% of the time, Pallas kernels for 15%

profile of v1, /device:TPU:0, one launch (start us, length us, event | category | flops | bytes accessed | tf_op | source)
XLA Modules:
  0.0 79.6 jit_solution(13708904491770181174)
XLA Ops:
  1.3 2.2 %shard_map.110 = (bf16[272,768]{1,0:T(8,128)(2,1)}, bf16[256,768]{1,0:T(8,128)(2,1)}) custom-call(s32[1]{0:T(128)S(6)} %copy.12.actions, bf16[128,768]{1,0:T(8,128)(2,1)} %queries.1, bf16[128,768]{1,0:T(8,128)(2,1)} %keys.1, bf16[128,768]{1,0:T(8,128)(2,1)} %values.1, bf16[128,768]{1,0:T(8,128)(2,1)} %d_out.1, bf16[8,768]{1,0:T(8,128)(2,1)} %table.1), custom_call_target="tpu_custom_call" | custom-call | tf_op jit(solution)/shard_map/pallas_call | solution.py:215
  3.4 4.9 %collective-permute-start.1 = (bf16[272,768]{1,0:T(8,128)(2,1)}, bf16[272,768]{1,0:T(8,128)(2,1)S(1)}, u32[]{:S(2)}, u32[]{:S(2)}) collective-permute-start(bf16[272,768]{1,0:T(8,128)(2,1)} %get-tuple-element.17.own), channel_id=1, source_target_pairs={{0,4},{2,6},{4,8},{6,10},{8,12},{10,14},{1,5},{3,7},{5,9},{7,11},{... | collective-permute-start | bytes 1253384 | tf_op jit(solution)/shard_map/ppermute | solution.py:24
  8.4 1.6 %collective-permute-start.2 = (bf16[272,768]{1,0:T(8,128)(2,1)}, bf16[272,768]{1,0:T(8,128)(2,1)S(1)}, u32[]{:S(2)}, u32[]{:S(2)}) collective-permute-start(bf16[272,768]{1,0:T(8,128)(2,1)} %get-tuple-element.17.own), channel_id=1, source_target_pairs={{0,2},{2,0},{4,6},{6,4},{8,10},{10,8},{12,14},{14,12},{1,3},{3,1},... | collective-permute-start | bytes 1253384 | tf_op jit(solution)/shard_map/ppermute | solution.py:35
  9.9 0.0 collective-permute-start
  9.9 1.3 %collective-permute-start.6 = (bf16[256,768]{1,0:T(8,128)(2,1)}, bf16[256,768]{1,0:T(8,128)(2,1)S(1)}, u32[]{:S(2)}, u32[]{:S(2)}) collective-permute-start(bf16[256,768]{1,0:T(8,128)(2,1)} %get-tuple-element.16.qo), channel_id=1, source_target_pairs={{4,0},{6,2},{8,4},{10,6},{12,8},{14,10},{5,1},{7,3},{9,5},{11,7},{... | collective-permute-start | bytes 1179656 | tf_op jit(solution)/shard_map/ppermute | solution.py:24
  11.2 0.6 collective-permute-start.7
  11.8 5.7 %collective-permute-done.1.near2 = bf16[272,768]{1,0:T(8,128)(2,1)S(1)} collective-permute-done((bf16[272,768]{1,0:T(8,128)(2,1)}, bf16[272,768]{1,0:T(8,128)(2,1)S(1)}, u32[]{:S(2)}, u32[]{:S(2)}) %collective-permute-start.1) | collective-permute-done | bytes 417824 | tf_op jit(solution)/shard_map/ppermute | solution.py:24
  17.6 0.0 copy-start
  17.6 3.4 %collective-permute-start.3 = (bf16[272,768]{1,0:T(8,128)(2,1)S(1)}, bf16[272,768]{1,0:T(8,128)(2,1)S(1)}, u32[]{:S(2)}, u32[]{:S(2)}) collective-permute-start(bf16[272,768]{1,0:T(8,128)(2,1)S(1)} %collective-permute-done.1.near2), channel_id=1, source_target_pairs={{0,2},{2,4},{4,6},{6,8},{8,10},{10,12},{12,14},{1,3},{3,5},{5,7},{... | collective-permute-start | bytes 1253384 | tf_op jit(solution)/shard_map/ppermute | solution.py:24
  21.0 0.3 collective-permute-done.2.pair
  21.2 4.1 %collective-permute-start.4 = (bf16[272,768]{1,0:T(8,128)(2,1)S(1)}, bf16[272,768]{1,0:T(8,128)(2,1)S(1)}, u32[]{:S(2)}, u32[]{:S(2)}) collective-permute-start(bf16[272,768]{1,0:T(8,128)(2,1)S(1)} %collective-permute-done.2.pair), channel_id=1, source_target_pairs={{0,4},{4,8},{8,12},{1,5},{5,9},{9,13},{16,20},{20,24},{24,28},{17,... | collective-permute-start | bytes 1253384 | tf_op jit(solution)/shard_map/ppermute | solution.py:30
  25.3 0.0 collective-permute-done.6.late2
  25.3 0.0 copy-start.5
  25.3 0.1 collective-permute-start.5
  25.4 3.4 %collective-permute-done.7.late_pair = bf16[256,768]{1,0:T(8,128)(2,1)S(1)} collective-permute-done((bf16[256,768]{1,0:T(8,128)(2,1)}, bf16[256,768]{1,0:T(8,128)(2,1)S(1)}, u32[]{:S(2)}, u32[]{:S(2)}) %collective-permute-start.7) | collective-permute-done | bytes 393248 | tf_op jit(solution)/shard_map/ppermute | solution.py:35
  28.8 1.3 %collective-permute-start.8 = (bf16[256,768]{1,0:T(8,128)(2,1)S(1)}, bf16[256,768]{1,0:T(8,128)(2,1)}, u32[]{:S(2)}, u32[]{:S(2)}) collective-permute-start(bf16[256,768]{1,0:T(8,128)(2,1)S(1)} %collective-permute-done.6.late2), channel_id=1, source_target_pairs={{2,0},{4,2},{6,4},{8,6},{10,8},{12,10},{14,12},{3,1},{5,3},{7,5},{... | collective-permute-start | bytes 1179656 | tf_op jit(solution)/shard_map/ppermute | solution.py:24
  30.1 0.0 collective-permute-done.partner
  30.1 0.0 copy-start.2
  30.1 1.4 %collective-permute-start.9 = (bf16[256,768]{1,0:T(8,128)(2,1)S(1)}, bf16[256,768]{1,0:T(8,128)(2,1)}, u32[]{:S(2)}, u32[]{:S(2)}) collective-permute-start(bf16[256,768]{1,0:T(8,128)(2,1)S(1)} %collective-permute-done.7.late_pair), channel_id=1, source_target_pairs={{6,2},{10,6},{14,10},{7,3},{11,7},{15,11},{22,18},{26,22},{30,26},... | collective-permute-start | bytes 1179656 | tf_op jit(solution)/shard_map/ppermute | solution.py:30
  31.5 4.6 %collective-permute-done.3.near3 = bf16[272,768]{1,0:T(8,128)(2,1)S(1)} collective-permute-done((bf16[272,768]{1,0:T(8,128)(2,1)S(1)}, bf16[272,768]{1,0:T(8,128)(2,1)S(1)}, u32[]{:S(2)}, u32[]{:S(2)}) %collective-permute-start.3) | collective-permute-done | bytes 417824 | tf_op jit(solution)/shard_map/ppermute | solution.py:24
  36.2 0.0 collective-permute-done.4.near1
  36.2 0.0 copy-done
  36.2 0.0 copy-done.1
  36.2 0.0 copy-done.2
  36.2 0.7 copy-done.3
  36.9 0.2 copy-done.4
  37.1 7.3 %shard_map.111 = (bf16[128,768]{1,0:T(8,128)(2,1)}, bf16[128,768]{1,0:T(8,128)(2,1)}, f32[24,128]{1,0:T(8,128)}, f32[24,128]{1,0:T(8,128)}, f32[24,128]{1,0:T(8,...) custom-call(s32[1]{0:T(128)} %bitcast.frame, s32[1,2]{1,0:T(1,128)} %listed.1, bf16[256,768]{1,0:T(8,128)(2,1)} %get-tuple-element.16.qo, ...), custom_call_target="tpu_custom_call" | custom-call | tf_op jit(solution)/shard_map/pallas_call | solution.py:232
  44.3 0.0 copy-done.5
  44.3 0.0 copy-done.6
  44.3 0.1 collective-permute-start.14
  44.4 1.4 %collective-permute-done.14 = f32[8,768]{1,0:T(8,128)S(1)} collective-permute-done((f32[8,768]{1,0:T(8,128)}, f32[8,768]{1,0:T(8,128)S(1)}, u32[]{:S(2)}, u32[]{:S(2)}) %collective-permute-start.14) | collective-permute-done | bytes 24608 | tf_op jit(solution)/shard_map/ppermute | solution.py:39
  45.8 0.7 add.12
  46.6 2.5 %collective-permute-start.15 = (f32[8,768]{1,0:T(8,128)S(1)}, f32[8,768]{1,0:T(8,128)S(1)}, u32[]{:S(2)}, u32[]{:S(2)}) collective-permute-start(f32[8,768]{1,0:T(8,128)S(1)} %add.12), channel_id=1, source_target_pairs={{0,2},{2,0},{4,6},{6,4},{8,10},{10,8},{12,14},{14,12},{1,3},{3,1},... | collective-permute-start | bytes 73736 | tf_op jit(solution)/shard_map/ppermute | solution.py:206
  49.0 1.8 %collective-permute-done.15 = f32[8,768]{1,0:T(8,128)S(1)} collective-permute-done((f32[8,768]{1,0:T(8,128)S(1)}, f32[8,768]{1,0:T(8,128)S(1)}, u32[]{:S(2)}, u32[]{:S(2)}) %collective-permute-start.15) | collective-permute-done | bytes 24608 | tf_op jit(solution)/shard_map/ppermute | solution.py:206
  50.9 0.0 copy-start.13
  50.9 0.0 copy-start.11
  50.9 6.0 %collective-permute-start.16 = (f32[8,768]{1,0:T(8,128)S(1)}, f32[8,768]{1,0:T(8,128)S(1)}, u32[]{:S(2)}, u32[]{:S(2)}) collective-permute-start(f32[8,768]{1,0:T(8,128)S(1)} %add.13), channel_id=1, source_target_pairs={{0,4},{2,6},{4,0},{6,2},{8,12},{10,14},{12,8},{14,10},{1,5},{3,7},... | collective-permute-start | bytes 73736 | tf_op jit(solution)/shard_map/ppermute | solution.py:206
  56.9 1.8 %collective-permute-done.16 = f32[8,768]{1,0:T(8,128)S(1)} collective-permute-done((f32[8,768]{1,0:T(8,128)S(1)}, f32[8,768]{1,0:T(8,128)S(1)}, u32[]{:S(2)}, u32[]{:S(2)}) %collective-permute-start.16) | collective-permute-done | bytes 24608 | tf_op jit(solution)/shard_map/ppermute | solution.py:206
  58.7 3.8 %collective-permute-start.17 = (f32[8,768]{1,0:T(8,128)S(1)}, f32[8,768]{1,0:T(8,128)S(1)}, u32[]{:S(2)}, u32[]{:S(2)}) collective-permute-start(f32[8,768]{1,0:T(8,128)S(1)} %add.14), channel_id=1, source_target_pairs={{0,8},{2,10},{4,12},{6,14},{8,0},{10,2},{12,4},{14,6},{1,9},{3,11}... | collective-permute-start | bytes 73736 | tf_op jit(solution)/shard_map/ppermute | solution.py:206
  62.5 0.0 copy-done.15
  62.5 1.3 %collective-permute-start.11 = (f32[24,128]{1,0:T(8,128)S(1)}, f32[24,128]{1,0:T(8,128)S(1)}, u32[]{:S(2)}, u32[]{:S(2)}) collective-permute-start(f32[24,128]{1,0:T(8,128)S(1)} %copy-done.15), channel_id=1, source_target_pairs={{2,0},{4,2},{6,4},{8,6},{10,8},{12,10},{14,12},{3,1},{5,3},{7,5},{... | collective-permute-start | bytes 36872 | tf_op jit(solution)/shard_map/ppermute | solution.py:24
  63.8 0.0 collective-permute-done.5.qo_partner
  63.8 0.0 copy-start.7
  63.8 0.0 copy-done.14
  63.8 1.3 %collective-permute-start.12 = (f32[24,128]{1,0:T(8,128)S(1)}, f32[24,128]{1,0:T(8,128)S(1)}, u32[]{:S(2)}, u32[]{:S(2)}) collective-permute-start(f32[24,128]{1,0:T(8,128)S(1)} %copy-done.14), channel_id=1, source_target_pairs={{4,0},{6,2},{8,4},{10,6},{12,8},{14,10},{5,1},{7,3},{9,5},{11,7},{... | collective-permute-start | bytes 36872 | tf_op jit(solution)/shard_map/ppermute | solution.py:24
  65.1 0.0 collective-permute-done.8.late3
  65.1 0.0 copy-done.13
  65.1 1.3 %collective-permute-start.13 = (f32[24,128]{1,0:T(8,128)S(1)}, f32[24,128]{1,0:T(8,128)S(1)}, u32[]{:S(2)}, u32[]{:S(2)}) collective-permute-start(f32[24,128]{1,0:T(8,128)S(1)} %copy-done.13), channel_id=1, source_target_pairs={{6,0},{8,2},{10,4},{12,6},{14,8},{7,1},{9,3},{11,5},{13,7},{15,9},... | collective-permute-start | bytes 36872 | tf_op jit(solution)/shard_map/ppermute | solution.py:24
  66.4 0.0 collective-permute-done.9.late1
  66.4 0.0 copy-done.11
  66.4 0.1 collective-permute-start.10
  66.5 1.2 %collective-permute-done.10.stats_partner = f32[16,128]{1,0:T(8,128)S(1)} collective-permute-done((f32[16,128]{1,0:T(8,128)S(1)}, f32[16,128]{1,0:T(8,128)S(1)}, u32[]{:S(2)}, u32[]{:S(2)}) %collective-permute-start.10) | collective-permute-done | bytes 8224 | tf_op jit(solution)/shard_map/ppermute | solution.py:39
  67.7 0.4 collective-permute-done.11.stats1
  68.1 3.5 %collective-permute-done.12.stats2 = f32[24,128]{1,0:T(8,128)S(1)} collective-permute-done((f32[24,128]{1,0:T(8,128)S(1)}, f32[24,128]{1,0:T(8,128)S(1)}, u32[]{:S(2)}, u32[]{:S(2)}) %collective-permute-start.12) | collective-permute-done | bytes 12320 | tf_op jit(solution)/shard_map/ppermute | solution.py:24
  71.6 1.8 %collective-permute-done.13.stats3 = f32[24,128]{1,0:T(8,128)S(1)} collective-permute-done((f32[24,128]{1,0:T(8,128)S(1)}, f32[24,128]{1,0:T(8,128)S(1)}, u32[]{:S(2)}, u32[]{:S(2)}) %collective-permute-start.13) | collective-permute-done | bytes 12320 | tf_op jit(solution)/shard_map/ppermute | solution.py:24
  73.4 0.0 copy-done.7
  73.4 0.0 copy-done.12
  73.4 0.0 copy-done.8
  73.4 0.0 copy-done.9
  73.4 0.0 copy-start.10
  73.5 0.6 copy-done.10
  74.0 5.0 %shard_map.112 = (bf16[128,768]{1,0:T(8,128)(2,1)}, bf16[128,768]{1,0:T(8,128)(2,1)}) custom-call(s32[1]{0:T(128)} %bitcast.frame, bf16[272,768]{1,0:T(8,128)(2,1)} %get-tuple-element.17.own, bf16[256,768]{1,0:T(8,128)(2,1)} %get-tuple-element.16.qo, bf16[256,768]{1,0:T(8,128)(2,1)} %copy-done.7, bf16[256,768]{1,0:T(8,128)(2,1)} %copy-done.5, ...), custom_call_target="tpu_custom_call" | custom-call | tf_op jit(solution)/shard_map/pallas_call | solution.py:251
  79.0 0.0 collective-permute-done.17
  79.0 0.6 add.15
  (11 shorter events, 0.0 us)
Async XLA Ops:
  3.4 14.1 %collective-permute-start.1 = (bf16[272,768]{1,0:T(8,128)(2,1)}, bf16[272,768]{1,0:T(8,128)(2,1)S(1)}, u32[]{:S(2)}, u32[]{:S(2)}) collective-permute-start(bf16[272,768]{1,0:T(8,128)(2,1)} %get-tuple-element.17.own), channel_id=1, source_target_pairs={{0,4},{2,6},{4,8},{6,10},{8,12},{10,14},{1,5},{3,7},{5,9},{7,11},{... | collective-permute-start | bytes 1253384 | tf_op jit(solution)/shard_map/ppermute | solution.py:24
  8.4 12.8 %collective-permute-start.2 = (bf16[272,768]{1,0:T(8,128)(2,1)}, bf16[272,768]{1,0:T(8,128)(2,1)S(1)}, u32[]{:S(2)}, u32[]{:S(2)}) collective-permute-start(bf16[272,768]{1,0:T(8,128)(2,1)} %get-tuple-element.17.own), channel_id=1, source_target_pairs={{0,2},{2,0},{4,6},{6,4},{8,10},{10,8},{12,14},{14,12},{1,3},{3,1},... | collective-permute-start | bytes 1253384 | tf_op jit(solution)/shard_map/ppermute | solution.py:35
  9.9 20.1 %collective-permute-start = (bf16[272,768]{1,0:T(8,128)(2,1)}, bf16[272,768]{1,0:T(8,128)(2,1)S(1)}, u32[]{:S(2)}, u32[]{:S(2)}) collective-permute-start(bf16[272,768]{1,0:T(8,128)(2,1)} %get-tuple-element.17.own), channel_id=1, source_target_pairs={{0,1},{1,0},{2,3},{3,2},{4,5},{5,4},{6,7},{7,6},{8,9},{9,8},{10,11... | collective-permute-start | bytes 1253384 | tf_op jit(solution)/shard_map/ppermute | solution.py:39
  9.9 15.3 %collective-permute-start.6 = (bf16[256,768]{1,0:T(8,128)(2,1)}, bf16[256,768]{1,0:T(8,128)(2,1)S(1)}, u32[]{:S(2)}, u32[]{:S(2)}) collective-permute-start(bf16[256,768]{1,0:T(8,128)(2,1)} %get-tuple-element.16.qo), channel_id=1, source_target_pairs={{4,0},{6,2},{8,4},{10,6},{12,8},{14,10},{5,1},{7,3},{9,5},{11,7},{... | collective-permute-start | bytes 1179656 | tf_op jit(solution)/shard_map/ppermute | solution.py:24
  11.2 17.5 %collective-permute-start.7 = (bf16[256,768]{1,0:T(8,128)(2,1)}, bf16[256,768]{1,0:T(8,128)(2,1)S(1)}, u32[]{:S(2)}, u32[]{:S(2)}) collective-permute-start(bf16[256,768]{1,0:T(8,128)(2,1)} %get-tuple-element.16.qo), channel_id=1, source_target_pairs={{0,2},{2,0},{4,6},{6,4},{8,10},{10,8},{12,14},{14,12},{1,3},{3,1},... | collective-permute-start | bytes 1179656 | tf_op jit(solution)/shard_map/ppermute | solution.py:35
  17.6 18.6 %copy-start = (bf16[272,768]{1,0:T(8,128)(2,1)}, bf16[272,768]{1,0:T(8,128)(2,1)S(1)}, u32[]{:S(2)}) copy-start(bf16[272,768]{1,0:T(8,128)(2,1)S(1)} %collective-permute-done.1.near2) | copy-start | bytes 1253380
  17.6 18.6 %collective-permute-start.3 = (bf16[272,768]{1,0:T(8,128)(2,1)S(1)}, bf16[272,768]{1,0:T(8,128)(2,1)S(1)}, u32[]{:S(2)}, u32[]{:S(2)}) collective-permute-start(bf16[272,768]{1,0:T(8,128)(2,1)S(1)} %collective-permute-done.1.near2), channel_id=1, source_target_pairs={{0,2},{2,4},{4,6},{6,8},{8,10},{10,12},{12,14},{1,3},{3,5},{5,7},{... | collective-permute-start | bytes 1253384 | tf_op jit(solution)/shard_map/ppermute | solution.py:24
  21.2 14.9 %copy-start.1 = (bf16[272,768]{1,0:T(8,128)(2,1)}, bf16[272,768]{1,0:T(8,128)(2,1)S(1)}, u32[]{:S(2)}) copy-start(bf16[272,768]{1,0:T(8,128)(2,1)S(1)} %collective-permute-done.2.pair) | copy-start | bytes 1253380
  21.2 14.9 %collective-permute-start.4 = (bf16[272,768]{1,0:T(8,128)(2,1)S(1)}, bf16[272,768]{1,0:T(8,128)(2,1)S(1)}, u32[]{:S(2)}, u32[]{:S(2)}) collective-permute-start(bf16[272,768]{1,0:T(8,128)(2,1)S(1)} %collective-permute-done.2.pair), channel_id=1, source_target_pairs={{0,4},{4,8},{8,12},{1,5},{5,9},{9,13},{16,20},{20,24},{24,28},{17,... | collective-permute-start | bytes 1253384 | tf_op jit(solution)/shard_map/ppermute | solution.py:30
  25.3 19.0 %copy-start.5 = (bf16[256,768]{1,0:T(8,128)(2,1)}, bf16[256,768]{1,0:T(8,128)(2,1)S(1)}, u32[]{:S(2)}) copy-start(bf16[256,768]{1,0:T(8,128)(2,1)S(1)} %collective-permute-done.6.late2) | copy-start | bytes 1179652
  25.3 38.5 %collective-permute-start.5 = (bf16[256,768]{1,0:T(8,128)(2,1)}, bf16[256,768]{1,0:T(8,128)(2,1)S(1)}, u32[]{:S(2)}, u32[]{:S(2)}) collective-permute-start(bf16[256,768]{1,0:T(8,128)(2,1)} %get-tuple-element.16.qo), channel_id=1, source_target_pairs={{0,1},{1,0},{2,3},{3,2},{4,5},{5,4},{6,7},{7,6},{8,9},{9,8},{10,11... | collective-permute-start | bytes 1179656 | tf_op jit(solution)/shard_map/ppermute | solution.py:39
  28.8 15.6 %copy-start.6 = (bf16[256,768]{1,0:T(8,128)(2,1)}, bf16[256,768]{1,0:T(8,128)(2,1)S(1)}, u32[]{:S(2)}) copy-start(bf16[256,768]{1,0:T(8,128)(2,1)S(1)} %collective-permute-done.7.late_pair) | copy-start | bytes 1179652
  28.8 36.3 %collective-permute-start.8 = (bf16[256,768]{1,0:T(8,128)(2,1)S(1)}, bf16[256,768]{1,0:T(8,128)(2,1)}, u32[]{:S(2)}, u32[]{:S(2)}) collective-permute-start(bf16[256,768]{1,0:T(8,128)(2,1)S(1)} %collective-permute-done.6.late2), channel_id=1, source_target_pairs={{2,0},{4,2},{6,4},{8,6},{10,8},{12,10},{14,12},{3,1},{5,3},{7,5},{... | collective-permute-start | bytes 1179656 | tf_op jit(solution)/shard_map/ppermute | solution.py:24
  30.1 6.1 %copy-start.2 = (bf16[272,768]{1,0:T(8,128)(2,1)}, bf16[272,768]{1,0:T(8,128)(2,1)S(1)}, u32[]{:S(2)}) copy-start(bf16[272,768]{1,0:T(8,128)(2,1)S(1)} %collective-permute-done.partner) | copy-start | bytes 1253380
  30.1 36.3 %collective-permute-start.9 = (bf16[256,768]{1,0:T(8,128)(2,1)S(1)}, bf16[256,768]{1,0:T(8,128)(2,1)}, u32[]{:S(2)}, u32[]{:S(2)}) collective-permute-start(bf16[256,768]{1,0:T(8,128)(2,1)S(1)} %collective-permute-done.7.late_pair), channel_id=1, source_target_pairs={{6,2},{10,6},{14,10},{7,3},{11,7},{15,11},{22,18},{26,22},{30,26},... | collective-permute-start | bytes 1179656 | tf_op jit(solution)/shard_map/ppermute | solution.py:30
  36.2 0.8 copy-start.3
  36.2 0.9 %copy-start.4 = (bf16[272,768]{1,0:T(8,128)(2,1)}, bf16[272,768]{1,0:T(8,128)(2,1)S(1)}, u32[]{:S(2)}) copy-start(bf16[272,768]{1,0:T(8,128)(2,1)S(1)} %collective-permute-done.4.near1) | copy-start | bytes 1253380
  44.3 1.5 %collective-permute-start.14 = (f32[8,768]{1,0:T(8,128)}, f32[8,768]{1,0:T(8,128)S(1)}, u32[]{:S(2)}, u32[]{:S(2)}) collective-permute-start(f32[8,768]{1,0:T(8,128)} %get-tuple-element.26), channel_id=1, source_target_pairs={{0,1},{1,0},{2,3},{3,2},{4,5},{5,4},{6,7},{7,6},{8,9},{9,8},{10,11... | collective-permute-start | bytes 73736 | tf_op jit(solution)/shard_map/ppermute | solution.py:39
  46.6 4.3 %collective-permute-start.15 = (f32[8,768]{1,0:T(8,128)S(1)}, f32[8,768]{1,0:T(8,128)S(1)}, u32[]{:S(2)}, u32[]{:S(2)}) collective-permute-start(f32[8,768]{1,0:T(8,128)S(1)} %add.12), channel_id=1, source_target_pairs={{0,2},{2,0},{4,6},{6,4},{8,10},{10,8},{12,14},{14,12},{1,3},{3,1},... | collective-permute-start | bytes 73736 | tf_op jit(solution)/shard_map/ppermute | solution.py:206
  50.8 11.6 %copy-start.15 = (f32[24,128]{1,0:T(8,128)S(1)}, f32[24,128]{1,0:T(8,128)}, u32[]{:S(2)}) copy-start(f32[24,128]{1,0:T(8,128)} %get-tuple-element.21) | copy-start | bytes 36868
  50.8 12.9 %copy-start.14 = (f32[24,128]{1,0:T(8,128)S(1)}, f32[24,128]{1,0:T(8,128)}, u32[]{:S(2)}) copy-start(f32[24,128]{1,0:T(8,128)} %get-tuple-element.22) | copy-start | bytes 36868
  50.9 14.3 %copy-start.13 = (f32[24,128]{1,0:T(8,128)S(1)}, f32[24,128]{1,0:T(8,128)}, u32[]{:S(2)}) copy-start(f32[24,128]{1,0:T(8,128)} %get-tuple-element.23) | copy-start | bytes 36868
  50.9 15.6 %copy-start.11 = (f32[16,128]{1,0:T(8,128)S(1)}, f32[16,128]{1,0:T(8,128)}, u32[]{:S(2)}) copy-start(f32[16,128]{1,0:T(8,128)} %get-tuple-element.20.stats_own) | copy-start | bytes 24580
  50.9 7.8 %collective-permute-start.16 = (f32[8,768]{1,0:T(8,128)S(1)}, f32[8,768]{1,0:T(8,128)S(1)}, u32[]{:S(2)}, u32[]{:S(2)}) collective-permute-start(f32[8,768]{1,0:T(8,128)S(1)} %add.13), channel_id=1, source_target_pairs={{0,4},{2,6},{4,0},{6,2},{8,12},{10,14},{12,8},{14,10},{1,5},{3,7},... | collective-permute-start | bytes 73736 | tf_op jit(solution)/shard_map/ppermute | solution.py:206
  58.7 20.3 %collective-permute-start.17 = (f32[8,768]{1,0:T(8,128)S(1)}, f32[8,768]{1,0:T(8,128)S(1)}, u32[]{:S(2)}, u32[]{:S(2)}) collective-permute-start(f32[8,768]{1,0:T(8,128)S(1)} %add.14), channel_id=1, source_target_pairs={{0,8},{2,10},{4,12},{6,14},{8,0},{10,2},{12,4},{14,6},{1,9},{3,11}... | collective-permute-start | bytes 73736 | tf_op jit(solution)/shard_map/ppermute | solution.py:206
  62.5 5.6 %collective-permute-start.11 = (f32[24,128]{1,0:T(8,128)S(1)}, f32[24,128]{1,0:T(8,128)S(1)}, u32[]{:S(2)}, u32[]{:S(2)}) collective-permute-start(f32[24,128]{1,0:T(8,128)S(1)} %copy-done.15), channel_id=1, source_target_pairs={{2,0},{4,2},{6,4},{8,6},{10,8},{12,10},{14,12},{3,1},{5,3},{7,5},{... | collective-permute-start | bytes 36872 | tf_op jit(solution)/shard_map/ppermute | solution.py:24
  63.8 9.7 %copy-start.7 = (bf16[256,768]{1,0:T(8,128)(2,1)}, bf16[256,768]{1,0:T(8,128)(2,1)S(1)}, u32[]{:S(2)}) copy-start(bf16[256,768]{1,0:T(8,128)(2,1)S(1)} %collective-permute-done.5.qo_partner) | copy-start | bytes 1179652
  63.8 7.8 %collective-permute-start.12 = (f32[24,128]{1,0:T(8,128)S(1)}, f32[24,128]{1,0:T(8,128)S(1)}, u32[]{:S(2)}, u32[]{:S(2)}) collective-permute-start(f32[24,128]{1,0:T(8,128)S(1)} %copy-done.14), channel_id=1, source_target_pairs={{4,0},{6,2},{8,4},{10,6},{12,8},{14,10},{5,1},{7,3},{9,5},{11,7},{... | collective-permute-start | bytes 36872 | tf_op jit(solution)/shard_map/ppermute | solution.py:24
  65.1 8.3 %collective-permute-start.13 = (f32[24,128]{1,0:T(8,128)S(1)}, f32[24,128]{1,0:T(8,128)S(1)}, u32[]{:S(2)}, u32[]{:S(2)}) collective-permute-start(f32[24,128]{1,0:T(8,128)S(1)} %copy-done.13), channel_id=1, source_target_pairs={{6,0},{8,2},{10,4},{12,6},{14,8},{7,1},{9,3},{11,5},{13,7},{15,9},... | collective-permute-start | bytes 36872 | tf_op jit(solution)/shard_map/ppermute | solution.py:24
  66.4 1.2 %collective-permute-start.10 = (f32[16,128]{1,0:T(8,128)S(1)}, f32[16,128]{1,0:T(8,128)S(1)}, u32[]{:S(2)}, u32[]{:S(2)}) collective-permute-start(f32[16,128]{1,0:T(8,128)S(1)} %copy-done.11), channel_id=1, source_target_pairs={{0,1},{1,0},{2,3},{3,2},{4,5},{5,4},{6,7},{7,6},{8,9},{9,8},{10,11... | collective-permute-start | bytes 24584 | tf_op jit(solution)/shard_map/ppermute | solution.py:39
  67.7 5.8 %copy-start.12 = (f32[16,128]{1,0:T(8,128)}, f32[16,128]{1,0:T(8,128)S(1)}, u32[]{:S(2)}) copy-start(f32[16,128]{1,0:T(8,128)S(1)} %collective-permute-done.10.stats_partner) | copy-start | bytes 24580
  68.1 5.4 %copy-start.8 = (f32[24,128]{1,0:T(8,128)}, f32[24,128]{1,0:T(8,128)S(1)}, u32[]{:S(2)}) copy-start(f32[24,128]{1,0:T(8,128)S(1)} %collective-permute-done.11.stats1) | copy-start | bytes 36868
  71.6 1.8 %copy-start.9 = (f32[24,128]{1,0:T(8,128)}, f32[24,128]{1,0:T(8,128)S(1)}, u32[]{:S(2)}) copy-start(f32[24,128]{1,0:T(8,128)S(1)} %collective-permute-done.12.stats2) | copy-start | bytes 36868
  73.4 0.6 copy-start.10

commit v2 on v1

v2 whole, which is shorter than its diff:
```python
import math

import jax
import jax.numpy as jnp
from jax import lax
from jax.experimental import pallas as pl
from jax.experimental.pallas import tpu as pltpu
from jax.sharding import PartitionSpec as P

HEADS = 8
HEAD_DIM = 96
LANES = 128
SCALE = 1.0 / math.sqrt(HEAD_DIM)
STAT_ROWS = 24
ACTIONS = 8
EXP2_SCALE = SCALE * math.log2(math.e)
ACTION_ROWS = 16
MASKED = 1e30
F32 = jnp.float32
BF16 = jnp.bfloat16
VMEM_LIMIT = 56 * 1024 * 1024


def shift(block, distance):
    frames = range(lax.axis_size("tm"))
    return lax.ppermute(block, "tm", [(i - distance, i) for i in frames if i - distance in frames])


def shift_some(block, distance, parity):
    frames = range(lax.axis_size("tm"))
    route = [(i - distance, i) for i in frames if i - distance in frames and i % 2 == parity]
    return lax.ppermute(block, "tm", route)


def swap_pair(block):
    frames = range(lax.axis_size("tm"))
    return lax.ppermute(block, "tm", [(i, i ^ 1) for i in frames if i ^ 1 in frames])


def swap_row(block):
    return lax.ppermute(block, "row", [(0, 1), (1, 0)])


def pair_span(pair):
    first = 2 * pair * HEAD_DIM
    low = first // LANES * LANES
    high = -(-(first + 2 * HEAD_DIM) // LANES) * LANES
    return slice(low, high), (first - low, first - low + HEAD_DIM)


def split_pair(part, starts):
    lane = lax.broadcasted_iota(jnp.int32, part.shape, 1)
    none = jnp.zeros_like(part)
    return jnp.concatenate([jnp.where((lane >= start) & (lane < start + HEAD_DIM), part, none) for start in starts], axis=0)


def merge_pair(stacked, starts):
    half = stacked.shape[0] // 2
    lane = lax.broadcasted_iota(jnp.int32, (half, stacked.shape[1]), 1)
    return jnp.where(lane < starts[1], stacked[0:half], stacked[half:])


def join_pairs(parts):
    tiles = []
    for low in range(0, HEADS * HEAD_DIM, LANES):
        tile = None
        for pair in range(HEADS // 2):
            span, _ = pair_span(pair)
            if span.start <= low < span.stop:
                piece = parts[pair][:, low - span.start : low - span.start + LANES]
                if tile is None:
                    tile = piece
                else:
                    lane = lax.broadcasted_iota(jnp.int32, piece.shape, 1) + low
                    tile = jnp.where(lane >= 2 * pair * HEAD_DIM, piece, tile)
        tiles.append(tile)
    return tiles


def dot_t(left, right):
    return lax.dot_general(left, right, (((1,), (1,)), ((), ())), preferred_element_type=F32)


def dot(left, right):
    return jnp.dot(left, right, preferred_element_type=F32)


def prepare_kernel(actions, keys, values, table, queries, d_out, kv, qo):
    rows = values.shape[0]
    action = actions[0]
    chosen = jnp.zeros((1, table.shape[1]), F32)
    for label in range(table.shape[0]):
        row = table[label : label + 1, :].astype(F32)
        chosen = jnp.where(action == label, row, chosen)
    kv[0:rows, :] = keys[...]
    kv[rows : 2 * rows, :] = (values[...].astype(F32) + chosen).astype(BF16)
    kv[2 * rows :, :] = jnp.full((ACTION_ROWS, values.shape[1]), action.astype(F32), F32).astype(BF16)
    qo[0:rows, :] = queries[...]
    qo[rows:, :] = d_out[...]


def forward_kernel(frame, listed, queries, d_out, own, partner, near2, pair, near3, near1,
                   attended, grad_queries, row_message, all_k, all_v):
    rows = queries.shape[0]
    frame_id = frame[0]
    odd = frame_id % 2
    for index, source in ((0, own), (1, partner)):
        all_k[index * rows : (index + 1) * rows, :] = source[0:rows, :]
        all_v[index * rows : (index + 1) * rows, :] = source[rows : 2 * rows, :]
    present = []
    for slot in range(2):
        distance = listed[0, slot]
        code = jnp.where(distance == 1, jnp.where(odd == 1, 0, 1), distance)
        begin = (2 + slot) * rows
        for value, source in ((0, pair), (1, near1), (2, near2), (3, near3)):
            @pl.when(code == value)
            def _(begin=begin, source=source, slot=slot):
                all_k[begin : begin + rows, :] = source[0:rows, :]
                all_v[begin : begin + rows, :] = source[rows : 2 * rows, :]
                all_v[(4 * rows + slot * ACTION_ROWS) : (4 * rows + (slot + 1) * ACTION_ROWS), :] = source[2 * rows :, :]
        present.append(frame_id >= distance)
    lane = lax.broadcasted_iota(jnp.int32, (rows, LANES), 1)
    group_row = lax.broadcasted_iota(jnp.int32, (4 * rows, LANES), 0) // rows
    group_lane = lax.broadcasted_iota(jnp.int32, (4 * rows, LANES), 1)
    members = (jnp.maximum(group_row - 1, 0) == group_lane).astype(BF16)
    columns = jnp.zeros((rows, LANES), F32)
    out_parts, query_parts, sums = [], [], [[], [], []]
    for pair in range(HEADS // 2):
        span, starts = pair_span(pair)
        query = split_pair(queries[:, span], starts)
        grad = split_pair(d_out[:, span], starts)
        key = all_k[0 : 4 * rows, span]
        value = all_v[0 : 4 * rows, span]
        scores = dot_t(query, key)
        scores = [scores[:, 0 : 2 * rows]] + [
            jnp.where(present[slot], scores[:, (2 + slot) * rows : (3 + slot) * rows], -MASKED) for slot in range(2)
        ]
        scores = jnp.concatenate(scores, axis=1)
        highest = jnp.max(scores, axis=1, keepdims=True)
        weights = jnp.exp2((scores - highest) * EXP2_SCALE)
        total = jnp.sum(weights, axis=1, keepdims=True)
        probs = weights * (1.0 / total)
        probs_low = probs.astype(BF16)
        out = dot(probs_low, value)
        d_probs = dot_t(grad, value)
        wide = grad.astype(F32)
        centre = jnp.sum(wide * out, axis=1, keepdims=True)
        d_scores = (probs * (d_probs - centre)).astype(BF16)
        out_parts.append(merge_pair(out, starts))
        query_parts.append(merge_pair(dot(d_scores, key), starts))
        log_total = highest * EXP2_SCALE + jnp.log2(total)
        for half in range(2):
            picked = slice(half * rows, (half + 1) * rows)
            columns = jnp.where(lane == 2 * pair + half, log_total[picked], columns)
            columns = jnp.where(lane == HEADS + 2 * pair + half, centre[picked], columns)
        mass = dot(probs_low, members)
        for group in range(3):
            sums[group].append(jnp.sum(wide * mass[:, group : group + 1], axis=0, keepdims=True))
    out_tiles, query_tiles = join_pairs(out_parts), join_pairs(query_parts)
    attended[...] = jnp.concatenate(out_tiles, axis=1).astype(BF16)
    grad_queries[...] = (jnp.concatenate(query_tiles, axis=1) * SCALE).astype(BF16)
    turned = columns.T
    row_message[0 : 2 * HEADS, :] = turned[0 : 2 * HEADS, :]
    which = lax.broadcasted_iota(jnp.int32, (HEADS, LANES), 0)
    in_list = (which == listed[0, 0]) | (which == listed[0, 1])
    row_message[2 * HEADS : STAT_ROWS, :] = jnp.where(in_list, 1.0, 0.0)
    tiles = [add_pairs(parts) for parts in sums]
    label = lax.broadcasted_iota(jnp.int32, (ACTIONS, LANES), 0).astype(F32)
    for index in range(len(tiles[0])):
        totals = jnp.zeros((ACTIONS, LANES), F32)
        cut = slice(index * LANES, (index + 1) * LANES)
        actions = [own[2 * rows :, cut]]
        actions += [all_v[4 * rows + slot * ACTION_ROWS : 4 * rows + (slot + 1) * ACTION_ROWS, cut] for slot in range(2)]
        for group in range(3):
            action = actions[group].astype(F32)[0:1, :]
            totals = totals + jnp.where(label == action, tiles[group][index], 0.0)
        row_message[STAT_ROWS + index * ACTIONS : STAT_ROWS + (index + 1) * ACTIONS, :] = totals


def add_pairs(parts):
    tiles = []
    for low in range(0, HEADS * HEAD_DIM, LANES):
        tile = None
        for pair in range(HEADS // 2):
            span, _ = pair_span(pair)
            if span.start <= low < span.stop:
                piece = parts[pair][:, low - span.start : low - span.start + LANES]
                tile = piece if tile is None else tile + piece
        tiles.append(tile)
    return tiles


def backward_pairs(own, queries, grads, log_totals, centres):
    rows = (own.shape[0] - ACTION_ROWS) // 2
    key_parts, value_parts = [], []
    for pair in range(HEADS // 2):
        span, starts = pair_span(pair)
        key = split_pair(own[0:rows, span], starts)
        value = split_pair(own[rows : 2 * rows, span], starts)
        query = queries[:, span]
        grad = grads[:, span]
        scores = dot_t(key, query)
        d_probs = dot_t(value, grad)
        low, d_low = [], []
        for half in range(2):
            head = 2 * pair + half
            cut = slice(half * rows, (half + 1) * rows)
            probs = jnp.exp2(scores[cut] * EXP2_SCALE - log_totals[head : head + 1, :])
            low.append(probs.astype(BF16))
            d_low.append((probs * (d_probs[cut] - centres[head : head + 1, :])).astype(BF16))
        value_parts.append(merge_pair(dot(jnp.concatenate(low, axis=0), grad), starts))
        key_parts.append(merge_pair(dot(jnp.concatenate(d_low, axis=0), query), starts))
    return jnp.concatenate(join_pairs(key_parts), axis=1), jnp.concatenate(join_pairs(value_parts), axis=1)


def near_backward_kernel(own, qo, qo_partner, row_own, row_partner, near_keys, near_values, all_q, all_g):
    rows = qo.shape[0] // 2
    for index, source in ((0, qo), (1, qo_partner)):
        all_q[index * rows : (index + 1) * rows, :] = source[0:rows, :]
        all_g[index * rows : (index + 1) * rows, :] = source[rows:, :]
    log_totals = jnp.concatenate([row_own[0:HEADS, :], row_partner[0:HEADS, :]], axis=1)
    centres = jnp.concatenate([row_own[HEADS : 2 * HEADS, :], row_partner[HEADS : 2 * HEADS, :]], axis=1)
    near_keys[...], near_values[...] = backward_pairs(own, all_q, all_g, log_totals, centres)


def far_backward_kernel(frame, own, late2, late_pair, late3, late1, stats, near_keys, near_values,
                        grad_keys, grad_values, all_q, all_g):
    rows = late2.shape[0] // 2
    frame_id = frame[0]
    odd = frame_id % 2
    for index, source in ((1, late2), (2, late3)):
        all_q[index * rows : (index + 1) * rows, :] = source[0:rows, :]
        all_g[index * rows : (index + 1) * rows, :] = source[rows:, :]
    for value, source in ((0, late_pair), (1, late1)):
        @pl.when(odd == value)
        def _(source=source):
            all_q[0:rows, :] = source[0:rows, :]
            all_g[0:rows, :] = source[rows:, :]
    log_totals, centres = [], []
    for distance in (1, 2, 3):
        later = frame_id + distance
        exists = later < stats.shape[0]
        block = stats[jnp.where(exists, later ^ frame_id, 0)]
        uses = exists & (block[2 * HEADS + distance : 2 * HEADS + distance + 1, :] > 0.5)
        log_totals.append(jnp.where(uses, block[0:HEADS, :], MASKED))
        centres.append(block[HEADS : 2 * HEADS, :])
    log_totals = jnp.concatenate(log_totals, axis=1)
    centres = jnp.concatenate(centres, axis=1)
    far_keys, far_values = backward_pairs(own, all_q, all_g, log_totals, centres)
    grad_keys[...] = ((near_keys[...] + far_keys) * SCALE).astype(BF16)
    grad_values[...] = (near_values[...] + far_values).astype(BF16)


def vmem(count):
    return [pl.BlockSpec(memory_space=pltpu.VMEM)] * count


def smem(count):
    return [pl.BlockSpec(memory_space=pltpu.SMEM)] * count


def params():
    return pltpu.CompilerParams(vmem_limit_bytes=VMEM_LIMIT)


def call(kernel, outs, scalars, arrays, scratch=()):
    return pl.pallas_call(
        kernel,
        out_shape=outs,
        in_specs=smem(len(scalars)) + vmem(len(arrays)),
        out_specs=jax.tree.map(lambda _: pl.BlockSpec(memory_space=pltpu.VMEM), outs),
        scratch_shapes=list(scratch),
        compiler_params=params(),
        cost_estimate=pl.CostEstimate(flops=100000000000, transcendentals=1, bytes_accessed=1000),
    )(*scalars, *arrays)


def share(message):
    frames = lax.axis_size("tm")
    stats, table = message[:STAT_ROWS], message[STAT_ROWS:]
    gathered = stats[None]
    if frames & (frames - 1):
        around = lax.all_gather(stats, "tm")
        order = lax.iota(jnp.int32, 1 << (frames - 1).bit_length()) ^ lax.axis_index("tm").astype(jnp.int32)
        return lax.psum(table, "tm"), jnp.take(around, jnp.minimum(order, frames - 1), axis=0)
    step = 1
    while step < frames:
        if step > 1:
            message = jnp.concatenate([gathered.reshape(-1, LANES), table])
        message = lax.ppermute(message, "tm", [(i, i ^ step) for i in range(frames)])
        table = table + message[step * STAT_ROWS :]
        gathered = jnp.concatenate([gathered, message[: step * STAT_ROWS].reshape(gathered.shape)])
        step *= 2
    return table, gathered


def on_device(queries, keys, values, d_out, action_table, actions, temporal_list):
    rows, width = queries.shape
    tiles = width // LANES
    frame = lax.axis_index("tm").astype(jnp.int32).reshape(1)
    shape = jax.ShapeDtypeStruct
    kv, qo = call(
        prepare_kernel,
        (shape((2 * rows + ACTION_ROWS, width), BF16), shape((2 * rows, width), BF16)),
        [actions],
        [keys, values, action_table, queries, d_out],
    )
    near2, pair = shift(kv, 2), swap_pair(kv)
    late2, late_pair = shift(qo, -2), swap_pair(qo)
    partner, qo_partner = swap_row(kv), swap_row(qo)
    near3, near1 = shift(near2, 1), shift_some(pair, 2, 0)
    late3 = shift(late2, -1)
    late1 = shift_some(late_pair, -2, 1)
    attended, grad_queries, row_message = call(
        forward_kernel,
        (
            shape((rows, width), BF16),
            shape((rows, width), BF16),
            shape((STAT_ROWS + tiles * ACTIONS, LANES), F32),
        ),
        [frame, temporal_list],
        [queries, d_out, kv, partner, near2, pair, near3, near1],
        [pltpu.VMEM((4 * rows, width), BF16), pltpu.VMEM((4 * rows + 2 * ACTION_ROWS, width), BF16)],
    )
    row_partner = swap_row(row_message[:STAT_ROWS])
    table, stats = share(row_message)
    table = table + swap_row(table)
    near_keys, near_values = call(
        near_backward_kernel,
        (shape((rows, width), F32), shape((rows, width), F32)),
        [],
        [kv, qo, qo_partner, row_message, row_partner],
        [pltpu.VMEM((2 * rows, width), BF16), pltpu.VMEM((2 * rows, width), BF16)],
    )
    grad_table = table.reshape(tiles, ACTIONS, LANES).transpose(1, 0, 2).reshape(ACTIONS, width)
    grad_keys, grad_values = call(
        far_backward_kernel,
        (shape((rows, width), BF16), shape((rows, width), BF16)),
        [frame],
        [kv, late2, late_pair, late3, late1, stats, near_keys, near_values],
        [pltpu.VMEM((3 * rows, width), BF16), pltpu.VMEM((3 * rows, width), BF16)],
    )
    return attended, grad_queries, grad_keys, grad_values, grad_table


def solution(mesh):
    split = P(("grp", "tm", "row"), None)
    return jax.shard_map(
        on_device,
        mesh=mesh,
        in_specs=(split, split, split, split, P(), P(("grp", "tm")), split),
        out_specs=(split, split, split, split, P("grp", None)),
        check_vma=False,
    )
```

time: 80.5 us -> 72.1 us (0.90)
  the two profiles are of different devices: /device:TPU:0 before, /device:TPU:3 now
where the time goes in v2:
time: 72.1 us; the launch traced here: 71.7 us
  starting transfers between devices  32.5 us (45%)
  waiting for transfers between devices  17 us (24%)
  Pallas kernels  15.5 us (21%)
  local copies, waits for them, and re-layouts  3.86 us (5%)
  between operations  1.45 us (2%)
  other arithmetic  1.3 us (2%)
    pallas_call x4, Pallas kernels, call(): pl.pallas_call(kernel, out_shape=outs, in_specs=smem(len(scalars)) + vmem...  15.5 us
    ppermute x4, starting transfers between devices, shift(): lax.ppermute(block, 'tm', [(i - distance, i) for i in frames if i - dista...  11.6 us
    ppermute x4, waiting for transfers between devices, shift(): lax.ppermute(block, 'tm', [(i - distance, i) for i in frames if i - dista...  9.71 us
    ppermute x3, starting transfers between devices, share(): lax.ppermute(message, 'tm', [(i, i ^ step) for i in range(frames)])  8.14 us
    ppermute x4, starting transfers between devices, swap_row(): return lax.ppermute(block, 'row', [(0, 1), (1, 0)])  7.72 us
    ppermute x3, waiting for transfers between devices, share(): lax.ppermute(message, 'tm', [(i, i ^ step) for i in range(frames)])  7.32 us
    ppermute x2, starting transfers between devices, swap_pair(): lax.ppermute(block, 'tm', [(i, i ^ 1) for i in frames if i ^ 1 in frames])  3.12 us
    unnamed x26, local copies, waits for them, and re-layouts  3.11 us
  transfers between devices with their start and end apart: 15, of which 4 were waited for; matrix products, arithmetic and copies ran while one was open for 2% of the time, Pallas kernels for 19%

profile of v2, /device:TPU:3, one launch (start us, length us, event | category | flops | bytes accessed | tf_op | source)
XLA Modules:
  0.0 71.7 jit_solution(10353861897671886789)
XLA Ops:
  1.3 2.2 %shard_map.110 = (bf16[272,768]{1,0:T(8,128)(2,1)}, bf16[256,768]{1,0:T(8,128)(2,1)}) custom-call(s32[1]{0:T(128)S(6)} %copy.12.actions, bf16[128,768]{1,0:T(8,128)(2,1)} %keys.1, bf16[128,768]{1,0:T(8,128)(2,1)} %values.1, bf16[8,768]{1,0:T(8,128)(2,1)} %table.1, bf16[128,768]{1,0:T(8,128)(2,1)} %queries.3, bf16[128,768]{1,0:T(8,128)(2,1)} %d_out.3), custom_call_target="tpu_custom_call" | custom-call | flops 99999997952 | bytes 1000 | tf_op jit(solution)/shard_map/pallas_call | solution.py:267
  3.5 3.2 %collective-permute-start.1 = (bf16[272,768]{1,0:T(8,128)(2,1)}, bf16[272,768]{1,0:T(8,128)(2,1)S(1)}, u32[]{:S(2)}, u32[]{:S(2)}) collective-permute-start(bf16[272,768]{1,0:T(8,128)(2,1)} %get-tuple-element.14.own), channel_id=1, source_target_pairs={{0,4},{2,6},{4,8},{6,10},{8,12},{10,14},{1,5},{3,7},{5,9},{7,11},{... | collective-permute-start | bytes 1253384 | tf_op jit(solution)/shard_map/ppermute | solution.py:26
  6.7 0.3 collective-permute-start.2
  7.0 1.2 %collective-permute-start = (bf16[272,768]{1,0:T(8,128)(2,1)}, bf16[272,768]{1,0:T(8,128)(2,1)S(1)}, u32[]{:S(2)}, u32[]{:S(2)}) collective-permute-start(bf16[272,768]{1,0:T(8,128)(2,1)} %get-tuple-element.14.own), channel_id=1, source_target_pairs={{0,1},{1,0},{2,3},{3,2},{4,5},{5,4},{6,7},{7,6},{8,9},{9,8},{10,11... | collective-permute-start | bytes 1253384 | tf_op jit(solution)/shard_map/ppermute | solution.py:41
  8.3 7.0 %collective-permute-done.1.near2 = bf16[272,768]{1,0:T(8,128)(2,1)S(1)} collective-permute-done((bf16[272,768]{1,0:T(8,128)(2,1)}, bf16[272,768]{1,0:T(8,128)(2,1)S(1)}, u32[]{:S(2)}, u32[]{:S(2)}) %collective-permute-start.1) | collective-permute-done | bytes 417824 | tf_op jit(solution)/shard_map/ppermute | solution.py:26
  15.3 0.0 copy-start.1
  15.3 4.0 %collective-permute-start.3 = (bf16[272,768]{1,0:T(8,128)(2,1)S(1)}, bf16[272,768]{1,0:T(8,128)(2,1)S(1)}, u32[]{:S(2)}, u32[]{:S(2)}) collective-permute-start(bf16[272,768]{1,0:T(8,128)(2,1)S(1)} %collective-permute-done.1.near2), channel_id=1, source_target_pairs={{0,2},{2,4},{4,6},{6,8},{8,10},{10,12},{12,14},{1,3},{3,5},{5,7},{... | collective-permute-start | bytes 1253384 | tf_op jit(solution)/shard_map/ppermute | solution.py:26
  19.3 0.0 collective-permute-done.2.pair
  19.3 0.0 copy-start.2
  19.3 0.7 collective-permute-start.4
  20.0 1.3 %collective-permute-start.5 = (bf16[256,768]{1,0:T(8,128)(2,1)}, bf16[256,768]{1,0:T(8,128)(2,1)S(1)}, u32[]{:S(2)}, u32[]{:S(2)}) collective-permute-start(bf16[256,768]{1,0:T(8,128)(2,1)} %get-tuple-element.17.qo), channel_id=1, source_target_pairs={{4,0},{6,2},{8,4},{10,6},{12,8},{14,10},{5,1},{7,3},{9,5},{11,7},{... | collective-permute-start | bytes 1179656 | tf_op jit(solution)/shard_map/ppermute | solution.py:26
  21.3 2.8 %collective-permute-start.6 = (bf16[256,768]{1,0:T(8,128)(2,1)}, bf16[256,768]{1,0:T(8,128)(2,1)S(1)}, u32[]{:S(2)}, u32[]{:S(2)}) collective-permute-start(bf16[256,768]{1,0:T(8,128)(2,1)} %get-tuple-element.17.qo), channel_id=1, source_target_pairs={{0,2},{2,0},{4,6},{6,4},{8,10},{10,8},{12,14},{14,12},{1,3},{3,1},... | collective-permute-start | bytes 1179656 | tf_op jit(solution)/shard_map/ppermute | solution.py:37
  24.1 0.0 collective-permute-done.partner
  24.1 0.0 copy-start.3
  24.1 2.7 %collective-permute-done.3.near3 = bf16[272,768]{1,0:T(8,128)(2,1)S(1)} collective-permute-done((bf16[272,768]{1,0:T(8,128)(2,1)S(1)}, bf16[272,768]{1,0:T(8,128)(2,1)S(1)}, u32[]{:S(2)}, u32[]{:S(2)}) %collective-permute-start.3) | collective-permute-done | bytes 417824 | tf_op jit(solution)/shard_map/ppermute | solution.py:26
  26.8 0.0 copy-start.4
  26.8 0.0 collective-permute-done.4.near1
  26.8 0.0 copy-start.5
  26.8 0.0 copy-done.1
  26.8 0.0 copy-done.2
  26.8 0.0 copy-done.3
  26.8 0.7 %copy-done.4 = bf16[272,768]{1,0:T(8,128)(2,1)} copy-done((bf16[272,768]{1,0:T(8,128)(2,1)}, bf16[272,768]{1,0:T(8,128)(2,1)S(1)}, u32[]{:S(2)}) %copy-start.4) | copy-done | bytes 417816
  27.5 0.2 copy-done.5
  27.7 0.0 copy-start.6
  27.7 6.3 %shard_map.111 = (bf16[128,768]{1,0:T(8,128)(2,1)}, bf16[128,768]{1,0:T(8,128)(2,1)}, f32[72,128]{1,0:T(8,128)}) custom-call(s32[1]{0:T(128)} %bitcast.frame, s32[1,2]{1,0:T(1,128)} %listed.1, bf16[128,768]{1,0:T(8,128)(2,1)} %queries.3, bf16[128,768]{1,0:T(8,128)(2,1)} %d_out.3, bf16[272,768]{1,0:T(8,128)(2,1)} %get-tuple-element.14.own, ...), custom_call_target="tpu_custom_call" | custom-call | flops 99999997952 | bytes 1000 | tf_op jit(solution)/shard_map/pallas_call | solution.py:267
  33.9 2.9 %collective-permute-start.9 = (f32[72,128]{1,0:T(8,128)}, f32[72,128]{1,0:T(8,128)S(1)}, u32[]{:S(2)}, u32[]{:S(2)}) collective-permute-start(f32[72,128]{1,0:T(8,128)} %get-tuple-element.18.row_own), channel_id=1, source_target_pairs={{0,2},{2,0},{4,6},{6,4},{8,10},{10,8},{12,14},{14,12},{1,3},{3,1},... | collective-permute-start | bytes 110600 | tf_op jit(solution)/shard_map/ppermute | solution.py:290
  36.8 0.7 %fusion.1 = (f32[24,128]{1,0:T(8,128)S(1)}, f32[1,24,128]{2,1,0:T(8,128)S(1)}) fusion(f32[72,128]{1,0:T(8,128)} %get-tuple-element.18.row_own), kind=kLoop, calls=%fused_computation.12 | loop fusion | bytes 36864 | tf_op jit(solution)/shard_map/slice | solution.py:280
  37.5 0.0 copy-start
  37.5 0.8 %collective-permute-done.9 = f32[72,128]{1,0:T(8,128)S(1)} collective-permute-done((f32[72,128]{1,0:T(8,128)}, f32[72,128]{1,0:T(8,128)S(1)}, u32[]{:S(2)}, u32[]{:S(2)}) %collective-permute-start.9) | collective-permute-done | bytes 36896 | tf_op jit(solution)/shard_map/ppermute | solution.py:290
  38.4 0.0 copy-done
  38.4 2.3 %collective-permute-start.10 = (f32[96,128]{1,0:T(8,128)S(1)}, f32[96,128]{1,0:T(8,128)S(1)}, u32[]{:S(2)}, u32[]{:S(2)}) collective-permute-start(f32[96,128]{1,0:T(8,128)S(1)} %pad_maximum_fusion.2), channel_id=1, source_target_pairs={{0,4},{2,6},{4,0},{6,2},{8,12},{10,14},{12,8},{14,10},{1,5},{3,7},... | collective-permute-start | bytes 147464 | tf_op jit(solution)/shard_map/ppermute | solution.py:290
  40.7 0.0 copy-done.6
  40.7 4.5 %collective-permute-start.12 = (bf16[256,768]{1,0:T(8,128)(2,1)S(1)}, bf16[256,768]{1,0:T(8,128)(2,1)S(1)}, u32[]{:S(2)}, u32[]{:S(2)}) collective-permute-start(bf16[256,768]{1,0:T(8,128)(2,1)S(1)} %copy-done.6), channel_id=1, source_target_pairs={{0,1},{1,0},{2,3},{3,2},{4,5},{5,4},{6,7},{7,6},{8,9},{9,8},{10,11... | collective-permute-start | bytes 1179656 | tf_op jit(solution)/shard_map/ppermute | solution.py:41
  45.1 0.0 collective-permute-done.5.late2
  45.1 0.0 copy-start.7
  45.1 3.1 %collective-permute-start.7 = (bf16[256,768]{1,0:T(8,128)(2,1)S(1)}, bf16[256,768]{1,0:T(8,128)(2,1)S(1)}, u32[]{:S(2)}, u32[]{:S(2)}) collective-permute-start(bf16[256,768]{1,0:T(8,128)(2,1)S(1)} %collective-permute-done.5.late2), channel_id=1, source_target_pairs={{2,0},{4,2},{6,4},{8,6},{10,8},{12,10},{14,12},{3,1},{5,3},{7,5},{... | collective-permute-start | bytes 1179656 | tf_op jit(solution)/shard_map/ppermute | solution.py:26
  48.2 0.0 collective-permute-done.6.late_pair
  48.2 0.0 copy-start.8
  48.2 1.3 %collective-permute-start.8 = (bf16[256,768]{1,0:T(8,128)(2,1)S(1)}, bf16[256,768]{1,0:T(8,128)(2,1)S(1)}, u32[]{:S(2)}, u32[]{:S(2)}) collective-permute-start(bf16[256,768]{1,0:T(8,128)(2,1)S(1)} %collective-permute-done.6.late_pair), channel_id=1, source_target_pairs={{6,2},{10,6},{14,10},{7,3},{11,7},{15,11},{22,18},{26,22},{30,26},... | collective-permute-start | bytes 1179656 | tf_op jit(solution)/shard_map/ppermute | solution.py:32
  49.5 0.4 collective-permute-start.13
  49.9 0.0 collective-permute-done.10
  49.9 3.0 %collective-permute-start.11 = (f32[144,128]{1,0:T(8,128)S(1)}, f32[144,128]{1,0:T(8,128)S(1)}, u32[]{:S(2)}, u32[]{:S(2)}) collective-permute-start(f32[144,128]{1,0:T(8,128)S(1)} %pad_maximum_fusion.1), channel_id=1, source_target_pairs={{0,8},{2,10},{4,12},{6,14},{8,0},{10,2},{12,4},{14,6},{1,9},{3,11}... | collective-permute-start | bytes 221192 | tf_op jit(solution)/shard_map/ppermute | solution.py:290
  53.0 0.0 collective-permute-done.12.qo_partner
  53.0 0.0 copy-start.11
  53.0 0.0 collective-permute-done.13.row_partner
  53.0 0.7 %copy-done.11 = bf16[256,768]{1,0:T(8,128)(2,1)} copy-done((bf16[256,768]{1,0:T(8,128)(2,1)}, bf16[256,768]{1,0:T(8,128)(2,1)S(1)}, u32[]{:S(2)}) %copy-start.11) | copy-done | bytes 393240
  53.7 0.0 copy-start.12
  53.7 0.6 copy-done.12
  54.3 3.2 %shard_map.112 = (f32[128,768]{1,0:T(8,128)}, f32[128,768]{1,0:T(8,128)}) custom-call(bf16[272,768]{1,0:T(8,128)(2,1)} %get-tuple-element.14.own, bf16[256,768]{1,0:T(8,128)(2,1)} %get-tuple-element.17.qo, bf16[256,768]{1,0:T(8,128)(2,1)} %copy-done.11, f32[72,128]{1,0:T(8,128)} %get-tuple-element.18.row_own, f32[24,128]{1,0:T(8,128)} %copy-done.12), custom_call_target="tpu_custom_call" | custom-call | flops 99999997952 | bytes 1000 | tf_op jit(solution)/shard_map/pallas_call | solution.py:267
  57.5 0.0 copy-done.7
  57.5 0.0 copy-done.8
  57.5 6.5 %collective-permute-done.11 = f32[144,128]{1,0:T(8,128)S(1)} collective-permute-done((f32[144,128]{1,0:T(8,128)S(1)}, f32[144,128]{1,0:T(8,128)S(1)}, u32[]{:S(2)}, u32[]{:S(2)}) %collective-permute-start.11) | collective-permute-done | bytes 73760 | tf_op jit(solution)/shard_map/ppermute | solution.py:290
  64.0 1.7 %collective-permute-start.14 = (f32[48,128]{1,0:T(8,128)S(1)}, f32[48,128]{1,0:T(8,128)S(1)}, u32[]{:S(2)}, u32[]{:S(2)}) collective-permute-start(f32[48,128]{1,0:T(8,128)S(1)} %slice_add_fusion), channel_id=1, source_target_pairs={{0,1},{1,0},{2,3},{3,2},{4,5},{5,4},{6,7},{7,6},{8,9},{9,8},{10,11... | collective-permute-start | bytes 73736 | tf_op jit(solution)/shard_map/ppermute | solution.py:41
  65.7 0.6 pad_maximum_fusion.stats
  66.3 0.0 collective-permute-done.7.late3
  66.3 0.0 copy-start.9
  66.3 0.0 collective-permute-done.8.late1
  66.3 0.0 copy-start.10
  66.4 0.7 %copy-done.9 = bf16[256,768]{1,0:T(8,128)(2,1)} copy-done((bf16[256,768]{1,0:T(8,128)(2,1)}, bf16[256,768]{1,0:T(8,128)(2,1)S(1)}, u32[]{:S(2)}) %copy-start.9) | copy-done | bytes 393240
  67.1 0.1 copy-done.10
  67.2 3.8 %shard_map.113 = (bf16[128,768]{1,0:T(8,128)(2,1)}, bf16[128,768]{1,0:T(8,128)(2,1)}) custom-call(s32[1]{0:T(128)} %bitcast.frame, bf16[272,768]{1,0:T(8,128)(2,1)} %get-tuple-element.14.own, bf16[256,768]{1,0:T(8,128)(2,1)} %copy-done.7, bf16[256,768]{1,0:T(8,128)(2,1)} %copy-done.8, bf16[256,768]{1,0:T(8,128)(2,1)} %copy-done.9, ...), custom_call_target="tpu_custom_call" | custom-call | flops 99999997952 | bytes 1000 | tf_op jit(solution)/shard_map/pallas_call | solution.py:267
  71.1 0.0 collective-permute-done.14
  71.1 0.6 add_bitcast_fusion
  (9 shorter events, 0.0 us)
Async XLA Ops:
  3.5 11.8 %collective-permute-start.1 = (bf16[272,768]{1,0:T(8,128)(2,1)}, bf16[272,768]{1,0:T(8,128)(2,1)S(1)}, u32[]{:S(2)}, u32[]{:S(2)}) collective-permute-start(bf16[272,768]{1,0:T(8,128)(2,1)} %get-tuple-element.14.own), channel_id=1, source_target_pairs={{0,4},{2,6},{4,8},{6,10},{8,12},{10,14},{1,5},{3,7},{5,9},{7,11},{... | collective-permute-start | bytes 1253384 | tf_op jit(solution)/shard_map/ppermute | solution.py:26
  6.7 12.6 %collective-permute-start.2 = (bf16[272,768]{1,0:T(8,128)(2,1)}, bf16[272,768]{1,0:T(8,128)(2,1)S(1)}, u32[]{:S(2)}, u32[]{:S(2)}) collective-permute-start(bf16[272,768]{1,0:T(8,128)(2,1)} %get-tuple-element.14.own), channel_id=1, source_target_pairs={{0,2},{2,0},{4,6},{6,4},{8,10},{10,8},{12,14},{14,12},{1,3},{3,1},... | collective-permute-start | bytes 1253384 | tf_op jit(solution)/shard_map/ppermute | solution.py:37
  7.0 17.1 %collective-permute-start = (bf16[272,768]{1,0:T(8,128)(2,1)}, bf16[272,768]{1,0:T(8,128)(2,1)S(1)}, u32[]{:S(2)}, u32[]{:S(2)}) collective-permute-start(bf16[272,768]{1,0:T(8,128)(2,1)} %get-tuple-element.14.own), channel_id=1, source_target_pairs={{0,1},{1,0},{2,3},{3,2},{4,5},{5,4},{6,7},{7,6},{8,9},{9,8},{10,11... | collective-permute-start | bytes 1253384 | tf_op jit(solution)/shard_map/ppermute | solution.py:41
  15.3 11.5 %copy-start.1 = (bf16[272,768]{1,0:T(8,128)(2,1)}, bf16[272,768]{1,0:T(8,128)(2,1)S(1)}, u32[]{:S(2)}) copy-start(bf16[272,768]{1,0:T(8,128)(2,1)S(1)} %collective-permute-done.1.near2) | copy-start | bytes 1253380
  15.3 11.5 %collective-permute-start.3 = (bf16[272,768]{1,0:T(8,128)(2,1)S(1)}, bf16[272,768]{1,0:T(8,128)(2,1)S(1)}, u32[]{:S(2)}, u32[]{:S(2)}) collective-permute-start(bf16[272,768]{1,0:T(8,128)(2,1)S(1)} %collective-permute-done.1.near2), channel_id=1, source_target_pairs={{0,2},{2,4},{4,6},{6,8},{8,10},{10,12},{12,14},{1,3},{3,5},{5,7},{... | collective-permute-start | bytes 1253384 | tf_op jit(solution)/shard_map/ppermute | solution.py:26
  19.3 7.5 %copy-start.2 = (bf16[272,768]{1,0:T(8,128)(2,1)}, bf16[272,768]{1,0:T(8,128)(2,1)S(1)}, u32[]{:S(2)}) copy-start(bf16[272,768]{1,0:T(8,128)(2,1)S(1)} %collective-permute-done.2.pair) | copy-start | bytes 1253380
  19.3 7.5 %collective-permute-start.4 = (bf16[272,768]{1,0:T(8,128)(2,1)S(1)}, bf16[272,768]{1,0:T(8,128)(2,1)S(1)}, u32[]{:S(2)}, u32[]{:S(2)}) collective-permute-start(bf16[272,768]{1,0:T(8,128)(2,1)S(1)} %collective-permute-done.2.pair), channel_id=1, source_target_pairs={{0,4},{4,8},{8,12},{1,5},{5,9},{9,13},{16,20},{20,24},{24,28},{17,... | collective-permute-start | bytes 1253384 | tf_op jit(solution)/shard_map/ppermute | solution.py:32
  20.0 25.1 %collective-permute-start.5 = (bf16[256,768]{1,0:T(8,128)(2,1)}, bf16[256,768]{1,0:T(8,128)(2,1)S(1)}, u32[]{:S(2)}, u32[]{:S(2)}) collective-permute-start(bf16[256,768]{1,0:T(8,128)(2,1)} %get-tuple-element.17.qo), channel_id=1, source_target_pairs={{4,0},{6,2},{8,4},{10,6},{12,8},{14,10},{5,1},{7,3},{9,5},{11,7},{... | collective-permute-start | bytes 1179656 | tf_op jit(solution)/shard_map/ppermute | solution.py:26
  21.3 26.9 %collective-permute-start.6 = (bf16[256,768]{1,0:T(8,128)(2,1)}, bf16[256,768]{1,0:T(8,128)(2,1)S(1)}, u32[]{:S(2)}, u32[]{:S(2)}) collective-permute-start(bf16[256,768]{1,0:T(8,128)(2,1)} %get-tuple-element.17.qo), channel_id=1, source_target_pairs={{0,2},{2,0},{4,6},{6,4},{8,10},{10,8},{12,14},{14,12},{1,3},{3,1},... | collective-permute-start | bytes 1179656 | tf_op jit(solution)/shard_map/ppermute | solution.py:37
  24.1 2.7 %copy-start.3 = (bf16[272,768]{1,0:T(8,128)(2,1)}, bf16[272,768]{1,0:T(8,128)(2,1)S(1)}, u32[]{:S(2)}) copy-start(bf16[272,768]{1,0:T(8,128)(2,1)S(1)} %collective-permute-done.partner) | copy-start | bytes 1253380
  26.8 0.8 %copy-start.4 = (bf16[272,768]{1,0:T(8,128)(2,1)}, bf16[272,768]{1,0:T(8,128)(2,1)S(1)}, u32[]{:S(2)}) copy-start(bf16[272,768]{1,0:T(8,128)(2,1)S(1)} %collective-permute-done.3.near3) | copy-start | bytes 1253380
  26.8 0.9 %copy-start.5 = (bf16[272,768]{1,0:T(8,128)(2,1)}, bf16[272,768]{1,0:T(8,128)(2,1)S(1)}, u32[]{:S(2)}) copy-start(bf16[272,768]{1,0:T(8,128)(2,1)S(1)} %collective-permute-done.4.near1) | copy-start | bytes 1253380
  27.7 13.0 %copy-start.6 = (bf16[256,768]{1,0:T(8,128)(2,1)S(1)}, bf16[256,768]{1,0:T(8,128)(2,1)}, u32[]{:S(2)}) copy-start(bf16[256,768]{1,0:T(8,128)(2,1)} %get-tuple-element.17.qo) | copy-start | bytes 1179652
  33.9 4.4 %collective-permute-start.9 = (f32[72,128]{1,0:T(8,128)}, f32[72,128]{1,0:T(8,128)S(1)}, u32[]{:S(2)}, u32[]{:S(2)}) collective-permute-start(f32[72,128]{1,0:T(8,128)} %get-tuple-element.18.row_own), channel_id=1, source_target_pairs={{0,2},{2,0},{4,6},{6,4},{8,10},{10,8},{12,14},{14,12},{1,3},{3,1},... | collective-permute-start | bytes 110600 | tf_op jit(solution)/shard_map/ppermute | solution.py:290
  37.5 0.8 %copy-start = (f32[72,128]{1,0:T(8,128)S(1)}, f32[72,128]{1,0:T(8,128)}, u32[]{:S(2)}) copy-start(f32[72,128]{1,0:T(8,128)} %get-tuple-element.18.row_own) | copy-start | bytes 110596
  38.4 11.5 %collective-permute-start.10 = (f32[96,128]{1,0:T(8,128)S(1)}, f32[96,128]{1,0:T(8,128)S(1)}, u32[]{:S(2)}, u32[]{:S(2)}) collective-permute-start(f32[96,128]{1,0:T(8,128)S(1)} %pad_maximum_fusion.2), channel_id=1, source_target_pairs={{0,4},{2,6},{4,0},{6,2},{8,12},{10,14},{12,8},{14,10},{1,5},{3,7},... | collective-permute-start | bytes 147464 | tf_op jit(solution)/shard_map/ppermute | solution.py:290
  40.7 12.3 %collective-permute-start.12 = (bf16[256,768]{1,0:T(8,128)(2,1)S(1)}, bf16[256,768]{1,0:T(8,128)(2,1)S(1)}, u32[]{:S(2)}, u32[]{:S(2)}) collective-permute-start(bf16[256,768]{1,0:T(8,128)(2,1)S(1)} %copy-done.6), channel_id=1, source_target_pairs={{0,1},{1,0},{2,3},{3,2},{4,5},{5,4},{6,7},{7,6},{8,9},{9,8},{10,11... | collective-permute-start | bytes 1179656 | tf_op jit(solution)/shard_map/ppermute | solution.py:41
  45.1 12.4 %copy-start.7 = (bf16[256,768]{1,0:T(8,128)(2,1)}, bf16[256,768]{1,0:T(8,128)(2,1)S(1)}, u32[]{:S(2)}) copy-start(bf16[256,768]{1,0:T(8,128)(2,1)S(1)} %collective-permute-done.5.late2) | copy-start | bytes 1179652
  45.1 21.2 %collective-permute-start.7 = (bf16[256,768]{1,0:T(8,128)(2,1)S(1)}, bf16[256,768]{1,0:T(8,128)(2,1)S(1)}, u32[]{:S(2)}, u32[]{:S(2)}) collective-permute-start(bf16[256,768]{1,0:T(8,128)(2,1)S(1)} %collective-permute-done.5.late2), channel_id=1, source_target_pairs={{2,0},{4,2},{6,4},{8,6},{10,8},{12,10},{14,12},{3,1},{5,3},{7,5},{... | collective-permute-start | bytes 1179656 | tf_op jit(solution)/shard_map/ppermute | solution.py:26
  48.2 9.3 %copy-start.8 = (bf16[256,768]{1,0:T(8,128)(2,1)}, bf16[256,768]{1,0:T(8,128)(2,1)S(1)}, u32[]{:S(2)}) copy-start(bf16[256,768]{1,0:T(8,128)(2,1)S(1)} %collective-permute-done.6.late_pair) | copy-start | bytes 1179652
  48.2 18.1 %collective-permute-start.8 = (bf16[256,768]{1,0:T(8,128)(2,1)S(1)}, bf16[256,768]{1,0:T(8,128)(2,1)S(1)}, u32[]{:S(2)}, u32[]{:S(2)}) collective-permute-start(bf16[256,768]{1,0:T(8,128)(2,1)S(1)} %collective-permute-done.6.late_pair), channel_id=1, source_target_pairs={{6,2},{10,6},{14,10},{7,3},{11,7},{15,11},{22,18},{26,22},{30,26},... | collective-permute-start | bytes 1179656 | tf_op jit(solution)/shard_map/ppermute | solution.py:32
  49.5 3.4 %collective-permute-start.13 = (f32[24,128]{1,0:T(8,128)S(1)}, f32[24,128]{1,0:T(8,128)S(1)}, u32[]{:S(2)}, u32[]{:S(2)}) collective-permute-start(f32[24,128]{1,0:T(8,128)S(1)} %get-tuple-element.25), channel_id=1, source_target_pairs={{0,1},{1,0},{2,3},{3,2},{4,5},{5,4},{6,7},{7,6},{8,9},{9,8},{10,11... | collective-permute-start | bytes 36872 | tf_op jit(solution)/shard_map/ppermute | solution.py:41
  49.9 14.1 %collective-permute-start.11 = (f32[144,128]{1,0:T(8,128)S(1)}, f32[144,128]{1,0:T(8,128)S(1)}, u32[]{:S(2)}, u32[]{:S(2)}) collective-permute-start(f32[144,128]{1,0:T(8,128)S(1)} %pad_maximum_fusion.1), channel_id=1, source_target_pairs={{0,8},{2,10},{4,12},{6,14},{8,0},{10,2},{12,4},{14,6},{1,9},{3,11}... | collective-permute-start | bytes 221192 | tf_op jit(solution)/shard_map/ppermute | solution.py:290
  53.0 0.7 %copy-start.11 = (bf16[256,768]{1,0:T(8,128)(2,1)}, bf16[256,768]{1,0:T(8,128)(2,1)S(1)}, u32[]{:S(2)}) copy-start(bf16[256,768]{1,0:T(8,128)(2,1)S(1)} %collective-permute-done.12.qo_partner) | copy-start | bytes 1179652
  53.7 0.6 copy-start.12
  64.0 7.0 %collective-permute-start.14 = (f32[48,128]{1,0:T(8,128)S(1)}, f32[48,128]{1,0:T(8,128)S(1)}, u32[]{:S(2)}, u32[]{:S(2)}) collective-permute-start(f32[48,128]{1,0:T(8,128)S(1)} %slice_add_fusion), channel_id=1, source_target_pairs={{0,1},{1,0},{2,3},{3,2},{4,5},{5,4},{6,7},{7,6},{8,9},{9,8},{10,11... | collective-permute-start | bytes 73736 | tf_op jit(solution)/shard_map/ppermute | solution.py:41
  66.3 0.7 %copy-start.9 = (bf16[256,768]{1,0:T(8,128)(2,1)}, bf16[256,768]{1,0:T(8,128)(2,1)S(1)}, u32[]{:S(2)}) copy-start(bf16[256,768]{1,0:T(8,128)(2,1)S(1)} %collective-permute-done.7.late3) | copy-start | bytes 1179652
  66.3 0.9 %copy-start.10 = (bf16[256,768]{1,0:T(8,128)(2,1)}, bf16[256,768]{1,0:T(8,128)(2,1)S(1)}, u32[]{:S(2)}) copy-start(bf16[256,768]{1,0:T(8,128)(2,1)S(1)} %collective-permute-done.8.late1) | copy-start | bytes 1179652

commit v3 on v2

v3 whole, which is shorter than its diff:
```python
import math

import jax
import jax.numpy as jnp
from jax import lax
from jax.experimental import pallas as pl
from jax.experimental.pallas import tpu as pltpu
from jax.sharding import PartitionSpec as P

HEADS = 8
HEAD_DIM = 96
LANES = 128
SCALE = 1.0 / math.sqrt(HEAD_DIM)
STAT_ROWS = 24
HOLD = True
PREP, FWD, NEAR, FAR, QUERY = 10**11, 10**10, 10**9, 10**11, 10**9
GROUP_ROWS = 16
ACTIONS = 8
EXP2_SCALE = SCALE * math.log2(math.e)
ACTION_ROWS = 16
MASKED = 1e30
F32 = jnp.float32
BF16 = jnp.bfloat16
VMEM_LIMIT = 56 * 1024 * 1024


def shift(block, distance):
    frames = range(lax.axis_size("tm"))
    return lax.ppermute(block, "tm", [(i - distance, i) for i in frames if i - distance in frames])


def shift_some(block, distance, parity):
    frames = range(lax.axis_size("tm"))
    route = [(i - distance, i) for i in frames if i - distance in frames and i % 2 == parity]
    return lax.ppermute(block, "tm", route)


def swap_pair(block):
    frames = range(lax.axis_size("tm"))
    return lax.ppermute(block, "tm", [(i, i ^ 1) for i in frames if i ^ 1 in frames])


def swap_row(block):
    return lax.ppermute(block, "row", [(0, 1), (1, 0)])


def pair_span(pair):
    first = 2 * pair * HEAD_DIM
    low = first // LANES * LANES
    high = -(-(first + 2 * HEAD_DIM) // LANES) * LANES
    return slice(low, high), (first - low, first - low + HEAD_DIM)


def split_pair(part, starts):
    lane = lax.broadcasted_iota(jnp.int32, part.shape, 1)
    none = jnp.zeros_like(part)
    return jnp.concatenate([jnp.where((lane >= start) & (lane < start + HEAD_DIM), part, none) for start in starts], axis=0)


def merge_pair(stacked, starts):
    half = stacked.shape[0] // 2
    lane = lax.broadcasted_iota(jnp.int32, (half, stacked.shape[1]), 1)
    return jnp.where(lane < starts[1], stacked[0:half], stacked[half:])


def join_pairs(parts):
    tiles = []
    for low in range(0, HEADS * HEAD_DIM, LANES):
        tile = None
        for pair in range(HEADS // 2):
            span, _ = pair_span(pair)
            if span.start <= low < span.stop:
                piece = parts[pair][:, low - span.start : low - span.start + LANES]
                if tile is None:
                    tile = piece
                else:
                    lane = lax.broadcasted_iota(jnp.int32, piece.shape, 1) + low
                    tile = jnp.where(lane >= 2 * pair * HEAD_DIM, piece, tile)
        tiles.append(tile)
    return tiles


def dot_t(left, right):
    return lax.dot_general(left, right, (((1,), (1,)), ((), ())), preferred_element_type=F32)


def dot(left, right):
    return jnp.dot(left, right, preferred_element_type=F32)


def prepare_kernel(actions, keys, values, table, queries, d_out, kv, qo):
    rows = values.shape[0]
    action = actions[...]
    label = lax.broadcasted_iota(jnp.int32, table.shape, 0)
    chosen = jnp.sum(jnp.where(label == action, table[...].astype(F32), 0.0), axis=0, keepdims=True)
    kv[0:rows, :] = keys[...]
    kv[rows : 2 * rows, :] = (values[...].astype(F32) + chosen).astype(BF16)
    kv[2 * rows :, :] = jnp.broadcast_to(action.astype(F32), (ACTION_ROWS, values.shape[1])).astype(BF16)
    qo[0:rows, :] = queries[...]
    qo[rows:, :] = d_out[...]


def forward_kernel(frame, listed, own_action, queries, d_out, own, partner, near2, pair, near3, near1,
                   row_message, attended, d_low, picked):
    rows = queries.shape[0]
    frame_id = frame[0]
    odd = frame_id % 2
    present = []
    for slot in range(2):
        distance = listed[0, slot]
        code = jnp.where(distance == 1, jnp.where(odd == 1, 0, 1), distance)
        for value, source in ((0, pair), (1, near1), (2, near2), (3, near3)):
            @pl.when(code == value)
            def _(source=source, slot=slot):
                picked[slot] = source[...]
        present.append(frame_id >= distance)
    blocks = [own, partner, picked.at[0], picked.at[1]]
    lane = lax.broadcasted_iota(jnp.int32, (rows, LANES), 1)
    member_row = lax.broadcasted_iota(jnp.int32, (GROUP_ROWS, 4 * rows), 0)
    member_block = lax.broadcasted_iota(jnp.int32, (GROUP_ROWS, 4 * rows), 1) // rows
    members = jnp.where(jnp.maximum(member_block - 1, 0) == member_row, 1.0, 0.0).astype(BF16)
    columns = jnp.zeros((rows, LANES), F32)
    out_parts, sums = [], [[], [], []]
    for pair in range(HEADS // 2):
        span, starts = pair_span(pair)
        query = split_pair(queries[:, span], starts)
        grad = split_pair(d_out[:, span], starts)
        key = jnp.concatenate([block[0:rows, span] for block in blocks], axis=0)
        value = jnp.concatenate([block[rows : 2 * rows, span] for block in blocks], axis=0)
        scores = dot_t(query, key)
        scores = [scores[:, 0 : 2 * rows]] + [
            jnp.where(present[slot], scores[:, (2 + slot) * rows : (3 + slot) * rows], -MASKED) for slot in range(2)
        ]
        scores = jnp.concatenate(scores, axis=1)
        highest = jnp.max(scores, axis=1, keepdims=True)
        weights = jnp.exp2((scores - highest) * EXP2_SCALE)
        total = jnp.sum(weights, axis=1, keepdims=True)
        probs = weights * (1.0 / total)
        probs_low = probs.astype(BF16)
        out = dot(probs_low, value)
        d_probs = dot_t(grad, value)
        centre = jnp.sum(grad.astype(F32) * out, axis=1, keepdims=True)
        d_low[pair] = (probs * (d_probs - centre)).astype(BF16)
        out_parts.append(merge_pair(out, starts))
        log_total = highest * EXP2_SCALE + jnp.log2(total)
        for half in range(2):
            cut = slice(half * rows, (half + 1) * rows)
            columns = jnp.where(lane == 2 * pair + half, log_total[cut], columns)
            columns = jnp.where(lane == HEADS + 2 * pair + half, centre[cut], columns)
        mass = dot_t(members, probs_low)
        mass_high = mass.astype(BF16)
        mass_low = (mass - mass_high.astype(F32)).astype(BF16)
        weighted = dot(jnp.concatenate([mass_high, mass_low], axis=0), grad)
        weighted = weighted[0:GROUP_ROWS] + weighted[GROUP_ROWS:]
        for group in range(3):
            sums[group].append(weighted[group : group + 1])
    attended[...] = jnp.concatenate(join_pairs(out_parts), axis=1).astype(BF16)
    turned = columns.T
    row_message[0 : 2 * HEADS, :] = turned[0 : 2 * HEADS, :]
    which = lax.broadcasted_iota(jnp.int32, (HEADS, LANES), 0)
    in_list = (which == listed[0, 0]) | (which == listed[0, 1])
    row_message[2 * HEADS : STAT_ROWS, :] = jnp.where(in_list, 1.0, 0.0)
    tiles = [add_pairs(parts) for parts in sums]
    label = lax.broadcasted_iota(jnp.int32, (ACTIONS, LANES), 0).astype(F32)
    for index in range(len(tiles[0])):
        totals = jnp.zeros((ACTIONS, LANES), F32)
        cut = slice(index * LANES, (index + 1) * LANES)
        actions = [own_action[0].astype(F32)] + [picked[slot, 2 * rows :, cut].astype(F32)[0:1, :] for slot in range(2)]
        for group in range(3):
            action = actions[group]
            totals = totals + jnp.where(label == action, tiles[group][index], 0.0)
        row_message[STAT_ROWS + index * ACTIONS : STAT_ROWS + (index + 1) * ACTIONS, :] = totals


def query_kernel(own, partner, picked, d_low, held, attended, grad_queries):
    rows = held.shape[0]
    parts = []
    for pair in range(HEADS // 2):
        span, starts = pair_span(pair)
        key = jnp.concatenate([block[0:rows, span] for block in (own, partner, picked.at[0], picked.at[1])], axis=0)
        parts.append(merge_pair(dot(d_low[pair], key), starts))
    grad_queries[...] = (jnp.concatenate(join_pairs(parts), axis=1) * SCALE).astype(BF16)
    attended[...] = held[...]


def add_pairs(parts):
    tiles = []
    for low in range(0, HEADS * HEAD_DIM, LANES):
        tile = None
        for pair in range(HEADS // 2):
            span, _ = pair_span(pair)
            if span.start <= low < span.stop:
                piece = parts[pair][:, low - span.start : low - span.start + LANES]
                tile = piece if tile is None else tile + piece
        tiles.append(tile)
    return tiles


def backward_pairs(own, sources, log_totals, centres):
    rows = (own.shape[0] - ACTION_ROWS) // 2
    key_parts, value_parts = [], []
    for pair in range(HEADS // 2):
        span, starts = pair_span(pair)
        key = split_pair(own[0:rows, span], starts)
        value = split_pair(own[rows : 2 * rows, span], starts)
        query = jnp.concatenate([source(slice(0, rows), span) for source in sources], axis=0)
        grad = jnp.concatenate([source(slice(rows, 2 * rows), span) for source in sources], axis=0)
        scores = dot_t(key, query)
        d_probs = dot_t(value, grad)
        low, d_low = [], []
        for half in range(2):
            head = 2 * pair + half
            cut = slice(half * rows, (half + 1) * rows)
            probs = jnp.exp2(scores[cut] * EXP2_SCALE - log_totals[head : head + 1, :])
            low.append(probs.astype(BF16))
            d_low.append((probs * (d_probs[cut] - centres[head : head + 1, :])).astype(BF16))
        value_parts.append(merge_pair(dot(jnp.concatenate(low, axis=0), grad), starts))
        key_parts.append(merge_pair(dot(jnp.concatenate(d_low, axis=0), query), starts))
    return jnp.concatenate(join_pairs(key_parts), axis=1), jnp.concatenate(join_pairs(value_parts), axis=1)


def reader(ref):
    return lambda rows, lanes: ref[rows, lanes]


def near_backward_kernel(own, row_own, row_partner, qo, qo_partner, near_keys, near_values):
    log_totals = jnp.concatenate([row_own[0:HEADS, :], row_partner[0:HEADS, :]], axis=1)
    centres = jnp.concatenate([row_own[HEADS : 2 * HEADS, :], row_partner[HEADS : 2 * HEADS, :]], axis=1)
    sources = [reader(qo), reader(qo_partner)]
    near_keys[...], near_values[...] = backward_pairs(own, sources, log_totals, centres)


def reverse_bits(index, count):
    bits = (count - 1).bit_length()
    return sum(((index >> bit) & 1) << (bits - 1 - bit) for bit in range(bits))


def far_backward_kernel(frame, own, stats, near_keys, near_values, late2, late_pair, late3, late1,
                        grad_keys, grad_values):
    frame_id = frame[0]
    odd = frame_id % 2 == 1
    sources = [lambda rows, lanes: jnp.where(odd, late1[rows, lanes], late_pair[rows, lanes]), reader(late2), reader(late3)]
    log_totals, centres = [], []
    for distance in (1, 2, 3):
        later = frame_id + distance
        exists = later < stats.shape[0]
        block = stats[jnp.where(exists, reverse_bits(later ^ frame_id, stats.shape[0]), 0)]
        uses = exists & (block[2 * HEADS + distance : 2 * HEADS + distance + 1, :] > 0.5)
        log_totals.append(jnp.where(uses, block[0:HEADS, :], MASKED))
        centres.append(block[HEADS : 2 * HEADS, :])
    log_totals = jnp.concatenate(log_totals, axis=1)
    centres = jnp.concatenate(centres, axis=1)
    far_keys, far_values = backward_pairs(own, sources, log_totals, centres)
    grad_keys[...] = ((near_keys[...] + far_keys) * SCALE).astype(BF16)
    grad_values[...] = (near_values[...] + far_values).astype(BF16)


VMEM, SMEM = pltpu.VMEM, pltpu.SMEM


def call(kernel, flops, outs, scalars, arrays, scratch=()):
    return pl.pallas_call(
        kernel,
        out_shape=tuple(pltpu.VMEM(shape, dtype) if stays else jax.ShapeDtypeStruct(shape, dtype) for shape, dtype, stays in outs),
        in_specs=[pl.BlockSpec(memory_space=SMEM)] * len(scalars) + [pl.BlockSpec(memory_space=VMEM)] * len(arrays),
        out_specs=(pl.BlockSpec(memory_space=VMEM),) * len(outs),
        scratch_shapes=list(scratch),
        compiler_params=pltpu.CompilerParams(vmem_limit_bytes=VMEM_LIMIT),
        cost_estimate=pl.CostEstimate(flops=flops, transcendentals=0, bytes_accessed=0),
    )(*scalars, *[pltpu.with_memory_space_constraint(array, VMEM) if hold else array for array, hold in arrays])


def share(message):
    frames = lax.axis_size("tm")
    stats, table = message[:STAT_ROWS], message[STAT_ROWS:]
    gathered = stats[None]
    if frames & (frames - 1):
        around = lax.all_gather(stats, "tm")
        count = 1 << (frames - 1).bit_length()
        order = reverse_bits(lax.iota(jnp.int32, count), count) ^ lax.axis_index("tm").astype(jnp.int32)
        return lax.psum(table, "tm"), jnp.take(around, jnp.minimum(order, frames - 1), axis=0)
    count = 1
    while count < frames:
        if count > 1:
            message = jnp.concatenate([gathered.reshape(-1, LANES), table])
        steps = [frames // (2 * count)]
        if 4 * count <= frames:
            steps += [frames // (4 * count), 3 * frames // (4 * count)]
        arrived = [lax.ppermute(message, "tm", [(i, i ^ step) for i in range(frames)]) for step in steps]
        table = table + sum(other[count * STAT_ROWS :] for other in arrived)
        gathered = jnp.concatenate([gathered] + [other[: count * STAT_ROWS].reshape(gathered.shape) for other in arrived])
        count *= len(steps) + 1
    return table, gathered


def on_device(queries, keys, values, d_out, action_table, actions, temporal_list):
    rows, width = queries.shape
    tiles = width // LANES
    frame = lax.axis_index("tm").astype(jnp.int32).reshape(1)
    wide = (rows, width)
    kv, qo = call(
        prepare_kernel,
        PREP,
        [((2 * rows + ACTION_ROWS, width), BF16, HOLD), ((2 * rows, width), BF16, HOLD)],
        [],
        [(array, False) for array in (actions.reshape(1, 1), keys, values, action_table, queries, d_out)],
    )
    near2, pair = shift(kv, 2), swap_pair(kv)
    late2, late_pair = shift(qo, -2), swap_pair(qo)
    partner, qo_partner = swap_row(kv), swap_row(qo)
    near3, near1 = shift(near2, 1), shift_some(pair, 2, 0)

    row_message, held, d_low, picked = call(
        forward_kernel,
        FWD,
        [
            ((STAT_ROWS + tiles * ACTIONS, LANES), F32, HOLD),
            (wide, BF16, HOLD),
            ((HEADS // 2, 2 * rows, 4 * rows), BF16, HOLD),
            ((2, 2 * rows + ACTION_ROWS, width), BF16, HOLD),
        ],
        [frame, temporal_list, actions],
        [(queries, False), (d_out, False)] + [(block, HOLD) for block in (kv, partner, near2, pair, near3, near1)],
    )
    attended, grad_queries = call(
        query_kernel,
        QUERY,
        [(wide, BF16, False), (wide, BF16, False)],
        [],
        [(block, HOLD) for block in (kv, partner, picked, d_low, held)],
    )
    late2, late_pair, _ = lax.optimization_barrier((late2, late_pair, held))
    late3 = shift(late2, -1)
    late1 = shift_some(late_pair, -2, 1)
    row_partner = swap_row(row_message[:STAT_ROWS])
    table, stats = share(row_message)
    table_partner = swap_row(table)
    near_keys, near_values = call(
        near_backward_kernel,
        NEAR,
        [(wide, F32, HOLD), (wide, F32, HOLD)],
        [],
        [(array, HOLD) for array in (kv, row_message, row_partner, qo, qo_partner)],
    )
    grad_keys, grad_values = call(
        far_backward_kernel,
        FAR,
        [(wide, BF16, False), (wide, BF16, False)],
        [frame],
        [(array, HOLD) for array in (kv, stats, near_keys, near_values, late2, late_pair, late3, late1)],
    )
    table_partner, grad_keys = lax.optimization_barrier((table_partner, grad_keys))
    table = table + table_partner
    grad_table = table.reshape(tiles, ACTIONS, LANES).transpose(1, 0, 2).reshape(ACTIONS, width)
    return attended, grad_queries, grad_keys, grad_values, grad_table


def solution(mesh):
    split = P(("grp", "tm", "row"), None)
    return jax.shard_map(
        on_device,
        mesh=mesh,
        in_specs=(split, split, split, split, P(), P(("grp", "tm")), split),
        out_specs=(split, split, split, split, P("grp", None)),
        check_vma=False,
    )
```

time: 72.1 us -> 60.1 us (0.83)
  the two profiles are of different devices: /device:TPU:3 before, /device:TPU:0 now
where the time goes in v3:
time: 60.1 us; the launch traced here: 59.8 us
  starting transfers between devices  26.1 us (43%)
  waiting for transfers between devices  20.6 us (34%)
  Pallas kernels  10.9 us (18%)
  between operations  1.48 us (2%)
  other arithmetic  0.64 us (1%)
    ppermute x4, starting transfers between devices, shift(): lax.ppermute(block, 'tm', [(i - distance, i) for i in frames if i - dista...  10.9 us
    pallas_call x5, Pallas kernels, call(): pl.pallas_call(kernel, out_shape=tuple((pltpu.VMEM(shape, dtype) if stays...  10.9 us
    ppermute x4, waiting for transfers between devices, shift(): lax.ppermute(block, 'tm', [(i - distance, i) for i in frames if i - dista...  10.6 us
    ppermute x4, starting transfers between devices, share(): lax.ppermute(message, 'tm', [(i, i ^ step) for i in range(frames)])  8.35 us
    ppermute x4, waiting for transfers between devices, share(): lax.ppermute(message, 'tm', [(i, i ^ step) for i in range(frames)])  7.09 us
    ppermute x2, starting transfers between devices, shift_some(): return lax.ppermute(block, 'tm', route)  5.08 us
    ppermute x2, waiting for transfers between devices, shift_some(): return lax.ppermute(block, 'tm', route)  2.96 us
    ppermute x2, starting transfers between devices, swap_pair(): lax.ppermute(block, 'tm', [(i, i ^ 1) for i in frames if i ^ 1 in frames])  1.63 us
  transfers between devices with their start and end apart: 16, of which 5 were waited for; matrix products, arithmetic and copies ran while one was open for 0% of the time, Pallas kernels for 16%

profile of v3, /device:TPU:0, one launch (start us, length us, event | category | flops | bytes accessed | tf_op | source)
XLA Modules:
  0.0 59.8 jit_solution(17304504412916019062)
XLA Ops:
  1.3 1.4 %shard_map.110 = (bf16[272,768]{1,0:T(8,128)(2,1)S(1)}, bf16[256,768]{1,0:T(8,128)(2,1)S(1)}) custom-call(s32[1,1]{1,0:T(1,128)} %bitcast.25.actions, bf16[128,768]{1,0:T(8,128)(2,1)} %keys.1, bf16[128,768]{1,0:T(8,128)(2,1)} %values.1, bf16[8,768]{1,0:T(8,128)(2,1)} %table.1, bf16[128,768]{1,0:T(8,128)(2,1)} %queries.3, bf16[128,768]{1,0:T(8,128)(2,1)} %d_out.3), custom_call_target="tpu_custom_call" | custom-call | flops 99999997952 | tf_op jit(solution)/shard_map/pallas_call | solution.py:262
  2.6 5.0 %collective-permute-start.1 = (bf16[272,768]{1,0:T(8,128)(2,1)S(1)}, bf16[272,768]{1,0:T(8,128)(2,1)S(1)}, u32[]{:S(2)}, u32[]{:S(2)}) collective-permute-start(bf16[272,768]{1,0:T(8,128)(2,1)S(1)} %get-tuple-element.21.own), channel_id=1, source_target_pairs={{0,4},{2,6},{4,8},{6,10},{8,12},{10,14},{1,5},{3,7},{5,9},{7,11},{... | collective-permute-start | bytes 1253384 | tf_op jit(solution)/shard_map/ppermute | solution.py:29
  7.6 1.6 %collective-permute-start.2 = (bf16[272,768]{1,0:T(8,128)(2,1)S(1)}, bf16[272,768]{1,0:T(8,128)(2,1)S(1)}, u32[]{:S(2)}, u32[]{:S(2)}) collective-permute-start(bf16[272,768]{1,0:T(8,128)(2,1)S(1)} %get-tuple-element.21.own), channel_id=1, source_target_pairs={{0,2},{2,0},{4,6},{6,4},{8,10},{10,8},{12,14},{14,12},{1,3},{3,1},... | collective-permute-start | bytes 1253384 | tf_op jit(solution)/shard_map/ppermute | solution.py:40
  9.2 0.0 collective-permute-start
  9.2 7.3 %collective-permute-done.1.near2 = bf16[272,768]{1,0:T(8,128)(2,1)S(1)} collective-permute-done((bf16[272,768]{1,0:T(8,128)(2,1)S(1)}, bf16[272,768]{1,0:T(8,128)(2,1)S(1)}, u32[]{:S(2)}, u32[]{:S(2)}) %collective-permute-start.1) | collective-permute-done | bytes 417824 | tf_op jit(solution)/shard_map/ppermute | solution.py:29
  16.5 3.4 %collective-permute-start.3 = (bf16[272,768]{1,0:T(8,128)(2,1)S(1)}, bf16[272,768]{1,0:T(8,128)(2,1)S(1)}, u32[]{:S(2)}, u32[]{:S(2)}) collective-permute-start(bf16[272,768]{1,0:T(8,128)(2,1)S(1)} %collective-permute-done.1.near2), channel_id=1, source_target_pairs={{0,2},{2,4},{4,6},{6,8},{8,10},{10,12},{12,14},{1,3},{3,5},{5,7},{... | collective-permute-start | bytes 1253384 | tf_op jit(solution)/shard_map/ppermute | solution.py:29
  19.9 0.0 collective-permute-done.2.pair
  19.9 4.4 %collective-permute-start.4 = (bf16[272,768]{1,0:T(8,128)(2,1)S(1)}, bf16[272,768]{1,0:T(8,128)(2,1)S(1)}, u32[]{:S(2)}, u32[]{:S(2)}) collective-permute-start(bf16[272,768]{1,0:T(8,128)(2,1)S(1)} %collective-permute-done.2.pair), channel_id=1, source_target_pairs={{0,4},{4,8},{8,12},{1,5},{5,9},{9,13},{16,20},{20,24},{24,28},{17,... | collective-permute-start | bytes 1253384 | tf_op jit(solution)/shard_map/ppermute | solution.py:35
  24.3 0.1 collective-permute-start.11
  24.4 1.3 %collective-permute-start.12 = (bf16[256,768]{1,0:T(8,128)(2,1)S(1)}, bf16[256,768]{1,0:T(8,128)(2,1)S(1)}, u32[]{:S(2)}, u32[]{:S(2)}) collective-permute-start(bf16[256,768]{1,0:T(8,128)(2,1)S(1)} %get-tuple-element.28.qo), channel_id=1, source_target_pairs={{4,0},{6,2},{8,4},{10,6},{12,8},{14,10},{5,1},{7,3},{9,5},{11,7},{... | collective-permute-start | bytes 1179656 | tf_op jit(solution)/shard_map/ppermute | solution.py:29
  25.7 0.0 collective-permute-done.partner
  25.7 0.1 collective-permute-start.13
  25.8 3.3 %collective-permute-done.3.near3 = bf16[272,768]{1,0:T(8,128)(2,1)S(1)} collective-permute-done((bf16[272,768]{1,0:T(8,128)(2,1)S(1)}, bf16[272,768]{1,0:T(8,128)(2,1)S(1)}, u32[]{:S(2)}, u32[]{:S(2)}) %collective-permute-start.3) | collective-permute-done | bytes 417824 | tf_op jit(solution)/shard_map/ppermute | solution.py:29
  29.0 3.0 %collective-permute-done.4.near1 = bf16[272,768]{1,0:T(8,128)(2,1)S(1)} collective-permute-done((bf16[272,768]{1,0:T(8,128)(2,1)S(1)}, bf16[272,768]{1,0:T(8,128)(2,1)S(1)}, u32[]{:S(2)}, u32[]{:S(2)}) %collective-permute-start.4) | collective-permute-done | bytes 417824 | tf_op jit(solution)/shard_map/ppermute | solution.py:35
  32.0 4.3 %shard_map.111 = (f32[72,128]{1,0:T(8,128)S(1)}, bf16[128,768]{1,0:T(8,128)(2,1)S(1)}, bf16[4,256,512]{2,1,0:T(8,128)(2,1)S(1)}, bf16[2,272,768]{2,1,0:T(8,128)(2,1)S(1)}) custom-call(s32[1]{0:T(128)} %bitcast.1.frame, s32[1,2]{1,0:T(1,128)} %listed.1, s32[1]{0:T(128)} %copy.16.own_action, bf16[128,768]{1,0:T(8,128)(2,1)} %queries.3, ...), custom_call_target="tpu_custom_call" | custom-call | flops 10000000000 | tf_op jit(solution)/shard_map/pallas_call | solution.py:262
  36.3 4.5 %collective-permute-start.7 = (f32[72,128]{1,0:T(8,128)S(1)}, f32[72,128]{1,0:T(8,128)S(1)}, u32[]{:S(2)}, u32[]{:S(2)}) collective-permute-start(f32[72,128]{1,0:T(8,128)S(1)} %get-tuple-element.27.row_own), channel_id=1, source_target_pairs={{0,12},{2,14},{4,8},{6,10},{8,4},{10,6},{12,0},{14,2},{1,13},{3,15... | collective-permute-start | bytes 110600 | tf_op jit(solution)/shard_map/ppermute | solution.py:289
  40.8 0.0 collective-permute-start.10
  40.8 1.1 %shard_map.112 = (bf16[128,768]{1,0:T(8,128)(2,1)}, bf16[128,768]{1,0:T(8,128)(2,1)}) custom-call(bf16[272,768]{1,0:T(8,128)(2,1)S(1)} %get-tuple-element.21.own, bf16[272,768]{1,0:T(8,128)(2,1)S(1)} %collective-permute-done.partner, bf16[2,272,768]{2,1,0:T(8,128)(2,1)S(1)} %get-tuple-element.22.picked, bf16[4,256,512]{2,1,0:T(8,128)(2,1)S(1)} %get-tuple-element.23.d_low, ...), custom_call_target="tpu_custom_call" | custom-call | flops 1000000000 | tf_op jit(solution)/shard_map/pallas_call | solution.py:262
  42.0 0.0 collective-permute-done.12.late2
  42.0 0.0 collective-permute-start.6
  42.0 0.0 collective-permute-done.13.late_pair
  42.0 0.7 %collective-permute-start.5 = (f32[72,128]{1,0:T(8,128)S(1)}, f32[72,128]{1,0:T(8,128)S(1)}, u32[]{:S(2)}, u32[]{:S(2)}) collective-permute-start(f32[72,128]{1,0:T(8,128)S(1)} %get-tuple-element.27.row_own), channel_id=1, source_target_pairs={{0,8},{2,10},{4,12},{6,14},{8,0},{10,2},{12,4},{14,6},{1,9},{3,11}... | collective-permute-start | bytes 110600 | tf_op jit(solution)/shard_map/ppermute | solution.py:289
  42.6 0.0 collective-permute-done.11.qo_partner
  42.6 1.3 %collective-permute-start.14 = (bf16[256,768]{1,0:T(8,128)(2,1)S(1)}, bf16[256,768]{1,0:T(8,128)(2,1)S(1)}, u32[]{:S(2)}, u32[]{:S(2)}) collective-permute-start(bf16[256,768]{1,0:T(8,128)(2,1)S(1)} %collective-permute-done.12.late2), channel_id=1, source_target_pairs={{2,0},{4,2},{6,4},{8,6},{10,8},{12,10},{14,12},{3,1},{5,3},{7,5},{... | collective-permute-start | bytes 1179656 | tf_op jit(solution)/shard_map/ppermute | solution.py:29
  43.9 0.0 collective-permute-done.10.row_partner
  43.9 0.7 %collective-permute-start.15 = (bf16[256,768]{1,0:T(8,128)(2,1)S(1)}, bf16[256,768]{1,0:T(8,128)(2,1)S(1)}, u32[]{:S(2)}, u32[]{:S(2)}) collective-permute-start(bf16[256,768]{1,0:T(8,128)(2,1)S(1)} %collective-permute-done.13.late_pair), channel_id=1, source_target_pairs={{6,2},{10,6},{14,10},{7,3},{11,7},{15,11},{22,18},{26,22},{30,26},... | collective-permute-start | bytes 1179656 | tf_op jit(solution)/shard_map/ppermute | solution.py:35
  44.6 2.1 %shard_map.113 = (f32[128,768]{1,0:T(8,128)S(1)}, f32[128,768]{1,0:T(8,128)S(1)}) custom-call(bf16[272,768]{1,0:T(8,128)(2,1)S(1)} %get-tuple-element.21.own, f32[72,128]{1,0:T(8,128)S(1)} %get-tuple-element.27.row_own, f32[24,128]{1,0:T(8,128)S(1)} %collective-permute-done.10.row_partner, bf16[256,768]{1,0:T(8,128)(2,1)S(1)} %get-tuple-element.28.qo, ...), custom_call_target="tpu_custom_call" | custom-call | flops 1000000000 | tf_op jit(solution)/shard_map/pallas_call | solution.py:262
  46.7 0.0 collective-permute-done.7
  46.7 0.0 collective-permute-done.6
  46.7 0.2 collective-permute-done.5
  46.9 3.2 %collective-permute-start.8 = (f32[144,128]{1,0:T(8,128)S(1)}, f32[144,128]{1,0:T(8,128)S(1)}, u32[]{:S(2)}, u32[]{:S(2)}) collective-permute-start(f32[144,128]{1,0:T(8,128)S(1)} %pad_maximum_fusion), channel_id=1, source_target_pairs={{0,2},{2,0},{4,6},{6,4},{8,10},{10,8},{12,14},{14,12},{1,3},{3,1},... | collective-permute-start | bytes 221192 | tf_op jit(solution)/shard_map/ppermute | solution.py:289
  50.1 6.9 %collective-permute-done.8 = f32[144,128]{1,0:T(8,128)S(1)} collective-permute-done((f32[144,128]{1,0:T(8,128)S(1)}, f32[144,128]{1,0:T(8,128)S(1)}, u32[]{:S(2)}, u32[]{:S(2)}) %collective-permute-start.8) | collective-permute-done | bytes 73760 | tf_op jit(solution)/shard_map/ppermute | solution.py:289
  57.1 0.0 collective-permute-start.9
  57.1 0.0 collective-permute-done.14.late3
  57.1 0.0 collective-permute-done.15.late1
  57.1 2.1 %shard_map.114 = (bf16[128,768]{1,0:T(8,128)(2,1)}, bf16[128,768]{1,0:T(8,128)(2,1)}) custom-call(s32[1]{0:T(128)} %bitcast.1.frame, bf16[272,768]{1,0:T(8,128)(2,1)S(1)} %get-tuple-element.21.own, f32[8,24,128]{2,1,0:T(8,128)S(1)} %constant_dynamic-update-slice_fusion.stats, f32[128,768]{1,0:T(8,128)S(1)} %get-tuple-element.29.near_keys, ...), custom_call_target="tpu_custom_call" | custom-call | flops 99999997952 | tf_op jit(solution)/shard_map/pallas_call | solution.py:262
  59.2 0.0 collective-permute-done.9
  59.2 0.6 %add_bitcast_fusion = f32[8,768]{1,0:T(8,128)} fusion(f32[48,128]{1,0:T(8,128)S(1)} %slice_add_fusion, f32[48,128]{1,0:T(8,128)S(1)} %collective-permute-done.9), kind=kLoop, calls=%fused_computation.6 | loop fusion | flops 6144 | bytes 73728 | tf_op jit(solution)/shard_map/reshape | solution.py:354
  (14 shorter events, 0.1 us)
Async XLA Ops:
  2.6 13.8 %collective-permute-start.1 = (bf16[272,768]{1,0:T(8,128)(2,1)S(1)}, bf16[272,768]{1,0:T(8,128)(2,1)S(1)}, u32[]{:S(2)}, u32[]{:S(2)}) collective-permute-start(bf16[272,768]{1,0:T(8,128)(2,1)S(1)} %get-tuple-element.21.own), channel_id=1, source_target_pairs={{0,4},{2,6},{4,8},{6,10},{8,12},{10,14},{1,5},{3,7},{5,9},{7,11},{... | collective-permute-start | bytes 1253384 | tf_op jit(solution)/shard_map/ppermute | solution.py:29
  7.6 12.3 %collective-permute-start.2 = (bf16[272,768]{1,0:T(8,128)(2,1)S(1)}, bf16[272,768]{1,0:T(8,128)(2,1)S(1)}, u32[]{:S(2)}, u32[]{:S(2)}) collective-permute-start(bf16[272,768]{1,0:T(8,128)(2,1)S(1)} %get-tuple-element.21.own), channel_id=1, source_target_pairs={{0,2},{2,0},{4,6},{6,4},{8,10},{10,8},{12,14},{14,12},{1,3},{3,1},... | collective-permute-start | bytes 1253384 | tf_op jit(solution)/shard_map/ppermute | solution.py:40
  9.2 16.5 %collective-permute-start = (bf16[272,768]{1,0:T(8,128)(2,1)S(1)}, bf16[272,768]{1,0:T(8,128)(2,1)S(1)}, u32[]{:S(2)}, u32[]{:S(2)}) collective-permute-start(bf16[272,768]{1,0:T(8,128)(2,1)S(1)} %get-tuple-element.21.own), channel_id=1, source_target_pairs={{0,1},{1,0},{2,3},{3,2},{4,5},{5,4},{6,7},{7,6},{8,9},{9,8},{10,11... | collective-permute-start | bytes 1253384 | tf_op jit(solution)/shard_map/ppermute | solution.py:44
  16.5 12.6 %collective-permute-start.3 = (bf16[272,768]{1,0:T(8,128)(2,1)S(1)}, bf16[272,768]{1,0:T(8,128)(2,1)S(1)}, u32[]{:S(2)}, u32[]{:S(2)}) collective-permute-start(bf16[272,768]{1,0:T(8,128)(2,1)S(1)} %collective-permute-done.1.near2), channel_id=1, source_target_pairs={{0,2},{2,4},{4,6},{6,8},{8,10},{10,12},{12,14},{1,3},{3,5},{5,7},{... | collective-permute-start | bytes 1253384 | tf_op jit(solution)/shard_map/ppermute | solution.py:29
  19.9 12.1 %collective-permute-start.4 = (bf16[272,768]{1,0:T(8,128)(2,1)S(1)}, bf16[272,768]{1,0:T(8,128)(2,1)S(1)}, u32[]{:S(2)}, u32[]{:S(2)}) collective-permute-start(bf16[272,768]{1,0:T(8,128)(2,1)S(1)} %collective-permute-done.2.pair), channel_id=1, source_target_pairs={{0,4},{4,8},{8,12},{1,5},{5,9},{9,13},{16,20},{20,24},{24,28},{17,... | collective-permute-start | bytes 1253384 | tf_op jit(solution)/shard_map/ppermute | solution.py:35
  24.3 18.3 %collective-permute-start.11 = (bf16[256,768]{1,0:T(8,128)(2,1)S(1)}, bf16[256,768]{1,0:T(8,128)(2,1)}, u32[]{:S(2)}, u32[]{:S(2)}) collective-permute-start(bf16[256,768]{1,0:T(8,128)(2,1)S(1)} %get-tuple-element.28.qo), channel_id=1, source_target_pairs={{0,1},{1,0},{2,3},{3,2},{4,5},{5,4},{6,7},{7,6},{8,9},{9,8},{10,11... | collective-permute-start | bytes 1179656 | tf_op jit(solution)/shard_map/ppermute | solution.py:44
  24.4 17.6 %collective-permute-start.12 = (bf16[256,768]{1,0:T(8,128)(2,1)S(1)}, bf16[256,768]{1,0:T(8,128)(2,1)S(1)}, u32[]{:S(2)}, u32[]{:S(2)}) collective-permute-start(bf16[256,768]{1,0:T(8,128)(2,1)S(1)} %get-tuple-element.28.qo), channel_id=1, source_target_pairs={{4,0},{6,2},{8,4},{10,6},{12,8},{14,10},{5,1},{7,3},{9,5},{11,7},{... | collective-permute-start | bytes 1179656 | tf_op jit(solution)/shard_map/ppermute | solution.py:29
  25.7 16.3 %collective-permute-start.13 = (bf16[256,768]{1,0:T(8,128)(2,1)S(1)}, bf16[256,768]{1,0:T(8,128)(2,1)S(1)}, u32[]{:S(2)}, u32[]{:S(2)}) collective-permute-start(bf16[256,768]{1,0:T(8,128)(2,1)S(1)} %get-tuple-element.28.qo), channel_id=1, source_target_pairs={{0,2},{2,0},{4,6},{6,4},{8,10},{10,8},{12,14},{14,12},{1,3},{3,1},... | collective-permute-start | bytes 1179656 | tf_op jit(solution)/shard_map/ppermute | solution.py:40
  36.3 10.4 %collective-permute-start.7 = (f32[72,128]{1,0:T(8,128)S(1)}, f32[72,128]{1,0:T(8,128)S(1)}, u32[]{:S(2)}, u32[]{:S(2)}) collective-permute-start(f32[72,128]{1,0:T(8,128)S(1)} %get-tuple-element.27.row_own), channel_id=1, source_target_pairs={{0,12},{2,14},{4,8},{6,10},{8,4},{10,6},{12,0},{14,2},{1,13},{3,15... | collective-permute-start | bytes 110600 | tf_op jit(solution)/shard_map/ppermute | solution.py:289
  40.8 3.1 %collective-permute-start.10 = (f32[24,128]{1,0:T(8,128)S(1)}, f32[24,128]{1,0:T(8,128)S(1)}, u32[]{:S(2)}, u32[]{:S(2)}) collective-permute-start(f32[24,128]{1,0:T(8,128)S(1)} %get-tuple-element.37), channel_id=1, source_target_pairs={{0,1},{1,0},{2,3},{3,2},{4,5},{5,4},{6,7},{7,6},{8,9},{9,8},{10,11... | collective-permute-start | bytes 36872 | tf_op jit(solution)/shard_map/ppermute | solution.py:44
  42.0 4.8 %collective-permute-start.6 = (f32[72,128]{1,0:T(8,128)S(1)}, f32[72,128]{1,0:T(8,128)S(1)}, u32[]{:S(2)}, u32[]{:S(2)}) collective-permute-start(f32[72,128]{1,0:T(8,128)S(1)} %get-tuple-element.27.row_own), channel_id=1, source_target_pairs={{0,4},{2,6},{4,0},{6,2},{8,12},{10,14},{12,8},{14,10},{1,5},{3,7},... | collective-permute-start | bytes 110600 | tf_op jit(solution)/shard_map/ppermute | solution.py:289
  42.0 4.9 %collective-permute-start.5 = (f32[72,128]{1,0:T(8,128)S(1)}, f32[72,128]{1,0:T(8,128)S(1)}, u32[]{:S(2)}, u32[]{:S(2)}) collective-permute-start(f32[72,128]{1,0:T(8,128)S(1)} %get-tuple-element.27.row_own), channel_id=1, source_target_pairs={{0,8},{2,10},{4,12},{6,14},{8,0},{10,2},{12,4},{14,6},{1,9},{3,11}... | collective-permute-start | bytes 110600 | tf_op jit(solution)/shard_map/ppermute | solution.py:289
  42.6 14.5 %collective-permute-start.14 = (bf16[256,768]{1,0:T(8,128)(2,1)S(1)}, bf16[256,768]{1,0:T(8,128)(2,1)S(1)}, u32[]{:S(2)}, u32[]{:S(2)}) collective-permute-start(bf16[256,768]{1,0:T(8,128)(2,1)S(1)} %collective-permute-done.12.late2), channel_id=1, source_target_pairs={{2,0},{4,2},{6,4},{8,6},{10,8},{12,10},{14,12},{3,1},{5,3},{7,5},{... | collective-permute-start | bytes 1179656 | tf_op jit(solution)/shard_map/ppermute | solution.py:29
  43.9 13.2 %collective-permute-start.15 = (bf16[256,768]{1,0:T(8,128)(2,1)S(1)}, bf16[256,768]{1,0:T(8,128)(2,1)S(1)}, u32[]{:S(2)}, u32[]{:S(2)}) collective-permute-start(bf16[256,768]{1,0:T(8,128)(2,1)S(1)} %collective-permute-done.13.late_pair), channel_id=1, source_target_pairs={{6,2},{10,6},{14,10},{7,3},{11,7},{15,11},{22,18},{26,22},{30,26},... | collective-permute-start | bytes 1179656 | tf_op jit(solution)/shard_map/ppermute | solution.py:35
  46.9 10.1 %collective-permute-start.8 = (f32[144,128]{1,0:T(8,128)S(1)}, f32[144,128]{1,0:T(8,128)S(1)}, u32[]{:S(2)}, u32[]{:S(2)}) collective-permute-start(f32[144,128]{1,0:T(8,128)S(1)} %pad_maximum_fusion), channel_id=1, source_target_pairs={{0,2},{2,0},{4,6},{6,4},{8,10},{10,8},{12,14},{14,12},{1,3},{3,1},... | collective-permute-start | bytes 221192 | tf_op jit(solution)/shard_map/ppermute | solution.py:289
  57.1 2.1 %collective-permute-start.9 = (f32[48,128]{1,0:T(8,128)S(1)}, f32[48,128]{1,0:T(8,128)S(1)}, u32[]{:S(2)}, u32[]{:S(2)}) collective-permute-start(f32[48,128]{1,0:T(8,128)S(1)} %slice_add_fusion), channel_id=1, source_target_pairs={{0,1},{1,0},{2,3},{3,2},{4,5},{5,4},{6,7},{7,6},{8,9},{9,8},{10,11... | collective-permute-start | bytes 73736 | tf_op jit(solution)/shard_map/ppermute | solution.py:44

commit v4 on v3

--- a/solution.py
+++ b/solution.py
@@ -13,15 +13,16 @@
 SCALE = 1.0 / math.sqrt(HEAD_DIM)
 STAT_ROWS = 24
 HOLD = True
-PREP, FWD, NEAR, FAR, QUERY = 10**11, 10**10, 10**9, 10**11, 10**9
+PREP, FWD, NEAR, FAR, QUERY = 10**11, 10**10, 10**9, 10**9, 10**9
 GROUP_ROWS = 16
 ACTIONS = 8
 EXP2_SCALE = SCALE * math.log2(math.e)
-ACTION_ROWS = 16
+ACTION_ROWS = 8
 MASKED = 1e30
 F32 = jnp.float32
 BF16 = jnp.bfloat16
 VMEM_LIMIT = 56 * 1024 * 1024
+SMALL_LIMIT = 12 * 1024 * 1024
 
 
 def shift(block, distance):
@@ -100,9 +101,9 @@
     qo[rows:, :] = d_out[...]
 
 
-def forward_kernel(frame, listed, own_action, queries, d_out, own, partner, near2, pair, near3, near1,
+def forward_kernel(frame, listed, own_action, qo, own, partner, near2, pair, near3, near1,
                    row_message, attended, d_low, picked):
-    rows = queries.shape[0]
+    rows = qo.shape[0] // 2
     frame_id = frame[0]
     odd = frame_id % 2
     present = []
@@ -123,8 +124,8 @@
     out_parts, sums = [], [[], [], []]
     for pair in range(HEADS // 2):
         span, starts = pair_span(pair)
-        query = split_pair(queries[:, span], starts)
-        grad = split_pair(d_out[:, span], starts)
+        query = split_pair(qo[0:rows, span], starts)
+        grad = split_pair(qo[rows:, span], starts)
         key = jnp.concatenate([block[0:rows, span] for block in blocks], axis=0)
         value = jnp.concatenate([block[rows : 2 * rows, span] for block in blocks], axis=0)
         scores = dot_t(query, key)
@@ -172,7 +173,7 @@
         row_message[STAT_ROWS + index * ACTIONS : STAT_ROWS + (index + 1) * ACTIONS, :] = totals
 
 
-def query_kernel(own, partner, picked, d_low, held, attended, grad_queries):
+def query_kernel(own, partner, picked, d_low, held, arrived, attended, grad_queries):
     rows = held.shape[0]
     parts = []
     for pair in range(HEADS // 2):
@@ -265,7 +266,7 @@
         in_specs=[pl.BlockSpec(memory_space=SMEM)] * len(scalars) + [pl.BlockSpec(memory_space=VMEM)] * len(arrays),
         out_specs=(pl.BlockSpec(memory_space=VMEM),) * len(outs),
         scratch_shapes=list(scratch),
-        compiler_params=pltpu.CompilerParams(vmem_limit_bytes=VMEM_LIMIT),
+        compiler_params=pltpu.CompilerParams(vmem_limit_bytes=VMEM_LIMIT if flops in (PREP, FWD) else SMALL_LIMIT),
         cost_estimate=pl.CostEstimate(flops=flops, transcendentals=0, bytes_accessed=0),
     )(*scalars, *[pltpu.with_memory_space_constraint(array, VMEM) if hold else array for array, hold in arrays])
 
@@ -278,7 +279,7 @@
         around = lax.all_gather(stats, "tm")
         count = 1 << (frames - 1).bit_length()
         order = reverse_bits(lax.iota(jnp.int32, count), count) ^ lax.axis_index("tm").astype(jnp.int32)
-        return lax.psum(table, "tm"), jnp.take(around, jnp.minimum(order, frames - 1), axis=0)
+        return lax.psum(table, "tm"), jnp.take(around, jnp.minimum(order, frames - 1), axis=0), message
     count = 1
     while count < frames:
         if count > 1:
@@ -289,8 +290,10 @@
         arrived = [lax.ppermute(message, "tm", [(i, i ^ step) for i in range(frames)]) for step in steps]
         table = table + sum(other[count * STAT_ROWS :] for other in arrived)
         gathered = jnp.concatenate([gathered] + [other[: count * STAT_ROWS].reshape(gathered.shape) for other in arrived])
+        if count == 1:
+            first = arrived[0]
         count *= len(steps) + 1
-    return table, gathered
+    return table, gathered, first
 
 
 def on_device(queries, keys, values, d_out, action_table, actions, temporal_list):
@@ -320,21 +323,21 @@
             ((2, 2 * rows + ACTION_ROWS, width), BF16, HOLD),
         ],
         [frame, temporal_list, actions],
-        [(queries, False), (d_out, False)] + [(block, HOLD) for block in (kv, partner, near2, pair, near3, near1)],
-    )
+        [(block, HOLD) for block in (qo, kv, partner, near2, pair, near3, near1)],
+    )
+    late2, late_pair, _ = lax.optimization_barrier((late2, late_pair, held))
+    late3 = shift(late2, -1)
+    late1 = shift_some(late_pair, -2, 1)
+    row_partner = swap_row(row_message[:STAT_ROWS])
+    table, stats, first = share(row_message)
+    table_partner = swap_row(table)
     attended, grad_queries = call(
         query_kernel,
         QUERY,
         [(wide, BF16, False), (wide, BF16, False)],
         [],
-        [(block, HOLD) for block in (kv, partner, picked, d_low, held)],
-    )
-    late2, late_pair, _ = lax.optimization_barrier((late2, late_pair, held))
-    late3 = shift(late2, -1)
-    late1 = shift_some(late_pair, -2, 1)
-    row_partner = swap_row(row_message[:STAT_ROWS])
-    table, stats = share(row_message)
-    table_partner = swap_row(table)
+        [(block, HOLD) for block in (kv, partner, picked, d_low, held, first)],
+    )
     near_keys, near_values = call(
         near_backward_kernel,
         NEAR,

time: 60.1 us -> 58.4 us (0.972)
  waiting for transfers between devices: 20.6 us -> 18.7 us
    ppermute x4, waiting for transfers between devices: 7.09 us -> 5.69 us  [share(): lax.ppermute(message, 'tm', [(i, i ^ step) for i in range(frames)])]
    ppermute x4, waiting for transfers between devices: 10.6 us -> 9.78 us  [shift(): lax.ppermute(block, 'tm', [(i - distance, i) for i in frames if i - dista...]
  transfers between devices with their start and end apart: 16 -> 16, of which waited for: 5 -> 4; matrix products, arithmetic and copies ran while one was open for 0% -> 0% of each run, Pallas kernels for 16% -> 16%
where the time goes in v4:
time: 58.4 us; the launch traced here: 58 us
  starting transfers between devices  26.6 us (46%)
  waiting for transfers between devices  18.7 us (32%)
  Pallas kernels  10.6 us (18%)
  between operations  1.49 us (3%)
  other arithmetic  0.64 us (1%)
    ppermute x4, starting transfers between devices, shift(): lax.ppermute(block, 'tm', [(i - distance, i) for i in frames if i - dista...  10.9 us
    pallas_call x5, Pallas kernels, call(): pl.pallas_call(kernel, out_shape=tuple((pltpu.VMEM(shape, dtype) if stays...  10.6 us
    ppermute x4, waiting for transfers between devices, shift(): lax.ppermute(block, 'tm', [(i - distance, i) for i in frames if i - dista...  9.78 us
    ppermute x4, starting transfers between devices, share(): lax.ppermute(message, 'tm', [(i, i ^ step) for i in range(frames)])  8.89 us
    ppermute x4, waiting for transfers between devices, share(): lax.ppermute(message, 'tm', [(i, i ^ step) for i in range(frames)])  5.69 us
    ppermute x2, starting transfers between devices, shift_some(): return lax.ppermute(block, 'tm', route)  5.08 us
    ppermute x2, waiting for transfers between devices, shift_some(): return lax.ppermute(block, 'tm', route)  3.22 us
    ppermute x2, starting transfers between devices, swap_pair(): lax.ppermute(block, 'tm', [(i, i ^ 1) for i in frames if i ^ 1 in frames])  1.63 us
  transfers between devices with their start and end apart: 16, of which 4 were waited for; matrix products, arithmetic and copies ran while one was open for 0% of the time, Pallas kernels for 16%

profile of v4, /device:TPU:0, one launch (start us, length us, event | category | flops | bytes accessed | tf_op | source)
XLA Modules:
  0.0 58.0 jit_solution(16864838440721775469)
XLA Ops:
  1.3 1.4 %shard_map.110 = (bf16[264,768]{1,0:T(8,128)(2,1)S(1)}, bf16[256,768]{1,0:T(8,128)(2,1)S(1)}) custom-call(s32[1,1]{1,0:T(1,128)} %bitcast.25.actions, bf16[128,768]{1,0:T(8,128)(2,1)} %keys.1, bf16[128,768]{1,0:T(8,128)(2,1)} %values.1, bf16[8,768]{1,0:T(8,128)(2,1)} %table.1, bf16[128,768]{1,0:T(8,128)(2,1)} %queries.1, bf16[128,768]{1,0:T(8,128)(2,1)} %d_out.1), custom_call_target="tpu_custom_call" | custom-call | flops 99999997952 | tf_op jit(solution)/shard_map/pallas_call | solution.py:263
  2.6 5.0 %collective-permute-start.1 = (bf16[264,768]{1,0:T(8,128)(2,1)S(1)}, bf16[264,768]{1,0:T(8,128)(2,1)S(1)}, u32[]{:S(2)}, u32[]{:S(2)}) collective-permute-start(bf16[264,768]{1,0:T(8,128)(2,1)S(1)} %get-tuple-element.21.own), channel_id=1, source_target_pairs={{0,4},{2,6},{4,8},{6,10},{8,12},{10,14},{1,5},{3,7},{5,9},{7,11},{... | collective-permute-start | bytes 1216520 | tf_op jit(solution)/shard_map/ppermute | solution.py:30
  7.6 1.6 %collective-permute-start.2 = (bf16[264,768]{1,0:T(8,128)(2,1)S(1)}, bf16[264,768]{1,0:T(8,128)(2,1)S(1)}, u32[]{:S(2)}, u32[]{:S(2)}) collective-permute-start(bf16[264,768]{1,0:T(8,128)(2,1)S(1)} %get-tuple-element.21.own), channel_id=1, source_target_pairs={{0,2},{2,0},{4,6},{6,4},{8,10},{10,8},{12,14},{14,12},{1,3},{3,1},... | collective-permute-start | bytes 1216520 | tf_op jit(solution)/shard_map/ppermute | solution.py:41
  9.2 0.0 collective-permute-start
  9.2 7.0 %collective-permute-done.1.near2 = bf16[264,768]{1,0:T(8,128)(2,1)S(1)} collective-permute-done((bf16[264,768]{1,0:T(8,128)(2,1)S(1)}, bf16[264,768]{1,0:T(8,128)(2,1)S(1)}, u32[]{:S(2)}, u32[]{:S(2)}) %collective-permute-start.1) | collective-permute-done | bytes 405536 | tf_op jit(solution)/shard_map/ppermute | solution.py:30
  16.2 3.4 %collective-permute-start.3 = (bf16[264,768]{1,0:T(8,128)(2,1)S(1)}, bf16[264,768]{1,0:T(8,128)(2,1)S(1)}, u32[]{:S(2)}, u32[]{:S(2)}) collective-permute-start(bf16[264,768]{1,0:T(8,128)(2,1)S(1)} %collective-permute-done.1.near2), channel_id=1, source_target_pairs={{0,2},{2,4},{4,6},{6,8},{8,10},{10,12},{12,14},{1,3},{3,5},{5,7},{... | collective-permute-start | bytes 1216520 | tf_op jit(solution)/shard_map/ppermute | solution.py:30
  19.6 0.0 collective-permute-done.2.pair
  19.6 4.4 %collective-permute-start.4 = (bf16[264,768]{1,0:T(8,128)(2,1)S(1)}, bf16[264,768]{1,0:T(8,128)(2,1)S(1)}, u32[]{:S(2)}, u32[]{:S(2)}) collective-permute-start(bf16[264,768]{1,0:T(8,128)(2,1)S(1)} %collective-permute-done.2.pair), channel_id=1, source_target_pairs={{0,4},{4,8},{8,12},{1,5},{5,9},{9,13},{16,20},{20,24},{24,28},{17,... | collective-permute-start | bytes 1216520 | tf_op jit(solution)/shard_map/ppermute | solution.py:36
  24.0 0.1 collective-permute-start.11
  24.1 1.3 %collective-permute-start.12 = (bf16[256,768]{1,0:T(8,128)(2,1)S(1)}, bf16[256,768]{1,0:T(8,128)(2,1)S(1)}, u32[]{:S(2)}, u32[]{:S(2)}) collective-permute-start(bf16[256,768]{1,0:T(8,128)(2,1)S(1)} %get-tuple-element.22.qo), channel_id=1, source_target_pairs={{4,0},{6,2},{8,4},{10,6},{12,8},{14,10},{5,1},{7,3},{9,5},{11,7},{... | collective-permute-start | bytes 1179656 | tf_op jit(solution)/shard_map/ppermute | solution.py:30
  25.4 0.0 collective-permute-done.partner
  25.4 0.1 collective-permute-start.13
  25.5 2.7 %collective-permute-done.3.near3 = bf16[264,768]{1,0:T(8,128)(2,1)S(1)} collective-permute-done((bf16[264,768]{1,0:T(8,128)(2,1)S(1)}, bf16[264,768]{1,0:T(8,128)(2,1)S(1)}, u32[]{:S(2)}, u32[]{:S(2)}) %collective-permute-start.3) | collective-permute-done | bytes 405536 | tf_op jit(solution)/shard_map/ppermute | solution.py:30
  28.2 3.2 %collective-permute-done.4.near1 = bf16[264,768]{1,0:T(8,128)(2,1)S(1)} collective-permute-done((bf16[264,768]{1,0:T(8,128)(2,1)S(1)}, bf16[264,768]{1,0:T(8,128)(2,1)S(1)}, u32[]{:S(2)}, u32[]{:S(2)}) %collective-permute-start.4) | collective-permute-done | bytes 405536 | tf_op jit(solution)/shard_map/ppermute | solution.py:36
  31.5 4.0 %shard_map.111 = (f32[72,128]{1,0:T(8,128)S(1)}, bf16[128,768]{1,0:T(8,128)(2,1)S(1)}, bf16[4,256,512]{2,1,0:T(8,128)(2,1)S(1)}, bf16[2,264,768]{2,1,0:T(8,128)(2,1)S(1)}) custom-call(s32[1]{0:T(128)} %bitcast.1.frame, s32[1,2]{1,0:T(1,128)} %listed.1, s32[1]{0:T(128)} %copy.16.own_action, bf16[256,768]{1,0:T(8,128)(2,1)S(1)} %get-tuple-element.22.qo, ...), custom_call_target="tpu_custom_call" | custom-call | flops 10000000000 | tf_op jit(solution)/shard_map/pallas_call | solution.py:263
  35.4 3.5 %collective-permute-start.5 = (f32[72,128]{1,0:T(8,128)S(1)}, f32[72,128]{1,0:T(8,128)S(1)}, u32[]{:S(2)}, u32[]{:S(2)}) collective-permute-start(f32[72,128]{1,0:T(8,128)S(1)} %get-tuple-element.26.row_own), channel_id=1, source_target_pairs={{0,8},{2,10},{4,12},{6,14},{8,0},{10,2},{12,4},{14,6},{1,9},{3,11}... | collective-permute-start | bytes 110600 | tf_op jit(solution)/shard_map/ppermute | solution.py:290
  38.9 0.0 collective-permute-start.10
  38.9 0.0 collective-permute-done.12.late2
  38.9 1.4 %collective-permute-start.7 = (f32[72,128]{1,0:T(8,128)S(1)}, f32[72,128]{1,0:T(8,128)S(1)}, u32[]{:S(2)}, u32[]{:S(2)}) collective-permute-start(f32[72,128]{1,0:T(8,128)S(1)} %get-tuple-element.26.row_own), channel_id=1, source_target_pairs={{0,12},{2,14},{4,8},{6,10},{8,4},{10,6},{12,0},{14,2},{1,13},{3,15... | collective-permute-start | bytes 110600 | tf_op jit(solution)/shard_map/ppermute | solution.py:290
  40.4 0.0 collective-permute-done.13.late_pair
  40.4 0.7 %collective-permute-start.6 = (f32[72,128]{1,0:T(8,128)S(1)}, f32[72,128]{1,0:T(8,128)S(1)}, u32[]{:S(2)}, u32[]{:S(2)}) collective-permute-start(f32[72,128]{1,0:T(8,128)S(1)} %get-tuple-element.26.row_own), channel_id=1, source_target_pairs={{0,4},{2,6},{4,0},{6,2},{8,12},{10,14},{12,8},{14,10},{1,5},{3,7},... | collective-permute-start | bytes 110600 | tf_op jit(solution)/shard_map/ppermute | solution.py:290
  41.0 0.0 collective-permute-done.11.qo_partner
  41.0 1.3 %collective-permute-start.14 = (bf16[256,768]{1,0:T(8,128)(2,1)S(1)}, bf16[256,768]{1,0:T(8,128)(2,1)S(1)}, u32[]{:S(2)}, u32[]{:S(2)}) collective-permute-start(bf16[256,768]{1,0:T(8,128)(2,1)S(1)} %collective-permute-done.12.late2), channel_id=1, source_target_pairs={{2,0},{4,2},{6,4},{8,6},{10,8},{12,10},{14,12},{3,1},{5,3},{7,5},{... | collective-permute-start | bytes 1179656 | tf_op jit(solution)/shard_map/ppermute | solution.py:30
  42.3 0.0 collective-permute-done.10.row_partner
  42.3 0.7 %collective-permute-start.15 = (bf16[256,768]{1,0:T(8,128)(2,1)S(1)}, bf16[256,768]{1,0:T(8,128)(2,1)S(1)}, u32[]{:S(2)}, u32[]{:S(2)}) collective-permute-start(bf16[256,768]{1,0:T(8,128)(2,1)S(1)} %collective-permute-done.13.late_pair), channel_id=1, source_target_pairs={{6,2},{10,6},{14,10},{7,3},{11,7},{15,11},{22,18},{26,22},{30,26},... | collective-permute-start | bytes 1179656 | tf_op jit(solution)/shard_map/ppermute | solution.py:36
  43.0 2.1 %shard_map.113 = (f32[128,768]{1,0:T(8,128)S(1)}, f32[128,768]{1,0:T(8,128)S(1)}) custom-call(bf16[264,768]{1,0:T(8,128)(2,1)S(1)} %get-tuple-element.21.own, f32[72,128]{1,0:T(8,128)S(1)} %get-tuple-element.26.row_own, f32[24,128]{1,0:T(8,128)S(1)} %collective-permute-done.10.row_partner, bf16[256,768]{1,0:T(8,128)(2,1)S(1)} %get-tuple-element.22.qo, ...), custom_call_target="tpu_custom_call" | custom-call | flops 1000000000 | tf_op jit(solution)/shard_map/pallas_call | solution.py:263
  45.1 0.0 collective-permute-done.7
  45.1 0.0 collective-permute-done.6
  45.1 0.0 collective-permute-done.5.arrived
  45.2 3.3 %collective-permute-start.8 = (f32[144,128]{1,0:T(8,128)S(1)}, f32[144,128]{1,0:T(8,128)S(1)}, u32[]{:S(2)}, u32[]{:S(2)}) collective-permute-start(f32[144,128]{1,0:T(8,128)S(1)} %pad_maximum_fusion), channel_id=1, source_target_pairs={{0,2},{2,0},{4,6},{6,4},{8,10},{10,8},{12,14},{14,12},{1,3},{3,1},... | collective-permute-start | bytes 221192 | tf_op jit(solution)/shard_map/ppermute | solution.py:290
  48.5 1.1 %shard_map.112 = (bf16[128,768]{1,0:T(8,128)(2,1)}, bf16[128,768]{1,0:T(8,128)(2,1)}) custom-call(bf16[264,768]{1,0:T(8,128)(2,1)S(1)} %get-tuple-element.21.own, bf16[264,768]{1,0:T(8,128)(2,1)S(1)} %collective-permute-done.partner, bf16[2,264,768]{2,1,0:T(8,128)(2,1)S(1)} %get-tuple-element.23.picked, bf16[4,256,512]{2,1,0:T(8,128)(2,1)S(1)} %get-tuple-element.24.d_low, ...), custom_call_target="tpu_custom_call" | custom-call | flops 1000000000 | tf_op jit(solution)/shard_map/pallas_call | solution.py:263
  49.6 5.7 %collective-permute-done.8 = f32[144,128]{1,0:T(8,128)S(1)} collective-permute-done((f32[144,128]{1,0:T(8,128)S(1)}, f32[144,128]{1,0:T(8,128)S(1)}, u32[]{:S(2)}, u32[]{:S(2)}) %collective-permute-start.8) | collective-permute-done | bytes 73760 | tf_op jit(solution)/shard_map/ppermute | solution.py:290
  55.3 0.0 collective-permute-start.9
  55.3 0.0 collective-permute-done.14.late3
  55.4 0.0 collective-permute-done.15.late1
  55.4 2.1 %shard_map.114 = (bf16[128,768]{1,0:T(8,128)(2,1)}, bf16[128,768]{1,0:T(8,128)(2,1)}) custom-call(s32[1]{0:T(128)} %bitcast.1.frame, bf16[264,768]{1,0:T(8,128)(2,1)S(1)} %get-tuple-element.21.own, f32[8,24,128]{2,1,0:T(8,128)S(1)} %constant_dynamic-update-slice_fusion.stats, f32[128,768]{1,0:T(8,128)S(1)} %get-tuple-element.29.near_keys, ...), custom_call_target="tpu_custom_call" | custom-call | flops 1000000000 | tf_op jit(solution)/shard_map/pallas_call | solution.py:263
  57.4 0.0 collective-permute-done.9
  57.4 0.6 %add_bitcast_fusion = f32[8,768]{1,0:T(8,128)} fusion(f32[48,128]{1,0:T(8,128)S(1)} %slice_add_fusion, f32[48,128]{1,0:T(8,128)S(1)} %collective-permute-done.9), kind=kLoop, calls=%fused_computation.6 | loop fusion | flops 6144 | bytes 73728 | tf_op jit(solution)/shard_map/reshape | solution.py:357
  (14 shorter events, 0.1 us)
Async XLA Ops:
  2.6 13.6 %collective-permute-start.1 = (bf16[264,768]{1,0:T(8,128)(2,1)S(1)}, bf16[264,768]{1,0:T(8,128)(2,1)S(1)}, u32[]{:S(2)}, u32[]{:S(2)}) collective-permute-start(bf16[264,768]{1,0:T(8,128)(2,1)S(1)} %get-tuple-element.21.own), channel_id=1, source_target_pairs={{0,4},{2,6},{4,8},{6,10},{8,12},{10,14},{1,5},{3,7},{5,9},{7,11},{... | collective-permute-start | bytes 1216520 | tf_op jit(solution)/shard_map/ppermute | solution.py:30
  7.6 12.0 %collective-permute-start.2 = (bf16[264,768]{1,0:T(8,128)(2,1)S(1)}, bf16[264,768]{1,0:T(8,128)(2,1)S(1)}, u32[]{:S(2)}, u32[]{:S(2)}) collective-permute-start(bf16[264,768]{1,0:T(8,128)(2,1)S(1)} %get-tuple-element.21.own), channel_id=1, source_target_pairs={{0,2},{2,0},{4,6},{6,4},{8,10},{10,8},{12,14},{14,12},{1,3},{3,1},... | collective-permute-start | bytes 1216520 | tf_op jit(solution)/shard_map/ppermute | solution.py:41
  9.2 16.2 %collective-permute-start = (bf16[264,768]{1,0:T(8,128)(2,1)S(1)}, bf16[264,768]{1,0:T(8,128)(2,1)S(1)}, u32[]{:S(2)}, u32[]{:S(2)}) collective-permute-start(bf16[264,768]{1,0:T(8,128)(2,1)S(1)} %get-tuple-element.21.own), channel_id=1, source_target_pairs={{0,1},{1,0},{2,3},{3,2},{4,5},{5,4},{6,7},{7,6},{8,9},{9,8},{10,11... | collective-permute-start | bytes 1216520 | tf_op jit(solution)/shard_map/ppermute | solution.py:45
  16.2 12.0 %collective-permute-start.3 = (bf16[264,768]{1,0:T(8,128)(2,1)S(1)}, bf16[264,768]{1,0:T(8,128)(2,1)S(1)}, u32[]{:S(2)}, u32[]{:S(2)}) collective-permute-start(bf16[264,768]{1,0:T(8,128)(2,1)S(1)} %collective-permute-done.1.near2), channel_id=1, source_target_pairs={{0,2},{2,4},{4,6},{6,8},{8,10},{10,12},{12,14},{1,3},{3,5},{5,7},{... | collective-permute-start | bytes 1216520 | tf_op jit(solution)/shard_map/ppermute | solution.py:30
  19.6 11.8 %collective-permute-start.4 = (bf16[264,768]{1,0:T(8,128)(2,1)S(1)}, bf16[264,768]{1,0:T(8,128)(2,1)S(1)}, u32[]{:S(2)}, u32[]{:S(2)}) collective-permute-start(bf16[264,768]{1,0:T(8,128)(2,1)S(1)} %collective-permute-done.2.pair), channel_id=1, source_target_pairs={{0,4},{4,8},{8,12},{1,5},{5,9},{9,13},{16,20},{20,24},{24,28},{17,... | collective-permute-start | bytes 1216520 | tf_op jit(solution)/shard_map/ppermute | solution.py:36
  24.0 17.0 %collective-permute-start.11 = (bf16[256,768]{1,0:T(8,128)(2,1)S(1)}, bf16[256,768]{1,0:T(8,128)(2,1)}, u32[]{:S(2)}, u32[]{:S(2)}) collective-permute-start(bf16[256,768]{1,0:T(8,128)(2,1)S(1)} %get-tuple-element.22.qo), channel_id=1, source_target_pairs={{0,1},{1,0},{2,3},{3,2},{4,5},{5,4},{6,7},{7,6},{8,9},{9,8},{10,11... | collective-permute-start | bytes 1179656 | tf_op jit(solution)/shard_map/ppermute | solution.py:45
  24.1 14.8 %collective-permute-start.12 = (bf16[256,768]{1,0:T(8,128)(2,1)S(1)}, bf16[256,768]{1,0:T(8,128)(2,1)S(1)}, u32[]{:S(2)}, u32[]{:S(2)}) collective-permute-start(bf16[256,768]{1,0:T(8,128)(2,1)S(1)} %get-tuple-element.22.qo), channel_id=1, source_target_pairs={{4,0},{6,2},{8,4},{10,6},{12,8},{14,10},{5,1},{7,3},{9,5},{11,7},{... | collective-permute-start | bytes 1179656 | tf_op jit(solution)/shard_map/ppermute | solution.py:30
  25.4 14.9 %collective-permute-start.13 = (bf16[256,768]{1,0:T(8,128)(2,1)S(1)}, bf16[256,768]{1,0:T(8,128)(2,1)S(1)}, u32[]{:S(2)}, u32[]{:S(2)}) collective-permute-start(bf16[256,768]{1,0:T(8,128)(2,1)S(1)} %get-tuple-element.22.qo), channel_id=1, source_target_pairs={{0,2},{2,0},{4,6},{6,4},{8,10},{10,8},{12,14},{14,12},{1,3},{3,1},... | collective-permute-start | bytes 1179656 | tf_op jit(solution)/shard_map/ppermute | solution.py:41
  35.4 9.7 %collective-permute-start.5 = (f32[72,128]{1,0:T(8,128)S(1)}, f32[72,128]{1,0:T(8,128)S(1)}, u32[]{:S(2)}, u32[]{:S(2)}) collective-permute-start(f32[72,128]{1,0:T(8,128)S(1)} %get-tuple-element.26.row_own), channel_id=1, source_target_pairs={{0,8},{2,10},{4,12},{6,14},{8,0},{10,2},{12,4},{14,6},{1,9},{3,11}... | collective-permute-start | bytes 110600 | tf_op jit(solution)/shard_map/ppermute | solution.py:290
  38.9 3.4 %collective-permute-start.10 = (f32[24,128]{1,0:T(8,128)S(1)}, f32[24,128]{1,0:T(8,128)S(1)}, u32[]{:S(2)}, u32[]{:S(2)}) collective-permute-start(f32[24,128]{1,0:T(8,128)S(1)} %get-tuple-element.37), channel_id=1, source_target_pairs={{0,1},{1,0},{2,3},{3,2},{4,5},{5,4},{6,7},{7,6},{8,9},{9,8},{10,11... | collective-permute-start | bytes 36872 | tf_op jit(solution)/shard_map/ppermute | solution.py:45
  38.9 6.2 %collective-permute-start.7 = (f32[72,128]{1,0:T(8,128)S(1)}, f32[72,128]{1,0:T(8,128)S(1)}, u32[]{:S(2)}, u32[]{:S(2)}) collective-permute-start(f32[72,128]{1,0:T(8,128)S(1)} %get-tuple-element.26.row_own), channel_id=1, source_target_pairs={{0,12},{2,14},{4,8},{6,10},{8,4},{10,6},{12,0},{14,2},{1,13},{3,15... | collective-permute-start | bytes 110600 | tf_op jit(solution)/shard_map/ppermute | solution.py:290
  40.4 4.8 %collective-permute-start.6 = (f32[72,128]{1,0:T(8,128)S(1)}, f32[72,128]{1,0:T(8,128)S(1)}, u32[]{:S(2)}, u32[]{:S(2)}) collective-permute-start(f32[72,128]{1,0:T(8,128)S(1)} %get-tuple-element.26.row_own), channel_id=1, source_target_pairs={{0,4},{2,6},{4,0},{6,2},{8,12},{10,14},{12,8},{14,10},{1,5},{3,7},... | collective-permute-start | bytes 110600 | tf_op jit(solution)/shard_map/ppermute | solution.py:290
  41.0 14.3 %collective-permute-start.14 = (bf16[256,768]{1,0:T(8,128)(2,1)S(1)}, bf16[256,768]{1,0:T(8,128)(2,1)S(1)}, u32[]{:S(2)}, u32[]{:S(2)}) collective-permute-start(bf16[256,768]{1,0:T(8,128)(2,1)S(1)} %collective-permute-done.12.late2), channel_id=1, source_target_pairs={{2,0},{4,2},{6,4},{8,6},{10,8},{12,10},{14,12},{3,1},{5,3},{7,5},{... | collective-permute-start | bytes 1179656 | tf_op jit(solution)/shard_map/ppermute | solution.py:30
  42.3 13.0 %collective-permute-start.15 = (bf16[256,768]{1,0:T(8,128)(2,1)S(1)}, bf16[256,768]{1,0:T(8,128)(2,1)S(1)}, u32[]{:S(2)}, u32[]{:S(2)}) collective-permute-start(bf16[256,768]{1,0:T(8,128)(2,1)S(1)} %collective-permute-done.13.late_pair), channel_id=1, source_target_pairs={{6,2},{10,6},{14,10},{7,3},{11,7},{15,11},{22,18},{26,22},{30,26},... | collective-permute-start | bytes 1179656 | tf_op jit(solution)/shard_map/ppermute | solution.py:36
  45.2 10.1 %collective-permute-start.8 = (f32[144,128]{1,0:T(8,128)S(1)}, f32[144,128]{1,0:T(8,128)S(1)}, u32[]{:S(2)}, u32[]{:S(2)}) collective-permute-start(f32[144,128]{1,0:T(8,128)S(1)} %pad_maximum_fusion), channel_id=1, source_target_pairs={{0,2},{2,0},{4,6},{6,4},{8,10},{10,8},{12,14},{14,12},{1,3},{3,1},... | collective-permute-start | bytes 221192 | tf_op jit(solution)/shard_map/ppermute | solution.py:290
  55.3 2.1 %collective-permute-start.9 = (f32[48,128]{1,0:T(8,128)S(1)}, f32[48,128]{1,0:T(8,128)S(1)}, u32[]{:S(2)}, u32[]{:S(2)}) collective-permute-start(f32[48,128]{1,0:T(8,128)S(1)} %slice_add_fusion), channel_id=1, source_target_pairs={{0,1},{1,0},{2,3},{3,2},{4,5},{5,4},{6,7},{7,6},{8,9},{9,8},{10,11... | collective-permute-start | bytes 73736 | tf_op jit(solution)/shard_map/ppermute | solution.py:45

commit v5 on v4

--- a/solution.py
+++ b/solution.py
@@ -266,7 +266,7 @@
         in_specs=[pl.BlockSpec(memory_space=SMEM)] * len(scalars) + [pl.BlockSpec(memory_space=VMEM)] * len(arrays),
         out_specs=(pl.BlockSpec(memory_space=VMEM),) * len(outs),
         scratch_shapes=list(scratch),
-        compiler_params=pltpu.CompilerParams(vmem_limit_bytes=VMEM_LIMIT if flops in (PREP, FWD) else SMALL_LIMIT),
+        compiler_params=pltpu.CompilerParams(vmem_limit_bytes=VMEM_LIMIT if flops == PREP else SMALL_LIMIT),
         cost_estimate=pl.CostEstimate(flops=flops, transcendentals=0, bytes_accessed=0),
     )(*scalars, *[pltpu.with_memory_space_constraint(array, VMEM) if hold else array for array, hold in arrays])
 

time: 58.4 us -> 58.3 us (level)
  no operation moved by 1% of the time
where the time goes in v5:
time: 58.3 us; the launch traced here: 57.9 us
  starting transfers between devices  26.7 us (46%)
  waiting for transfers between devices  18.6 us (32%)
  Pallas kernels  10.5 us (18%)
  between operations  1.52 us (3%)
  other arithmetic  0.64 us (1%)
    ppermute x4, starting transfers between devices, shift(): lax.ppermute(block, 'tm', [(i - distance, i) for i in frames if i - dista...  10.9 us
    pallas_call x5, Pallas kernels, call(): pl.pallas_call(kernel, out_shape=tuple((pltpu.VMEM(shape, dtype) if stays...  10.5 us
    ppermute x4, waiting for transfers between devices, shift(): lax.ppermute(block, 'tm', [(i - distance, i) for i in frames if i - dista...  9.76 us
    ppermute x4, starting transfers between devices, share(): lax.ppermute(message, 'tm', [(i, i ^ step) for i in range(frames)])  9.01 us
    ppermute x4, waiting for transfers between devices, share(): lax.ppermute(message, 'tm', [(i, i ^ step) for i in range(frames)])  5.54 us
    ppermute x2, starting transfers between devices, shift_some(): return lax.ppermute(block, 'tm', route)  5.08 us
    ppermute x2, waiting for transfers between devices, shift_some(): return lax.ppermute(block, 'tm', route)  3.24 us
    ppermute x2, starting transfers between devices, swap_pair(): lax.ppermute(block, 'tm', [(i, i ^ 1) for i in frames if i ^ 1 in frames])  1.63 us
  transfers between devices with their start and end apart: 16, of which 4 were waited for; matrix products, arithmetic and copies ran while one was open for 0% of the time, Pallas kernels for 16%

profile of v5, /device:TPU:0, one launch (start us, length us, event | category | flops | bytes accessed | tf_op | source)
XLA Modules:
  0.0 57.9 jit_solution(851669264448197694)
XLA Ops:
  1.3 1.4 %shard_map.110 = (bf16[264,768]{1,0:T(8,128)(2,1)S(1)}, bf16[256,768]{1,0:T(8,128)(2,1)S(1)}) custom-call(s32[1,1]{1,0:T(1,128)} %bitcast.25.actions, bf16[128,768]{1,0:T(8,128)(2,1)} %keys.1, bf16[128,768]{1,0:T(8,128)(2,1)} %values.1, bf16[8,768]{1,0:T(8,128)(2,1)} %table.1, bf16[128,768]{1,0:T(8,128)(2,1)} %queries.1, bf16[128,768]{1,0:T(8,128)(2,1)} %d_out.1), custom_call_target="tpu_custom_call" | custom-call | flops 99999997952 | tf_op jit(solution)/shard_map/pallas_call | solution.py:263
  2.6 5.0 %collective-permute-start.1 = (bf16[264,768]{1,0:T(8,128)(2,1)S(1)}, bf16[264,768]{1,0:T(8,128)(2,1)S(1)}, u32[]{:S(2)}, u32[]{:S(2)}) collective-permute-start(bf16[264,768]{1,0:T(8,128)(2,1)S(1)} %get-tuple-element.21.own), channel_id=1, source_target_pairs={{0,4},{2,6},{4,8},{6,10},{8,12},{10,14},{1,5},{3,7},{5,9},{7,11},{... | collective-permute-start | bytes 1216520 | tf_op jit(solution)/shard_map/ppermute | solution.py:30
  7.6 1.6 %collective-permute-start.2 = (bf16[264,768]{1,0:T(8,128)(2,1)S(1)}, bf16[264,768]{1,0:T(8,128)(2,1)S(1)}, u32[]{:S(2)}, u32[]{:S(2)}) collective-permute-start(bf16[264,768]{1,0:T(8,128)(2,1)S(1)} %get-tuple-element.21.own), channel_id=1, source_target_pairs={{0,2},{2,0},{4,6},{6,4},{8,10},{10,8},{12,14},{14,12},{1,3},{3,1},... | collective-permute-start | bytes 1216520 | tf_op jit(solution)/shard_map/ppermute | solution.py:41
  9.2 0.0 collective-permute-start
  9.2 7.0 %collective-permute-done.1.near2 = bf16[264,768]{1,0:T(8,128)(2,1)S(1)} collective-permute-done((bf16[264,768]{1,0:T(8,128)(2,1)S(1)}, bf16[264,768]{1,0:T(8,128)(2,1)S(1)}, u32[]{:S(2)}, u32[]{:S(2)}) %collective-permute-start.1) | collective-permute-done | bytes 405536 | tf_op jit(solution)/shard_map/ppermute | solution.py:30
  16.2 3.4 %collective-permute-start.3 = (bf16[264,768]{1,0:T(8,128)(2,1)S(1)}, bf16[264,768]{1,0:T(8,128)(2,1)S(1)}, u32[]{:S(2)}, u32[]{:S(2)}) collective-permute-start(bf16[264,768]{1,0:T(8,128)(2,1)S(1)} %collective-permute-done.1.near2), channel_id=1, source_target_pairs={{0,2},{2,4},{4,6},{6,8},{8,10},{10,12},{12,14},{1,3},{3,5},{5,7},{... | collective-permute-start | bytes 1216520 | tf_op jit(solution)/shard_map/ppermute | solution.py:30
  19.6 0.0 collective-permute-done.2.pair
  19.6 4.4 %collective-permute-start.4 = (bf16[264,768]{1,0:T(8,128)(2,1)S(1)}, bf16[264,768]{1,0:T(8,128)(2,1)S(1)}, u32[]{:S(2)}, u32[]{:S(2)}) collective-permute-start(bf16[264,768]{1,0:T(8,128)(2,1)S(1)} %collective-permute-done.2.pair), channel_id=1, source_target_pairs={{0,4},{4,8},{8,12},{1,5},{5,9},{9,13},{16,20},{20,24},{24,28},{17,... | collective-permute-start | bytes 1216520 | tf_op jit(solution)/shard_map/ppermute | solution.py:36
  24.0 0.1 collective-permute-start.11
  24.1 1.3 %collective-permute-start.12 = (bf16[256,768]{1,0:T(8,128)(2,1)S(1)}, bf16[256,768]{1,0:T(8,128)(2,1)S(1)}, u32[]{:S(2)}, u32[]{:S(2)}) collective-permute-start(bf16[256,768]{1,0:T(8,128)(2,1)S(1)} %get-tuple-element.22.qo), channel_id=1, source_target_pairs={{4,0},{6,2},{8,4},{10,6},{12,8},{14,10},{5,1},{7,3},{9,5},{11,7},{... | collective-permute-start | bytes 1179656 | tf_op jit(solution)/shard_map/ppermute | solution.py:30
  25.4 0.0 copy-start
  25.4 0.0 collective-permute-done.partner
  25.4 0.1 collective-permute-start.13
  25.5 2.7 %collective-permute-done.3.near3 = bf16[264,768]{1,0:T(8,128)(2,1)S(1)} collective-permute-done((bf16[264,768]{1,0:T(8,128)(2,1)S(1)}, bf16[264,768]{1,0:T(8,128)(2,1)S(1)}, u32[]{:S(2)}, u32[]{:S(2)}) %collective-permute-start.3) | collective-permute-done | bytes 405536 | tf_op jit(solution)/shard_map/ppermute | solution.py:30
  28.2 3.2 %collective-permute-done.4.near1 = bf16[264,768]{1,0:T(8,128)(2,1)S(1)} collective-permute-done((bf16[264,768]{1,0:T(8,128)(2,1)S(1)}, bf16[264,768]{1,0:T(8,128)(2,1)S(1)}, u32[]{:S(2)}, u32[]{:S(2)}) %collective-permute-start.4) | collective-permute-done | bytes 405536 | tf_op jit(solution)/shard_map/ppermute | solution.py:36
  31.5 0.0 copy-done
  31.5 3.8 %shard_map.111 = (f32[72,128]{1,0:T(8,128)S(1)}, bf16[128,768]{1,0:T(8,128)(2,1)S(1)}, bf16[4,256,512]{2,1,0:T(8,128)(2,1)S(1)}, bf16[2,264,768]{2,1,0:T(8,128)(2,1)S(1)}) custom-call(s32[1]{0:T(128)} %bitcast.1.frame, s32[1,2]{1,0:T(1,128)S(1)} %copy-done, s32[1]{0:T(128)} %copy.16.own_action, bf16[256,768]{1,0:T(8,128)(2,1)S(1)} %get-tuple-element.22.qo, ...), custom_call_target="tpu_custom_call" | custom-call | flops 10000000000 | tf_op jit(solution)/shard_map/pallas_call | solution.py:263
  35.3 3.5 %collective-permute-start.5 = (f32[72,128]{1,0:T(8,128)S(1)}, f32[72,128]{1,0:T(8,128)S(1)}, u32[]{:S(2)}, u32[]{:S(2)}) collective-permute-start(f32[72,128]{1,0:T(8,128)S(1)} %get-tuple-element.26.row_own), channel_id=1, source_target_pairs={{0,8},{2,10},{4,12},{6,14},{8,0},{10,2},{12,4},{14,6},{1,9},{3,11}... | collective-permute-start | bytes 110600 | tf_op jit(solution)/shard_map/ppermute | solution.py:290
  38.8 0.0 collective-permute-start.10
  38.8 0.0 collective-permute-done.12.late2
  38.8 1.4 %collective-permute-start.7 = (f32[72,128]{1,0:T(8,128)S(1)}, f32[72,128]{1,0:T(8,128)S(1)}, u32[]{:S(2)}, u32[]{:S(2)}) collective-permute-start(f32[72,128]{1,0:T(8,128)S(1)} %get-tuple-element.26.row_own), channel_id=1, source_target_pairs={{0,12},{2,14},{4,8},{6,10},{8,4},{10,6},{12,0},{14,2},{1,13},{3,15... | collective-permute-start | bytes 110600 | tf_op jit(solution)/shard_map/ppermute | solution.py:290
  40.2 0.0 collective-permute-done.13.late_pair
  40.2 0.8 %collective-permute-start.6 = (f32[72,128]{1,0:T(8,128)S(1)}, f32[72,128]{1,0:T(8,128)S(1)}, u32[]{:S(2)}, u32[]{:S(2)}) collective-permute-start(f32[72,128]{1,0:T(8,128)S(1)} %get-tuple-element.26.row_own), channel_id=1, source_target_pairs={{0,4},{2,6},{4,0},{6,2},{8,12},{10,14},{12,8},{14,10},{1,5},{3,7},... | collective-permute-start | bytes 110600 | tf_op jit(solution)/shard_map/ppermute | solution.py:290
  41.0 0.0 collective-permute-done.11.qo_partner
  41.0 1.3 %collective-permute-start.14 = (bf16[256,768]{1,0:T(8,128)(2,1)S(1)}, bf16[256,768]{1,0:T(8,128)(2,1)S(1)}, u32[]{:S(2)}, u32[]{:S(2)}) collective-permute-start(bf16[256,768]{1,0:T(8,128)(2,1)S(1)} %collective-permute-done.12.late2), channel_id=1, source_target_pairs={{2,0},{4,2},{6,4},{8,6},{10,8},{12,10},{14,12},{3,1},{5,3},{7,5},{... | collective-permute-start | bytes 1179656 | tf_op jit(solution)/shard_map/ppermute | solution.py:30
  42.3 0.0 collective-permute-done.10.row_partner
  42.3 0.7 %collective-permute-start.15 = (bf16[256,768]{1,0:T(8,128)(2,1)S(1)}, bf16[256,768]{1,0:T(8,128)(2,1)S(1)}, u32[]{:S(2)}, u32[]{:S(2)}) collective-permute-start(bf16[256,768]{1,0:T(8,128)(2,1)S(1)} %collective-permute-done.13.late_pair), channel_id=1, source_target_pairs={{6,2},{10,6},{14,10},{7,3},{11,7},{15,11},{22,18},{26,22},{30,26},... | collective-permute-start | bytes 1179656 | tf_op jit(solution)/shard_map/ppermute | solution.py:36
  43.0 2.1 %shard_map.113 = (f32[128,768]{1,0:T(8,128)S(1)}, f32[128,768]{1,0:T(8,128)S(1)}) custom-call(bf16[264,768]{1,0:T(8,128)(2,1)S(1)} %get-tuple-element.21.own, f32[72,128]{1,0:T(8,128)S(1)} %get-tuple-element.26.row_own, f32[24,128]{1,0:T(8,128)S(1)} %collective-permute-done.10.row_partner, bf16[256,768]{1,0:T(8,128)(2,1)S(1)} %get-tuple-element.22.qo, ...), custom_call_target="tpu_custom_call" | custom-call | flops 1000000000 | tf_op jit(solution)/shard_map/pallas_call | solution.py:263
  45.1 0.0 collective-permute-done.7
  45.1 0.0 collective-permute-done.6
  45.1 0.0 collective-permute-done.5.arrived
  45.2 3.3 %collective-permute-start.8 = (f32[144,128]{1,0:T(8,128)S(1)}, f32[144,128]{1,0:T(8,128)S(1)}, u32[]{:S(2)}, u32[]{:S(2)}) collective-permute-start(f32[144,128]{1,0:T(8,128)S(1)} %pad_maximum_fusion), channel_id=1, source_target_pairs={{0,2},{2,0},{4,6},{6,4},{8,10},{10,8},{12,14},{14,12},{1,3},{3,1},... | collective-permute-start | bytes 221192 | tf_op jit(solution)/shard_map/ppermute | solution.py:290
  48.5 1.1 %shard_map.112 = (bf16[128,768]{1,0:T(8,128)(2,1)}, bf16[128,768]{1,0:T(8,128)(2,1)}) custom-call(bf16[264,768]{1,0:T(8,128)(2,1)S(1)} %get-tuple-element.21.own, bf16[264,768]{1,0:T(8,128)(2,1)S(1)} %collective-permute-done.partner, bf16[2,264,768]{2,1,0:T(8,128)(2,1)S(1)} %get-tuple-element.23.picked, bf16[4,256,512]{2,1,0:T(8,128)(2,1)S(1)} %get-tuple-element.24.d_low, ...), custom_call_target="tpu_custom_call" | custom-call | flops 1000000000 | tf_op jit(solution)/shard_map/pallas_call | solution.py:263
  49.7 5.5 %collective-permute-done.8 = f32[144,128]{1,0:T(8,128)S(1)} collective-permute-done((f32[144,128]{1,0:T(8,128)S(1)}, f32[144,128]{1,0:T(8,128)S(1)}, u32[]{:S(2)}, u32[]{:S(2)}) %collective-permute-start.8) | collective-permute-done | bytes 73760 | tf_op jit(solution)/shard_map/ppermute | solution.py:290
  55.2 0.0 collective-permute-start.9
  55.2 0.0 collective-permute-done.14.late3
  55.2 0.0 collective-permute-done.15.late1
  55.3 2.1 %shard_map.114 = (bf16[128,768]{1,0:T(8,128)(2,1)}, bf16[128,768]{1,0:T(8,128)(2,1)}) custom-call(s32[1]{0:T(128)} %bitcast.1.frame, bf16[264,768]{1,0:T(8,128)(2,1)S(1)} %get-tuple-element.21.own, f32[8,24,128]{2,1,0:T(8,128)S(1)} %constant_dynamic-update-slice_fusion.stats, f32[128,768]{1,0:T(8,128)S(1)} %get-tuple-element.29.near_keys, ...), custom_call_target="tpu_custom_call" | custom-call | flops 1000000000 | tf_op jit(solution)/shard_map/pallas_call | solution.py:263
  57.3 0.0 collective-permute-done.9
  57.3 0.6 %add_bitcast_fusion = f32[8,768]{1,0:T(8,128)} fusion(f32[48,128]{1,0:T(8,128)S(1)} %slice_add_fusion, f32[48,128]{1,0:T(8,128)S(1)} %collective-permute-done.9), kind=kLoop, calls=%fused_computation.6 | loop fusion | flops 6144 | bytes 73728 | tf_op jit(solution)/shard_map/reshape | solution.py:357
  (14 shorter events, 0.1 us)
Async XLA Ops:
  2.6 13.6 %collective-permute-start.1 = (bf16[264,768]{1,0:T(8,128)(2,1)S(1)}, bf16[264,768]{1,0:T(8,128)(2,1)S(1)}, u32[]{:S(2)}, u32[]{:S(2)}) collective-permute-start(bf16[264,768]{1,0:T(8,128)(2,1)S(1)} %get-tuple-element.21.own), channel_id=1, source_target_pairs={{0,4},{2,6},{4,8},{6,10},{8,12},{10,14},{1,5},{3,7},{5,9},{7,11},{... | collective-permute-start | bytes 1216520 | tf_op jit(solution)/shard_map/ppermute | solution.py:30
  7.6 12.0 %collective-permute-start.2 = (bf16[264,768]{1,0:T(8,128)(2,1)S(1)}, bf16[264,768]{1,0:T(8,128)(2,1)S(1)}, u32[]{:S(2)}, u32[]{:S(2)}) collective-permute-start(bf16[264,768]{1,0:T(8,128)(2,1)S(1)} %get-tuple-element.21.own), channel_id=1, source_target_pairs={{0,2},{2,0},{4,6},{6,4},{8,10},{10,8},{12,14},{14,12},{1,3},{3,1},... | collective-permute-start | bytes 1216520 | tf_op jit(solution)/shard_map/ppermute | solution.py:41
  9.2 16.3 %collective-permute-start = (bf16[264,768]{1,0:T(8,128)(2,1)S(1)}, bf16[264,768]{1,0:T(8,128)(2,1)S(1)}, u32[]{:S(2)}, u32[]{:S(2)}) collective-permute-start(bf16[264,768]{1,0:T(8,128)(2,1)S(1)} %get-tuple-element.21.own), channel_id=1, source_target_pairs={{0,1},{1,0},{2,3},{3,2},{4,5},{5,4},{6,7},{7,6},{8,9},{9,8},{10,11... | collective-permute-start | bytes 1216520 | tf_op jit(solution)/shard_map/ppermute | solution.py:45
  16.2 12.0 %collective-permute-start.3 = (bf16[264,768]{1,0:T(8,128)(2,1)S(1)}, bf16[264,768]{1,0:T(8,128)(2,1)S(1)}, u32[]{:S(2)}, u32[]{:S(2)}) collective-permute-start(bf16[264,768]{1,0:T(8,128)(2,1)S(1)} %collective-permute-done.1.near2), channel_id=1, source_target_pairs={{0,2},{2,4},{4,6},{6,8},{8,10},{10,12},{12,14},{1,3},{3,5},{5,7},{... | collective-permute-start | bytes 1216520 | tf_op jit(solution)/shard_map/ppermute | solution.py:30
  19.6 11.8 %collective-permute-start.4 = (bf16[264,768]{1,0:T(8,128)(2,1)S(1)}, bf16[264,768]{1,0:T(8,128)(2,1)S(1)}, u32[]{:S(2)}, u32[]{:S(2)}) collective-permute-start(bf16[264,768]{1,0:T(8,128)(2,1)S(1)} %collective-permute-done.2.pair), channel_id=1, source_target_pairs={{0,4},{4,8},{8,12},{1,5},{5,9},{9,13},{16,20},{20,24},{24,28},{17,... | collective-permute-start | bytes 1216520 | tf_op jit(solution)/shard_map/ppermute | solution.py:36
  24.0 17.0 %collective-permute-start.11 = (bf16[256,768]{1,0:T(8,128)(2,1)S(1)}, bf16[256,768]{1,0:T(8,128)(2,1)}, u32[]{:S(2)}, u32[]{:S(2)}) collective-permute-start(bf16[256,768]{1,0:T(8,128)(2,1)S(1)} %get-tuple-element.22.qo), channel_id=1, source_target_pairs={{0,1},{1,0},{2,3},{3,2},{4,5},{5,4},{6,7},{7,6},{8,9},{9,8},{10,11... | collective-permute-start | bytes 1179656 | tf_op jit(solution)/shard_map/ppermute | solution.py:45
  24.1 14.7 %collective-permute-start.12 = (bf16[256,768]{1,0:T(8,128)(2,1)S(1)}, bf16[256,768]{1,0:T(8,128)(2,1)S(1)}, u32[]{:S(2)}, u32[]{:S(2)}) collective-permute-start(bf16[256,768]{1,0:T(8,128)(2,1)S(1)} %get-tuple-element.22.qo), channel_id=1, source_target_pairs={{4,0},{6,2},{8,4},{10,6},{12,8},{14,10},{5,1},{7,3},{9,5},{11,7},{... | collective-permute-start | bytes 1179656 | tf_op jit(solution)/shard_map/ppermute | solution.py:30
  25.4 6.1 %copy-start = (s32[1,2]{1,0:T(1,128)S(1)}, s32[1,2]{1,0:T(1,128)}, u32[]{:S(2)}) copy-start(s32[1,2]{1,0:T(1,128)} %listed.1) | copy-start | bytes 28
  25.4 14.8 %collective-permute-start.13 = (bf16[256,768]{1,0:T(8,128)(2,1)S(1)}, bf16[256,768]{1,0:T(8,128)(2,1)S(1)}, u32[]{:S(2)}, u32[]{:S(2)}) collective-permute-start(bf16[256,768]{1,0:T(8,128)(2,1)S(1)} %get-tuple-element.22.qo), channel_id=1, source_target_pairs={{0,2},{2,0},{4,6},{6,4},{8,10},{10,8},{12,14},{14,12},{1,3},{3,1},... | collective-permute-start | bytes 1179656 | tf_op jit(solution)/shard_map/ppermute | solution.py:41
  35.3 9.8 %collective-permute-start.5 = (f32[72,128]{1,0:T(8,128)S(1)}, f32[72,128]{1,0:T(8,128)S(1)}, u32[]{:S(2)}, u32[]{:S(2)}) collective-permute-start(f32[72,128]{1,0:T(8,128)S(1)} %get-tuple-element.26.row_own), channel_id=1, source_target_pairs={{0,8},{2,10},{4,12},{6,14},{8,0},{10,2},{12,4},{14,6},{1,9},{3,11}... | collective-permute-start | bytes 110600 | tf_op jit(solution)/shard_map/ppermute | solution.py:290
  38.8 3.5 %collective-permute-start.10 = (f32[24,128]{1,0:T(8,128)S(1)}, f32[24,128]{1,0:T(8,128)S(1)}, u32[]{:S(2)}, u32[]{:S(2)}) collective-permute-start(f32[24,128]{1,0:T(8,128)S(1)} %get-tuple-element.37), channel_id=1, source_target_pairs={{0,1},{1,0},{2,3},{3,2},{4,5},{5,4},{6,7},{7,6},{8,9},{9,8},{10,11... | collective-permute-start | bytes 36872 | tf_op jit(solution)/shard_map/ppermute | solution.py:45
  38.8 6.3 %collective-permute-start.7 = (f32[72,128]{1,0:T(8,128)S(1)}, f32[72,128]{1,0:T(8,128)S(1)}, u32[]{:S(2)}, u32[]{:S(2)}) collective-permute-start(f32[72,128]{1,0:T(8,128)S(1)} %get-tuple-element.26.row_own), channel_id=1, source_target_pairs={{0,12},{2,14},{4,8},{6,10},{8,4},{10,6},{12,0},{14,2},{1,13},{3,15... | collective-permute-start | bytes 110600 | tf_op jit(solution)/shard_map/ppermute | solution.py:290
  40.2 4.9 %collective-permute-start.6 = (f32[72,128]{1,0:T(8,128)S(1)}, f32[72,128]{1,0:T(8,128)S(1)}, u32[]{:S(2)}, u32[]{:S(2)}) collective-permute-start(f32[72,128]{1,0:T(8,128)S(1)} %get-tuple-element.26.row_own), channel_id=1, source_target_pairs={{0,4},{2,6},{4,0},{6,2},{8,12},{10,14},{12,8},{14,10},{1,5},{3,7},... | collective-permute-start | bytes 110600 | tf_op jit(solution)/shard_map/ppermute | solution.py:290
  41.0 14.2 %collective-permute-start.14 = (bf16[256,768]{1,0:T(8,128)(2,1)S(1)}, bf16[256,768]{1,0:T(8,128)(2,1)S(1)}, u32[]{:S(2)}, u32[]{:S(2)}) collective-permute-start(bf16[256,768]{1,0:T(8,128)(2,1)S(1)} %collective-permute-done.12.late2), channel_id=1, source_target_pairs={{2,0},{4,2},{6,4},{8,6},{10,8},{12,10},{14,12},{3,1},{5,3},{7,5},{... | collective-permute-start | bytes 1179656 | tf_op jit(solution)/shard_map/ppermute | solution.py:30
  42.3 12.9 %collective-permute-start.15 = (bf16[256,768]{1,0:T(8,128)(2,1)S(1)}, bf16[256,768]{1,0:T(8,128)(2,1)S(1)}, u32[]{:S(2)}, u32[]{:S(2)}) collective-permute-start(bf16[256,768]{1,0:T(8,128)(2,1)S(1)} %collective-permute-done.13.late_pair), channel_id=1, source_target_pairs={{6,2},{10,6},{14,10},{7,3},{11,7},{15,11},{22,18},{26,22},{30,26},... | collective-permute-start | bytes 1179656 | tf_op jit(solution)/shard_map/ppermute | solution.py:36
  45.2 10.0 %collective-permute-start.8 = (f32[144,128]{1,0:T(8,128)S(1)}, f32[144,128]{1,0:T(8,128)S(1)}, u32[]{:S(2)}, u32[]{:S(2)}) collective-permute-start(f32[144,128]{1,0:T(8,128)S(1)} %pad_maximum_fusion), channel_id=1, source_target_pairs={{0,2},{2,0},{4,6},{6,4},{8,10},{10,8},{12,14},{14,12},{1,3},{3,1},... | collective-permute-start | bytes 221192 | tf_op jit(solution)/shard_map/ppermute | solution.py:290
  55.2 2.1 %collective-permute-start.9 = (f32[48,128]{1,0:T(8,128)S(1)}, f32[48,128]{1,0:T(8,128)S(1)}, u32[]{:S(2)}, u32[]{:S(2)}) collective-permute-start(f32[48,128]{1,0:T(8,128)S(1)} %slice_add_fusion), channel_id=1, source_target_pairs={{0,1},{1,0},{2,3},{3,2},{4,5},{5,4},{6,7},{7,6},{8,9},{9,8},{10,11... | collective-permute-start | bytes 73736 | tf_op jit(solution)/shard_map/ppermute | solution.py:45
